TPU v7x, 128 devices: a whole 4x4x4 slice. The times are simulated.
128 devices in a mesh: row: 8 (over y, z_hi), col: 8 (over z_lo, x), grp: 2 (over core).
Axes of the slice: x: 4, y: 4, z: 4 (z_hi: 2, z_lo: 2; z = z_hi * 2 + z_lo), core: 2. Of those that a mesh axis runs over, the one named last changes fastest.
Arguments:
- krylov_basis: float32 [30, 8, 32768], P(None, None, 'row'), may hold values from -6 to 6
- lattice: int32 [3, 32768], P(None, 'row'), may hold values from 0 to 95, as said below
- strength_index: int32 [32768], P('row'), may hold values from 0 to 15
- strength_table: float32 [16], replicated, may hold values from 0.05 to 0.4
Outputs:
- new_block: float32 [8, 32768], P(None, 'row')
- hessenberg: float32 [30, 2, 4, 4], replicated
- block_gram: float32 [2, 4, 4], replicated
Inputs may be any that keep to these rules, and one draw needn't show every extreme that they name: The 32768 scatterers stand on distinct lattice points.
All inputs are finite; a program needn't handle non-finite values.
Results may differ from a plain program's by a relative error of at most 0.0003.
Values may be sent and summed in bfloat16 or wider, within the bound.
No kernel may reach another device: no remote copies, remote signals or barrier semaphores. Data moves between devices by JAX's collectives and lax.ppermute only.
A program may use at most 64 MiB of HBM per device.

v0:
```python
import math

import jax
import jax.numpy as jnp
from jax import lax
from jax.sharding import PartitionSpec as P

wave_number = 2.0
highest = lax.Precision.HIGHEST


def sent_to_all(x, axis):
    length = lax.axis_size(axis)
    return lax.all_to_all(jnp.broadcast_to(x[None], (length, *x.shape)), axis, 0, 0, tiled=True)


def taken_together(x, axis):
    everything = sent_to_all(x, axis)
    return jnp.sum(everything, axis=0)


def joined_along(tiles, dim):
    tiles = jnp.moveaxis(tiles, 0, dim)
    lengths = tiles.shape
    return tiles.reshape(*lengths[:dim], lengths[dim] * lengths[dim + 1], *lengths[dim + 2 :])


def gather_directly(x, axis, dim):
    return joined_along(sent_to_all(x, axis), dim)


def strength_of(strength_table, strength_index):
    matches = (
        strength_index[:, None] == jnp.arange(strength_table.shape[0], dtype=jnp.int32)[None, :]
    )
    return jnp.sum(
        jnp.where(matches, strength_table[None, :], jnp.zeros((), strength_table.dtype)), axis=1
    )


def green_pair(target, source):
    squared = jnp.zeros((target.shape[1], source.shape[1]), jnp.float32)
    for axis_id in range(3):
        offset = target[axis_id][:, None] - source[axis_id][None, :]
        squared = squared + offset * offset
    distance = jnp.sqrt(jnp.maximum(squared, 1.0))
    phases = wave_number * distance
    inverse = 1.0 / distance
    distinct = squared > 0.5
    real_part = jnp.where(distinct, jnp.cos(phases) * inverse, 0.0)
    imag_part = jnp.where(distinct, jnp.sin(phases) * inverse, 0.0)
    return jnp.concatenate([real_part, imag_part], 0).astype(jnp.bfloat16)


def combine(product, tile_size):
    half_rows = product.shape[0] // 2
    direct = product[:, :tile_size]
    turned = product[:, tile_size:]
    return jnp.concatenate(
        [direct[:half_rows] - turned[half_rows:], direct[half_rows:] + turned[:half_rows]], 0
    )


def scatter_block(target, source, weighted):
    stacked = green_pair(target, source)
    product = lax.dot_general(
        weighted, stacked, (((1,), (1,)), ((), ())), preferred_element_type=jnp.float32
    )
    return combine(product, target.shape[1])


def project(krylov_basis, field):
    return jnp.einsum("jan,bn->jab", krylov_basis, field, precision=highest)


def self_gram(field):
    return jnp.dot(field, field.T, precision=highest)


def complex_parts(gram):
    half_rows = gram.shape[-1] // 2
    real_part = gram[..., :half_rows, :half_rows] + gram[..., half_rows:, half_rows:]
    imag_part = gram[..., :half_rows, half_rows:] - gram[..., half_rows:, :half_rows]
    return (real_part, imag_part)


def subtract(krylov_basis, field, real_part, imag_part):
    upper = jnp.concatenate([real_part, imag_part], -1)
    lower = jnp.concatenate([-imag_part, real_part], -1)
    mixing = jnp.concatenate([upper, lower], -2)
    return field - jnp.einsum("jab,jan->bn", mixing, krylov_basis, precision=highest)


def row_first_sum(value):
    return taken_together(value, "row")


def row_second_sum(value):
    return taken_together(value, "row")


def row_norm_sum(value):
    return taken_together(value, "row")


def orthogonalize(krylov_basis, initial, point_total, summers):
    sum_first, sum_second, sum_norm = summers
    once_real, once_imag = complex_parts(sum_first(project(krylov_basis, initial)) / point_total)
    once = subtract(krylov_basis, initial, once_real, once_imag)
    twice_real, twice_imag = complex_parts(sum_second(project(krylov_basis, once)) / point_total)
    new_block = subtract(krylov_basis, once, twice_real, twice_imag)
    norm_real, norm_imag = complex_parts(sum_norm(self_gram(new_block)) / point_total)
    hessenberg = jnp.stack([once_real + twice_real, once_imag + twice_imag], 1)
    block_gram = jnp.stack([norm_real, norm_imag], 0)
    return (new_block, hessenberg, block_gram)


def local(krylov_basis, lattice, strength_index, strength_table):
    local_rows = krylov_basis.shape[2]
    column_parts = lax.axis_size(("col", "grp"))
    block_size = local_rows // column_parts
    column_id = lax.axis_index(("col", "grp"))
    point_total = local_rows * lax.axis_size("row")
    direction = krylov_basis[krylov_basis.shape[0] - 1]
    channel_rows = direction.shape[0]
    weighted = (direction * strength_of(strength_table, strength_index)[None, :]).astype(
        jnp.bfloat16
    )
    slice_start = column_id * block_size
    own_weights = lax.dynamic_slice_in_dim(weighted, slice_start, block_size, 1)
    own_sites = lax.dynamic_slice_in_dim(lattice, slice_start, block_size, 1).astype(jnp.bfloat16)
    packed = jnp.concatenate([own_weights, own_sites], 0)
    located = lattice.astype(jnp.float32)
    tile_size = math.gcd(local_rows, 512)
    targets = located.reshape(3, local_rows // tile_size, tile_size).transpose(1, 0, 2)
    portion = gather_directly(packed, "row", 1)
    source_weights = portion[:channel_rows]
    source_sites = portion[channel_rows:].astype(jnp.float32)
    tiles = lax.map(lambda target: scatter_block(target, source_sites, source_weights), targets)
    scattered = tiles.transpose(1, 0, 2).reshape(channel_rows, local_rows)
    initial = direction - taken_together(scattered, ("col", "grp"))
    summers = (row_first_sum, row_second_sum, row_norm_sum)
    new_block, hessenberg, block_gram = orthogonalize(krylov_basis, initial, point_total, summers)
    return (new_block, hessenberg, block_gram)


def solution(mesh):
    in_specs = (P(None, None, "row"), P(None, "row"), P("row"), P())
    out_specs = (P(None, "row"), P(), P())
    return jax.shard_map(local, mesh=mesh, in_specs=in_specs, out_specs=out_specs, check_vma=False)
```

profile of v0, /device:TPU:1, one launch (start us, length us, event | category | flops | bytes accessed | tf_op | source)
XLA Modules:
  0.0 283.2 jit_solution(8878123662840934535)
XLA Ops:
  0.6 0.9 slice_bitcast_fusion
  1.6 0.9 select_reduce_fusion
  2.4 0.1 dynamic-slice.3
  2.5 0.7 dynamic-slice_convert_fusion
  3.2 0.6 broadcast_in_dim.62
  3.8 8.3 %all-to-all-start = ((bf16[8,11,256]{2,1,0:T(8,128)(2,1)}), bf16[8,11,256]{2,1,0:T(8,128)(2,1)S(1)}, u32[]{:S(2)}, u32[]{:S(2)}) async-start(bf16[8,11,256]{2,1,0:T(8,128)(2,1)} %broadcast_in_dim.62), calls=%async_computation | async-start | bytes 131072 | tf_op jit(solution)/shard_map/all_to_all | solution.py:14
  12.2 0.9 convert_element_type.16
  13.0 5.8 %all-to-all-done = bf16[8,11,256]{2,1,0:T(8,128)(2,1)S(1)} async-done(((bf16[8,11,256]{2,1,0:T(8,128)(2,1)}), bf16[8,11,256]{2,1,0:T(8,128)(2,1)S(1)}, u32[]{:S(2)}, u32[]{:S(2)}) %all-to-all-start) | async-done | bytes 45088 | tf_op jit(solution)/shard_map/all_to_all | solution.py:14
  18.8 162.0 %while.10 = (s32[]{:T(128)}, f32[8,8,512]{2,1,0:T(8,128)S(1)}, f32[8,3,512]{2,1,0:T(4,128)S(1)}, f32[3,2048]{1,0:T(4,128)S(1)}, bf16[8,2048]{1,0:T(8,128)(2,1)S(1)}, /*index=5*/s32[]{:T(128)}, s32[]{:T(128)}, s32[]{}, s32[]{}) while((s32[]{:T(128)}, f32[8,8,512]{2,1,0:T(8,128)S(1)}, f32[8,3,512]{2,1,0:T(4,128)S(1)}, f32[3,2048]{1,0:T(4,128)S(1)}, ...), condition=%wide.region_2.3_spmd, body=%wide.region_1.2_spmd.sunk | while | flops 60825604 | bytes 8628357 | solution.py:139
  18.9 19.0 %select_convert_fusion.3 = (bf16[512,2048]{1,0:T(8,128)(2,1)S(1)}, bf16[512,2048]{1,0:T(8,128)(2,1)S(1)}) fusion(f32[2048]{0:T(1024)S(1)} %bitcast.87, f32[512]{0:T(512)S(1)} %bitcast.96, f32[2048]{0:T(1024)S(1)} %bitcast.88, f32[512]{0:T(512)S(1)} %bitcast.95, f32[2048]{0:T(1024)S(1)} %bitcast.86, f32[512]{0:T(512)S(1)} %bitcast.94), kind=kLoop, calls=%fused_computation.5.clone.1 | loop fusion | flops 18874368 | bytes 4225024 | tf_op jit(solution)/shard_map/convert
  37.9 1.2 fusion.60
  39.1 19.0 %select_convert_fusion.3 = (bf16[512,2048]{1,0:T(8,128)(2,1)S(1)}, bf16[512,2048]{1,0:T(8,128)(2,1)S(1)}) fusion(f32[2048]{0:T(1024)S(1)} %bitcast.87, f32[512]{0:T(512)S(1)} %bitcast.96, f32[2048]{0:T(1024)S(1)} %bitcast.88, f32[512]{0:T(512)S(1)} %bitcast.95, f32[2048]{0:T(1024)S(1)} %bitcast.86, f32[512]{0:T(512)S(1)} %bitcast.94), kind=kLoop, calls=%fused_computation.5.clone.1 | loop fusion | flops 18874368 | bytes 4225024 | tf_op jit(solution)/shard_map/convert
  58.1 1.2 fusion.60
  59.4 19.0 %select_convert_fusion.3 = (bf16[512,2048]{1,0:T(8,128)(2,1)S(1)}, bf16[512,2048]{1,0:T(8,128)(2,1)S(1)}) fusion(f32[2048]{0:T(1024)S(1)} %bitcast.87, f32[512]{0:T(512)S(1)} %bitcast.96, f32[2048]{0:T(1024)S(1)} %bitcast.88, f32[512]{0:T(512)S(1)} %bitcast.95, f32[2048]{0:T(1024)S(1)} %bitcast.86, f32[512]{0:T(512)S(1)} %bitcast.94), kind=kLoop, calls=%fused_computation.5.clone.1 | loop fusion | flops 18874368 | bytes 4225024 | tf_op jit(solution)/shard_map/convert
  78.4 1.2 fusion.60
  79.7 19.0 %select_convert_fusion.3 = (bf16[512,2048]{1,0:T(8,128)(2,1)S(1)}, bf16[512,2048]{1,0:T(8,128)(2,1)S(1)}) fusion(f32[2048]{0:T(1024)S(1)} %bitcast.87, f32[512]{0:T(512)S(1)} %bitcast.96, f32[2048]{0:T(1024)S(1)} %bitcast.88, f32[512]{0:T(512)S(1)} %bitcast.95, f32[2048]{0:T(1024)S(1)} %bitcast.86, f32[512]{0:T(512)S(1)} %bitcast.94), kind=kLoop, calls=%fused_computation.5.clone.1 | loop fusion | flops 18874368 | bytes 4225024 | tf_op jit(solution)/shard_map/convert
  98.6 1.2 fusion.60
  99.9 19.0 %select_convert_fusion.3 = (bf16[512,2048]{1,0:T(8,128)(2,1)S(1)}, bf16[512,2048]{1,0:T(8,128)(2,1)S(1)}) fusion(f32[2048]{0:T(1024)S(1)} %bitcast.87, f32[512]{0:T(512)S(1)} %bitcast.96, f32[2048]{0:T(1024)S(1)} %bitcast.88, f32[512]{0:T(512)S(1)} %bitcast.95, f32[2048]{0:T(1024)S(1)} %bitcast.86, f32[512]{0:T(512)S(1)} %bitcast.94), kind=kLoop, calls=%fused_computation.5.clone.1 | loop fusion | flops 18874368 | bytes 4225024 | tf_op jit(solution)/shard_map/convert
  118.9 1.2 fusion.60
  120.2 19.0 %select_convert_fusion.3 = (bf16[512,2048]{1,0:T(8,128)(2,1)S(1)}, bf16[512,2048]{1,0:T(8,128)(2,1)S(1)}) fusion(f32[2048]{0:T(1024)S(1)} %bitcast.87, f32[512]{0:T(512)S(1)} %bitcast.96, f32[2048]{0:T(1024)S(1)} %bitcast.88, f32[512]{0:T(512)S(1)} %bitcast.95, f32[2048]{0:T(1024)S(1)} %bitcast.86, f32[512]{0:T(512)S(1)} %bitcast.94), kind=kLoop, calls=%fused_computation.5.clone.1 | loop fusion | flops 18874368 | bytes 4225024 | tf_op jit(solution)/shard_map/convert
  139.1 1.2 fusion.60
  140.4 19.0 %select_convert_fusion.3 = (bf16[512,2048]{1,0:T(8,128)(2,1)S(1)}, bf16[512,2048]{1,0:T(8,128)(2,1)S(1)}) fusion(f32[2048]{0:T(1024)S(1)} %bitcast.87, f32[512]{0:T(512)S(1)} %bitcast.96, f32[2048]{0:T(1024)S(1)} %bitcast.88, f32[512]{0:T(512)S(1)} %bitcast.95, f32[2048]{0:T(1024)S(1)} %bitcast.86, f32[512]{0:T(512)S(1)} %bitcast.94), kind=kLoop, calls=%fused_computation.5.clone.1 | loop fusion | flops 18874368 | bytes 4225024 | tf_op jit(solution)/shard_map/convert
  159.4 1.2 fusion.60
  160.7 19.0 %select_convert_fusion.3 = (bf16[512,2048]{1,0:T(8,128)(2,1)S(1)}, bf16[512,2048]{1,0:T(8,128)(2,1)S(1)}) fusion(f32[2048]{0:T(1024)S(1)} %bitcast.87, f32[512]{0:T(512)S(1)} %bitcast.96, f32[2048]{0:T(1024)S(1)} %bitcast.88, f32[512]{0:T(512)S(1)} %bitcast.95, f32[2048]{0:T(1024)S(1)} %bitcast.86, f32[512]{0:T(512)S(1)} %bitcast.94), kind=kLoop, calls=%fused_computation.5.clone.1 | loop fusion | flops 18874368 | bytes 4225024 | tf_op jit(solution)/shard_map/convert
  179.6 1.2 fusion.60
  180.9 0.2 broadcast_in_dim.64
  181.1 33.4 %all_to_all.25 = f32[16,8,4096]{2,1,0:T(8,128)S(1)} all-to-all(f32[16,8,4096]{2,1,0:T(8,128)S(1)} %broadcast_in_dim.64), channel_id=1, replica_groups=mesh['row'=8,'col'=8,'grp'=2] {'col','grp'}, dimensions={0} | all-to-all | bytes 4194304 | tf_op jit(solution)/shard_map/all_to_all | solution.py:14
  214.5 0.1 reduce_sum.46
  214.6 11.6 %fusion.19 = f32[30,8,8]{0,2,1:T(8,128)S(1)} fusion(f32[30,8,4096]{2,1,0:T(8,128)} %param.6, f32[8,4096]{1,0:T(8,128)S(1)} %reduce_sum.46), kind=kOutput, calls=%fused_computation.29 | convolution fusion | flops 94404608 | bytes 4201984 | tf_op jit(solution)/shard_map/jan,bn->jab/dot_general | solution.py:73
  226.2 0.2 reshape.37
  226.5 9.4 %all_to_all.26 = f32[8,1,1920]{2,1,0:T(1,128)S(1)} all-to-all(f32[8,1,1920]{2,1,0:T(1,128)S(1)} %reshape.37), channel_id=1, replica_groups=mesh['row'=8,'col'=8,'grp'=2] {'row'}, dimensions={0} | all-to-all | bytes 122880 | tf_op jit(solution)/shard_map/all_to_all | solution.py:14
  235.9 0.5 broadcast.39
  236.4 0.8 reduce
  237.2 0.2 reshape.38
  237.6 7.0 %fusion.12 = f32[8,4096]{1,0:T(8,128)S(1)} fusion(f32[30,8,4096]{2,1,0:T(8,128)} %param.6, f32[30,4,4]{0,2,1:T(4,128)S(1)} %get-tuple-element.59, f32[30,4,4]{0,2,1:T(4,128)S(1)} %get-tuple-element.45, f32[30,4,4]{0,2,1:T(4,128)S(1)} %get-tuple-element.46, f32[8,4096]{1,0:T(8,128)S(1)} %reduce_sum.46), kind=kOutput, calls=%fused_computation.22 | convolution fusion | flops 94443136 | bytes 4331136 | tf_op jit(solution)/shard_map/jab,jan->bn/dot_general | solution.py:91
  244.6 9.7 %fusion.22 = f32[30,8,8]{0,2,1:T(8,128)S(1)} fusion(f32[30,8,4096]{2,1,0:T(8,128)S(1)} %copy-done, f32[8,4096]{1,0:T(8,128)S(1)} %fusion.12), kind=kOutput, calls=%fused_computation.30 | convolution fusion | flops 94371840 | bytes 4070912 | tf_op jit(solution)/shard_map/jan,bn->jab/dot_general | solution.py:73
  254.3 0.2 reshape.39
  254.5 9.1 %all_to_all.27 = f32[8,1,1920]{2,1,0:T(1,128)S(1)} all-to-all(f32[8,1,1920]{2,1,0:T(1,128)S(1)} %reshape.39), channel_id=1, replica_groups=mesh['row'=8,'col'=8,'grp'=2] {'row'}, dimensions={0} | all-to-all | bytes 122880 | tf_op jit(solution)/shard_map/all_to_all | solution.py:14
  263.6 0.8 reduce.1
  264.4 0.2 reshape.40
  264.8 6.9 %fusion.11 = f32[8,4096]{1,0:T(8,128)S(1)} fusion(f32[8,4096]{1,0:T(8,128)S(1)} %fusion.12, f32[30,8,4096]{2,1,0:T(8,128)} %param.6, f32[30,4,4]{0,2,1:T(4,128)S(1)} %get-tuple-element.58, f32[30,4,4]{0,2,1:T(4,128)S(1)} %neg.7, f32[30,4,4]{0,2,1:T(4,128)S(1)} %get-tuple-element.44), kind=kOutput, calls=%fused_computation.20 | convolution fusion | flops 94410368 | bytes 4200064 | tf_op jit(solution)/shard_map/jab,jan->bn/dot_general | solution.py:91
  271.6 0.4 fusion.48
  272.0 0.6 broadcast_in_dim.67
  272.6 3.3 %all-to-all-start.4 = ((f32[8,8,8]{2,1,0:T(8,128)}), f32[8,8,8]{2,1,0:T(8,128)S(1)}, u32[]{:S(2)}, u32[]{:S(2)}) async-start(f32[8,8,8]{2,1,0:T(8,128)} %broadcast_in_dim.67), calls=%async_computation.4 | async-start | bytes 65536 | tf_op jit(solution)/shard_map/all_to_all | solution.py:14
  276.0 0.6 pad_maximum_fusion
  276.6 5.9 %all-to-all-done.4 = f32[8,8,8]{2,1,0:T(8,128)S(1)} async-done(((f32[8,8,8]{2,1,0:T(8,128)}), f32[8,8,8]{2,1,0:T(8,128)S(1)}, u32[]{:S(2)}, u32[]{:S(2)}) %all-to-all-start.4) | async-done | bytes 2080 | tf_op jit(solution)/shard_map/all_to_all | solution.py:14
  282.5 0.1 add_bitcast_fusion.2
  282.6 0.6 pad_maximum_fusion.2
  (53 shorter events, 0.7 us)
Async XLA Ops:
  3.8 14.9 %all-to-all-start = ((bf16[8,11,256]{2,1,0:T(8,128)(2,1)}), bf16[8,11,256]{2,1,0:T(8,128)(2,1)S(1)}, u32[]{:S(2)}, u32[]{:S(2)}) async-start(bf16[8,11,256]{2,1,0:T(8,128)(2,1)} %broadcast_in_dim.62), calls=%async_computation | async-start | bytes 131072 | tf_op jit(solution)/shard_map/all_to_all | solution.py:14
  237.5 7.1 %copy-start = (f32[30,8,4096]{2,1,0:T(8,128)S(1)}, f32[30,8,4096]{2,1,0:T(8,128)}, u32[]{:S(2)}) copy-start(f32[30,8,4096]{2,1,0:T(8,128)} %param.6) | copy-start | bytes 11796484
  271.6 11.5 %copy-start.1 = (f32[8,4096]{1,0:T(8,128)}, f32[8,4096]{1,0:T(8,128)S(1)}, u32[]{:S(2)}) copy-start(f32[8,4096]{1,0:T(8,128)S(1)} %fusion.11) | copy-start | bytes 393220
  272.6 9.8 %all-to-all-start.4 = ((f32[8,8,8]{2,1,0:T(8,128)}), f32[8,8,8]{2,1,0:T(8,128)S(1)}, u32[]{:S(2)}, u32[]{:S(2)}) async-start(f32[8,8,8]{2,1,0:T(8,128)} %broadcast_in_dim.67), calls=%async_computation.4 | async-start | bytes 65536 | tf_op jit(solution)/shard_map/all_to_all | solution.py:14
where the time goes:
time: 287 us; the launch traced here: 283 us
  other arithmetic  157 us (55%)
  blocking collectives  52 us (18%)
  matrix products  44.9 us (16%)
  starting transfers between devices  11.7 us (4%)
  waiting for transfers between devices  11.6 us (4%)
  local copies, waits for them, and re-layouts  4.32 us (2%)
    another operation x8, other arithmetic  152 us
    all_to_all x3, blocking collectives, sent_to_all(): lax.all_to_all(jnp.broadcast_to(x[None], (length, *x.shape)), axis, 0, 0,...  52 us
    dot_general x2, matrix products, project(): return jnp.einsum('jan,bn->jab', krylov_basis, field, precision=highest)  21.3 us
    dot_general x2, matrix products, subtract(): jnp.einsum('jab,jan->bn', mixing, krylov_basis, precision=highest)  13.9 us
    all_to_all x2, starting transfers between devices, sent_to_all(): lax.all_to_all(jnp.broadcast_to(x[None], (length, *x.shape)), axis, 0, 0,...  11.7 us
    all_to_all x2, waiting for transfers between devices, sent_to_all(): lax.all_to_all(jnp.broadcast_to(x[None], (length, *x.shape)), axis, 0, 0,...  11.6 us
    dot_general x8, matrix products, scatter_block(): lax.dot_general(weighted, stacked, (((1,), (1,)), ((), ())), preferred_el...  9.44 us
  transfers between devices with their start and end apart: 2, of which 2 were waited for; matrix products, arithmetic and copies ran while one was open for 1% of the time, Pallas kernels for 0%

commit v1 on v0

v1 whole, which is shorter than its diff:
```python
import functools

import jax
import jax.numpy as jnp
import numpy as np
from jax import lax
from jax.experimental import pallas as pl
from jax.experimental.pallas import tpu as pltpu
from jax.sharding import PartitionSpec as P

f32 = jnp.float32
bf16 = jnp.bfloat16
highest = lax.Precision.HIGHEST
NT = (((1,), (1,)), ((), ()))
TN = (((0,), (0,)), ((), ()))

SINE = (4.442867902958593, -7.30744341838288, 3.5947880506690506, -0.7843739567334573)
SUB = 256
STEP = 512


def green_pair(squared, masked):
    if masked:
        distinct = squared > 0.5
        squared = jnp.maximum(squared, 1.0)
    inverse = lax.rsqrt(squared)
    turns = (squared * inverse) * np.float32(1.0 / np.pi)
    part = turns - jnp.round(turns)
    z = part * part
    poly = z * np.float32(SINE[3]) + np.float32(SINE[2])
    poly = poly * z + np.float32(SINE[1])
    poly = poly * z + np.float32(SINE[0])
    sine = part * poly
    cosine_2 = 1.0 - sine * sine
    rest = jnp.maximum(cosine_2 + 1.0, 1e-12)
    real_part = cosine_2 * inverse
    imag_part = (sine * inverse) * (rest * lax.rsqrt(rest))
    if masked:
        real_part = jnp.where(distinct, real_part, 0.0)
        imag_part = jnp.where(distinct, imag_part, 0.0)
    return real_part.astype(bf16), imag_part.astype(bf16)


def scatter_tiles(tiles, read, targets, held, acc, masked):
    width = targets.shape[1]

    def fill(i, slot):
        sites = read(i, 8)
        held[slot] = lax.dot_general(sites, targets[...], TN, preferred_element_type=f32)

    def work(i, slot):
        weights = read(i, 0)
        for k in range(width // SUB):
            cut = slice(k * SUB, (k + 1) * SUB)
            real_part, imag_part = green_pair(held[slot, :, cut], masked)
            acc[0:8, cut] += jnp.dot(weights, real_part, preferred_element_type=f32)
            acc[8:16, cut] += jnp.dot(weights, imag_part, preferred_element_type=f32)

    fill(0, 0)

    def body(h, carry):
        i = 2 * h
        fill(i + 1, 1)
        work(i, 0)
        fill(jnp.minimum(i + 2, tiles - 1), 0)
        work(i + 1, 1)
        return carry

    lax.fori_loop(0, tiles // 2, body, 0)


def local_kernel(targets, sources, acc, held):
    acc[...] = jnp.zeros_like(acc)

    def read(i, first):
        return sources[first : first + 8, pl.ds(pl.multiple_of(i * STEP, STEP), STEP)]

    scatter_tiles(sources.shape[1] // STEP, read, targets, held, acc, True)


def remote_kernel(place, targets, sources, begun, keep, send, held, acc):
    rows, _, length = sources.shape
    per_row = length // STEP
    row = place[0]
    acc[...] = begun[...]

    def read(i, first):
        chunk = lax.rem(row + 1 + i // per_row, rows)
        off = pl.multiple_of(lax.rem(i, per_row) * STEP, STEP)
        return sources[chunk, first : first + 8, pl.ds(off, STEP)]

    scatter_tiles((rows - 1) * per_row, read, targets, held, acc, False)
    real = acc[0:8]
    imag = acc[8:16]
    upper = real[0:4] - imag[4:8]
    lower = real[4:8] + imag[0:4]
    both = jnp.concatenate([upper, lower], 0)
    half = both.shape[1] // 2
    first, second = both[:, :half], both[:, half:]
    mine = place[1] == 0
    keep[...] = jnp.where(mine, first, second)
    send[...] = jnp.where(mine, second, first)


def split(x):
    high = x.astype(bf16)
    return high, (x - high.astype(f32)).astype(bf16)


def gram_kernel(place, basis, out):
    @pl.when(pl.program_id(0) == 0)
    def _():
        out[...] = jnp.zeros_like(out)

    rows = out.shape[0]
    own = basis[pl.ds(pl.multiple_of(place[2], 8), rows), :]
    own_high, own_low = split(own)
    high, low = split(basis[...])
    both = jnp.concatenate([own_high, own_low], 0)
    first = lax.dot_general(both, high, NT, preferred_element_type=f32)
    second = lax.dot_general(own_high, low, NT, preferred_element_type=f32)
    out[:, : basis.shape[0]] += first[:rows] + first[rows:] + second


def project_kernel(place, keep, got, direction, basis, gram, initial, packed):
    field = direction[...] - (keep[...] + got[...])
    initial[...] = field
    count = basis.shape[0]
    packed[...] = jnp.zeros_like(packed)
    packed[0:8, 0:count] = lax.dot_general(
        field, basis[...], NT, preferred_element_type=f32, precision=highest
    )
    packed[0:8, count : count + 8] = lax.dot_general(
        field, field, NT, preferred_element_type=f32, precision=highest
    )
    packed[8:, :] = gram[...]


def complex_mix(products, total):
    lane = lax.broadcasted_iota(jnp.int32, products.shape, 1)
    sub = lax.broadcasted_iota(jnp.int32, products.shape, 0)
    upper = (lane & 4) == 0
    width = products.shape[1]
    rolled = pltpu.roll(products, 4, 0)
    swapped = jnp.where(upper, pltpu.roll(rolled, width - 4, 1), pltpu.roll(rolled, 4, 1))
    same = upper == (sub < 4)
    return (products + jnp.where(same, swapped, -swapped)) * np.float32(1.0 / total)


def dot3(left, right):
    left_high, left_low = split(left)
    right_high, right_low = split(right)
    rows = left.shape[0]
    first = jnp.dot(
        jnp.concatenate([left_high, left_low], 0), right_high, preferred_element_type=f32
    )
    second = jnp.dot(left_high, right_low, preferred_element_type=f32)
    return first[:rows] + first[rows:] + second


def final_kernel(total, shared, basis, new, coef, norm, mix):
    parts = shared.shape[0]
    count = basis.shape[0]

    @pl.when(pl.program_id(0) == 0)
    def _():
        sums = shared[0, 8:16, :]
        for q in range(1, parts):
            sums = sums + shared[q, 8:16, :]
        products = sums[:, :count]
        own = sums[:, count : count + 8]
        gram = jnp.concatenate([shared[q, 16:32, :] for q in range(count // 16)], 0)[:, :count]
        dot = functools.partial(jnp.dot, preferred_element_type=f32, precision=highest)
        once = complex_mix(sums, total)[:, :count]
        twice_products = products - dot(once, gram)
        pad = jnp.concatenate([twice_products, jnp.zeros_like(sums[:, count:])], 1)
        both = once + complex_mix(pad, total)[:, :count]
        mix[...] = both
        coef[...] = both
        cross = lax.dot_general(both, products, NT, preferred_element_type=f32, precision=highest)
        cross_t = lax.dot_general(products, both, NT, preferred_element_type=f32, precision=highest)
        square = lax.dot_general(
            dot(both, gram), both, NT, preferred_element_type=f32, precision=highest
        )
        norm[...] = own - cross - cross_t + square

    width = basis.shape[1]
    per = width // shared.shape[2]
    base = pl.program_id(0) * per
    field = jnp.concatenate([shared[base + k, 0:8, :] for k in range(per)], 1)
    new[...] = field - dot3(mix[...], basis[...])


def gather_all(x, axis):
    length = lax.axis_size(axis)
    return lax.all_to_all(jnp.broadcast_to(x[None], (length, *x.shape)), axis, 0, 0, tiled=True)


VMEM = pl.BlockSpec(memory_space=pltpu.VMEM)
SMEM = pl.BlockSpec(memory_space=pltpu.SMEM)


def params(**more):
    return pltpu.CompilerParams(vmem_limit_bytes=40 << 20, **more)


def local(krylov_basis, lattice, strength_index, strength_table):
    blocks, channels, points = krylov_basis.shape
    count = blocks * channels
    rows = lax.axis_size("row")
    groups = lax.axis_size("grp")
    parts = lax.axis_size(("col", "grp"))
    row, col, grp = lax.axis_index("row"), lax.axis_index("col"), lax.axis_index("grp")
    part = lax.axis_index(("col", "grp"))
    total = points * rows
    own = points // parts
    wide = own * groups
    length = points // groups
    flat = krylov_basis.reshape(count, points)
    place = jnp.stack([row, grp, jnp.minimum(part * 16, count - 16), part]).astype(jnp.int32)

    direction = krylov_basis[blocks - 1]
    matches = strength_index[None, :] == jnp.arange(strength_table.shape[0], dtype=jnp.int32)[:, None]
    strength = jnp.sum(jnp.where(matches, strength_table[:, None], 0.0), axis=0)
    weighted = (direction * strength[None, :]).astype(bf16)
    x, y, z = lattice[0], lattice[1], lattice[2]
    norm = x * x + y * y + z * z
    high = norm // 256
    low = norm - 256 * high
    one = jnp.ones_like(x)
    sites = jnp.stack([x, y, z, high, low, one, one, 0 * one]).astype(bf16)
    aims = jnp.stack([-2 * x, -2 * y, -2 * z, 256 * one, one, 256 * high, low, 0 * one]).astype(bf16)
    packed = jnp.concatenate([weighted, sites], 0)
    sources = lax.dynamic_slice_in_dim(packed, grp * length, length, 1)
    targets = lax.dynamic_slice_in_dim(aims, col * wide, wide, 1)
    gathered = gather_all(sources, "row")

    held = pltpu.VMEM((2, STEP, wide), f32)
    sums = jax.ShapeDtypeStruct((16, wide), f32)
    begun = pl.pallas_call(
        local_kernel,
        out_shape=sums,
        in_specs=[VMEM, VMEM],
        out_specs=VMEM,
        scratch_shapes=[held],
        compiler_params=params(),
        cost_estimate=pl.CostEstimate(flops=3_000_000_000, bytes_accessed=200_000, transcendentals=0),
        name="scatter_local",
    )(targets, sources)

    gram = pl.pallas_call(
        gram_kernel,
        grid_spec=pltpu.PrefetchScalarGridSpec(
            num_scalar_prefetch=1,
            grid=(4,),
            in_specs=[pl.BlockSpec((count, points // 4), lambda k, s: (0, k))],
            out_specs=pl.BlockSpec((16, 256), lambda k, s: (0, 0)),
        ),
        out_shape=jax.ShapeDtypeStruct((16, 256), f32),
        compiler_params=params(),
        cost_estimate=pl.CostEstimate(flops=2_000_000_000, bytes_accessed=4_000_000, transcendentals=0),
        name="basis_gram",
    )(place, flat)

    half = jax.ShapeDtypeStruct((8, own), f32)
    keep, send = pl.pallas_call(
        remote_kernel,
        out_shape=(half, half),
        in_specs=[SMEM, VMEM, VMEM, VMEM],
        out_specs=(VMEM, VMEM),
        scratch_shapes=[held, pltpu.VMEM((16, wide), f32)],
        compiler_params=params(),
        cost_estimate=pl.CostEstimate(flops=20_000_000_000, bytes_accessed=800_000, transcendentals=0),
        name="scatter_remote",
    )(place, targets, gathered, begun)
    got = lax.ppermute(send, "grp", [(i, groups - 1 - i) for i in range(groups)])

    initial, partial = pl.pallas_call(
        project_kernel,
        grid_spec=pltpu.PrefetchScalarGridSpec(
            num_scalar_prefetch=1,
            grid=(1,),
            in_specs=[
                pl.BlockSpec((8, own), lambda k, s: (0, 0)),
                pl.BlockSpec((8, own), lambda k, s: (0, 0)),
                pl.BlockSpec((8, own), lambda k, s: (blocks - 1, s[3])),
                pl.BlockSpec((count, own), lambda k, s: (0, s[3])),
                pl.BlockSpec((16, 256), lambda k, s: (0, 0)),
            ],
            out_specs=[
                pl.BlockSpec((8, own), lambda k, s: (0, 0)),
                pl.BlockSpec((24, 256), lambda k, s: (0, 0)),
            ],
        ),
        out_shape=(half, jax.ShapeDtypeStruct((24, 256), f32)),
        compiler_params=params(),
        name="project",
    )(place, keep, got, flat, flat, gram)

    row_sums = jnp.sum(gather_all(partial, "row"), axis=0)
    shared = gather_all(jnp.concatenate([initial, row_sums], 0), ("col", "grp"))

    new_block, coef, norm = pl.pallas_call(
        functools.partial(final_kernel, total),
        grid=(4,),
        in_specs=[
            pl.BlockSpec((parts, 32, 256), lambda k: (0, 0, 0)),
            pl.BlockSpec((count, points // 4), lambda k: (0, k)),
        ],
        out_specs=[
            pl.BlockSpec((8, points // 4), lambda k: (0, k)),
            pl.BlockSpec((8, count), lambda k: (0, 0)),
            pl.BlockSpec((8, 8), lambda k: (0, 0)),
        ],
        out_shape=(
            jax.ShapeDtypeStruct((8, points), f32),
            jax.ShapeDtypeStruct((8, count), f32),
            jax.ShapeDtypeStruct((8, 8), f32),
        ),
        scratch_shapes=[pltpu.VMEM((8, count), f32)],
        compiler_params=params(),
        name="finish",
    )(shared, flat)

    inc = channels // 2
    hessenberg = coef.reshape(2, inc, blocks, channels)[..., :inc].transpose(2, 0, 3, 1)
    norm = norm / total
    real_part = norm[:inc, :inc] + norm[inc:, inc:]
    imag_part = norm[:inc, inc:] - norm[inc:, :inc]
    return new_block, hessenberg, jnp.stack([real_part, imag_part], 0)


def solution(mesh):
    in_specs = (P(None, None, "row"), P(None, "row"), P("row"), P())
    out_specs = (P(None, "row"), P(), P())
    return jax.shard_map(local, mesh=mesh, in_specs=in_specs, out_specs=out_specs, check_vma=False)
```

time: 287 us -> 88.7 us (0.31); the launches traced: 283 us -> 88.2 us
  other arithmetic: 157 us -> 4.56 us
  matrix products: 44.9 us -> 0 us
  Pallas kernels: 0 us -> 36.5 us
  blocking collectives: 52 us -> 26.2 us
  waiting for transfers between devices: 11.6 us -> 5.72 us
    another operation x12 -> x6, other arithmetic: 153 us -> 2.76 us
    dot_general x13 -> x0, matrix products: 44.9 us -> none  [the longest x2 21.3 us: project(): return jnp.einsum('jan,bn->jab', krylov_basis, field, precision=highest)]
    pallas_call x0 -> x5, Pallas kernels: none -> 36.5 us  [the longest x1 25.8 us: local(): pl.pallas_call(remote_kernel, out_shape=(half, half), in_specs=[SMEM, VME...]
    all_to_all x3 -> x2, blocking collectives: 52 us -> 26.2 us  [gather_all(): lax.all_to_all(jnp.broadcast_to(x[None], (length, *x.shape)), axis, 0, 0,...]
    all_to_all x2 -> x1, waiting for transfers between devices: 11.6 us -> 5.72 us  [gather_all(): lax.all_to_all(jnp.broadcast_to(x[None], (length, *x.shape)), axis, 0, 0,...]
    all_to_all x2 -> x1, starting transfers between devices: 11.7 us -> 8.33 us  [gather_all(): lax.all_to_all(jnp.broadcast_to(x[None], (length, *x.shape)), axis, 0, 0,...]
  transfers between devices with their start and end apart: 2 -> 2, of which waited for: 2 -> 1; matrix products, arithmetic and copies ran while one was open for 1% -> 0% of each run, Pallas kernels for 0% -> 7%
where the time goes in v1:
time: 88.7 us; the launch traced here: 88.2 us
  Pallas kernels  36.5 us (41%)
  blocking collectives  26.2 us (30%)
  starting transfers between devices  10.2 us (11%)
  waiting for transfers between devices  5.72 us (6%)
  other arithmetic  4.56 us (5%)
  local copies, waits for them, and re-layouts  4.25 us (5%)
    all_to_all x2, blocking collectives, gather_all(): lax.all_to_all(jnp.broadcast_to(x[None], (length, *x.shape)), axis, 0, 0,...  26.2 us
    pallas_call x1, Pallas kernels, local(): pl.pallas_call(remote_kernel, out_shape=(half, half), in_specs=[SMEM, VME...  25.8 us
    all_to_all x1, starting transfers between devices, gather_all(): lax.all_to_all(jnp.broadcast_to(x[None], (length, *x.shape)), axis, 0, 0,...  8.33 us
    all_to_all x1, waiting for transfers between devices, gather_all(): lax.all_to_all(jnp.broadcast_to(x[None], (length, *x.shape)), axis, 0, 0,...  5.72 us
    pallas_call x1, Pallas kernels, local(): pl.pallas_call(local_kernel, out_shape=sums, in_specs=[VMEM, VMEM], out_s...  4.17 us
    pallas_call x1, Pallas kernels, local(): pl.pallas_call(functools.partial(final_kernel, total), grid=(4,), in_spec...  3.3 us
    unnamed x5, local copies, waits for them, and re-layouts  2.85 us
    pallas_call x1, Pallas kernels, local(): pl.pallas_call(gram_kernel, grid_spec=pltpu.PrefetchScalarGridSpec(num_sc...  2.34 us
  transfers between devices with their start and end apart: 2, of which 1 were waited for; matrix products, arithmetic and copies ran while one was open for 0% of the time, Pallas kernels for 7%

profile of v1, /device:TPU:1, one launch (start us, length us, event | category | flops | bytes accessed | tf_op | source)
XLA Modules:
  0.0 88.2 jit_solution(4310190182347407419)
XLA Ops:
  0.6 1.1 %fusion.1 = (bf16[1,4096]{1,0:T(2,128)(2,1)S(1)}, s32[1,4096]{1,0:T(1,128)S(1)}, s32[1,4096]{1,0:T(1,128)S(1)}, bf16[1,4096]{1,0:T(2,128)(2,1)S(1)}, bf16[1,4096...) fusion(s32[3,4096]{1,0:T(4,128)} %param.5), kind=kLoop, calls=%fused_computation.23 | loop fusion | flops 110592 | bytes 114688 | tf_op jit(solution)/shard_map/convert.1
  1.8 0.9 convert.37
  2.7 0.9 select_reduce_fusion
  3.5 0.9 %fusion = bf16[8,4096]{1,0:T(8,128)(2,1)S(1)} fusion(f32[30,8,4096]{2,1,0:T(8,128)} %param.4, f32[4096]{0:T(1024)S(1)} %select_reduce_fusion), kind=kLoop, calls=%fused_computation.4 | loop fusion | flops 65536 | bytes 212992 | tf_op jit(solution)/shard_map/convert_element_type | solution.py:225
  4.5 0.1 concatenate.7
  4.6 0.8 broadcast_in_dim.20
  5.5 8.3 %all-to-all-start = ((bf16[8,16,2048]{2,1,0:T(8,128)(2,1)}), bf16[8,16,2048]{2,1,0:T(8,128)(2,1)S(1)}, u32[]{:S(2)}, u32[]{:S(2)}) async-start(bf16[8,16,2048]{2,1,0:T(8,128)(2,1)} %broadcast_in_dim.20), calls=%async_computation | async-start | bytes 1048576 | tf_op jit(solution)/shard_map/all_to_all | solution.py:196
  13.8 0.2 stack.53
  14.0 0.1 pad_add_fusion.place
  14.1 4.2 %scatter_local.1.begun = f32[16,512]{1,0:T(8,128)S(1)} custom-call(bf16[8,512]{1,0:T(8,128)(2,1)S(1)} %constant_dynamic-slice_fusion.1.targets, bf16[16,2048]{1,0:T(8,128)(2,1)S(1)} %constant_dynamic-slice_fusion.sources), custom_call_target="tpu_custom_call" | custom-call | flops 3000000000 | bytes 200000 | tf_op jit(solution)/shard_map/scatter_local/pallas_call | solution.py:240
  18.3 5.7 %all-to-all-done.sources = bf16[8,16,2048]{2,1,0:T(8,128)(2,1)S(1)} async-done(((bf16[8,16,2048]{2,1,0:T(8,128)(2,1)}), bf16[8,16,2048]{2,1,0:T(8,128)(2,1)S(1)}, u32[]{:S(2)}, u32[]{:S(2)}) %all-to-all-start) | async-done | bytes 524320 | tf_op jit(solution)/shard_map/all_to_all | solution.py:196
  24.0 0.0 copy-start
  24.0 25.8 %scatter_remote.1 = (f32[8,256]{1,0:T(8,128)S(1)}, f32[8,256]{1,0:T(8,128)S(1)}) custom-call(s32[4]{0:T(128)S(1)} %pad_add_fusion.place, bf16[8,512]{1,0:T(8,128)(2,1)S(1)} %constant_dynamic-slice_fusion.1.targets, bf16[8,16,2048]{2,1,0:T(8,128)(2,1)S(1)} %all-to-all-done.sources, f32[16,512]{1,0:T(8,128)S(1)} %scatter_local.1.begun), custom_call_target="tpu_custom_call" | custom-call | flops 20000000000 | bytes 800000 | tf_op jit(solution)/shard_map/scatter_remote/pallas_call | solution.py:266
  49.8 1.9 %collective-permute-start = (f32[8,256]{1,0:T(8,128)S(1)}, f32[8,256]{1,0:T(8,128)S(1)}, u32[]{:S(2)}, u32[]{:S(2)}) collective-permute-start(f32[8,256]{1,0:T(8,128)S(1)} %get-tuple-element.11), channel_id=1, source_target_pairs={{0,1},{1,0},{2,3},{3,2},{4,5},{5,4},{6,7},{7,6},{8,9},{9,8},{10,11... | collective-permute-start | bytes 24584 | tf_op jit(solution)/shard_map/ppermute | solution.py:276
  51.7 0.0 copy-done
  51.7 2.3 %basis_gram.1.gram = f32[16,256]{1,0:T(8,128)S(1)} custom-call(s32[4]{0:T(128)S(1)} %pad_add_fusion.place, f32[240,4096]{1,0:T(8,128)S(1)} %bitcast.15), custom_call_target="tpu_custom_call" | custom-call | flops 2000000000 | bytes 4000000 | tf_op jit(solution)/shard_map/basis_gram/pallas_call | solution.py:251
  54.0 0.0 collective-permute-done.got
  54.1 0.9 %project.1 = (f32[8,256]{1,0:T(8,128)S(1)}, f32[24,256]{1,0:T(8,128)S(1)}) custom-call(s32[4]{0:T(128)S(1)} %pad_add_fusion.place, f32[8,256]{1,0:T(8,128)S(1)} %get-tuple-element.10.keep, f32[8,256]{1,0:T(8,128)S(1)} %collective-permute-done.got, f32[240,4096]{1,0:T(8,128)S(1)} %bitcast.16, f32[240,4096]{1,0:T(8,128)S(1)} %bitcast.17, ...), custom_call_target="tpu_custom_call" | custom-call | tf_op jit(solution)/shard_map/project/pallas_call | solution.py:278
  55.0 10.2 %all_to_all.15 = f32[8,24,256]{2,1,0:T(8,128)S(1)} all-to-all(f32[8,24,256]{2,1,0:T(8,128)S(1)} %broadcast_in_dim.21), channel_id=1, replica_groups=mesh['row'=8,'col'=8,'grp'=2] {'row'}, dimensions={0} | all-to-all | bytes 393216 | tf_op jit(solution)/shard_map/all_to_all | solution.py:196
  65.3 15.9 %all_to_all.16.shared = f32[16,32,256]{2,1,0:T(8,128)S(1)} all-to-all(f32[16,32,256]{2,1,0:T(8,128)S(1)} %broadcast_in_dim.22), channel_id=1, replica_groups=mesh['row'=8,'col'=8,'grp'=2] {'col','grp'}, dimensions={0} | all-to-all | bytes 1048576 | tf_op jit(solution)/shard_map/all_to_all | solution.py:196
  81.3 0.0 copy-start.1
  81.3 2.1 %copy-done.1 = f32[30,8,4096]{2,1,0:T(8,128)S(1)} copy-done((f32[30,8,4096]{2,1,0:T(8,128)S(1)}, f32[30,8,4096]{2,1,0:T(8,128)}, u32[]{:S(2)}) %copy-start.1) | copy-done | bytes 3932184
  83.4 3.3 %finish.1 = (f32[8,4096]{1,0:T(8,128)}, f32[8,240]{1,0:T(8,128)S(1)}, f32[8,8]{1,0:T(8,128)S(1)}) custom-call(f32[16,32,256]{2,1,0:T(8,128)S(1)} %all_to_all.16.shared, f32[240,4096]{1,0:T(8,128)S(1)} %bitcast.18), custom_call_target="tpu_custom_call" | custom-call | tf_op jit(solution)/shard_map/finish/pallas_call | solution.py:303
  86.7 0.1 add_bitcast_fusion
  86.8 0.1 reshape.19
  86.9 0.7 copy.9
  87.6 0.6 pad_maximum_fusion.1
  (13 shorter events, 0.2 us)
Async XLA Ops:
  5.5 18.5 %all-to-all-start = ((bf16[8,16,2048]{2,1,0:T(8,128)(2,1)}), bf16[8,16,2048]{2,1,0:T(8,128)(2,1)S(1)}, u32[]{:S(2)}, u32[]{:S(2)}) async-start(bf16[8,16,2048]{2,1,0:T(8,128)(2,1)} %broadcast_in_dim.20), calls=%async_computation | async-start | bytes 1048576 | tf_op jit(solution)/shard_map/all_to_all | solution.py:196
  24.0 27.7 %copy-start = (f32[30,8,4096]{2,1,0:T(8,128)S(1)}, f32[30,8,4096]{2,1,0:T(8,128)}, u32[]{:S(2)}) copy-start(f32[30,8,4096]{2,1,0:T(8,128)} %param.4) | copy-start | bytes 11796484
  49.8 4.2 %collective-permute-start = (f32[8,256]{1,0:T(8,128)S(1)}, f32[8,256]{1,0:T(8,128)S(1)}, u32[]{:S(2)}, u32[]{:S(2)}) collective-permute-start(f32[8,256]{1,0:T(8,128)S(1)} %get-tuple-element.11), channel_id=1, source_target_pairs={{0,1},{1,0},{2,3},{3,2},{4,5},{5,4},{6,7},{7,6},{8,9},{9,8},{10,11... | collective-permute-start | bytes 24584 | tf_op jit(solution)/shard_map/ppermute | solution.py:276
  81.3 2.1 %copy-start.1 = (f32[30,8,4096]{2,1,0:T(8,128)S(1)}, f32[30,8,4096]{2,1,0:T(8,128)}, u32[]{:S(2)}) copy-start(f32[30,8,4096]{2,1,0:T(8,128)} %param.4) | copy-start | bytes 11796484

commit v2 on v1

v2 whole, which is shorter than its diff:
```python
import functools

import jax
import jax.numpy as jnp
import numpy as np
from jax import lax
from jax.experimental import pallas as pl
from jax.experimental.pallas import tpu as pltpu
from jax.sharding import PartitionSpec as P

f32 = jnp.float32
bf16 = jnp.bfloat16
highest = lax.Precision.HIGHEST
NT = (((1,), (1,)), ((), ()))
TN = (((0,), (0,)), ((), ()))

SINE = (4.4428816249751035, -7.307782340256801, 3.5971494246649565, -0.7893218692014636)
SUB = 256
STEP = 512


def green_pair(squared, masked):
    if masked:
        distinct = squared > 0.5
        squared = jnp.maximum(squared, 1.0)
    inverse = lax.rsqrt(squared)
    turns = (squared * inverse) * np.float32(1.0 / np.pi)
    part = turns - jnp.round(turns)
    z = part * part
    poly = z * np.float32(SINE[3]) + np.float32(SINE[2])
    poly = poly * z + np.float32(SINE[1])
    poly = poly * z + np.float32(SINE[0])
    sine = part * poly
    rest = 2.0 - sine * sine
    both = rest * inverse
    real_part = both - inverse
    imag_part = (sine * both) * lax.rsqrt(rest)
    if masked:
        real_part = jnp.where(distinct, real_part, 0.0)
        imag_part = jnp.where(distinct, imag_part, 0.0)
    return real_part.astype(bf16), imag_part.astype(bf16)


def scatter_tiles(tiles, read, targets, held, acc, masked):
    width = targets.shape[1]

    def fill(i, slot):
        sites = read(i, 8)
        held[slot] = lax.dot_general(sites, targets[...], TN, preferred_element_type=f32)

    def work(i, slot):
        weights = read(i, 0)
        for k in range(width // SUB):
            cut = slice(k * SUB, (k + 1) * SUB)
            real_part, imag_part = green_pair(held[slot, :, cut], masked)
            acc[0:8, cut] += jnp.dot(weights, real_part, preferred_element_type=f32)
            acc[8:16, cut] += jnp.dot(weights, imag_part, preferred_element_type=f32)

    fill(0, 0)

    def body(h, carry):
        i = 2 * h
        fill(i + 1, 1)
        work(i, 0)
        fill(jnp.minimum(i + 2, tiles - 1), 0)
        work(i + 1, 1)
        return carry

    lax.fori_loop(0, tiles // 2, body, 0)


def local_kernel(targets, sources, gram, acc, held):
    del gram
    acc[...] = jnp.zeros_like(acc)

    def read(i, first):
        return sources[first : first + 8, pl.ds(pl.multiple_of(i * STEP, STEP), STEP)]

    scatter_tiles(sources.shape[1] // STEP, read, targets, held, acc, True)


def remote_kernel(place, targets, sources, begun, keep, send, held, acc):
    rows, _, length = sources.shape
    per_row = length // STEP
    row = place[0]
    acc[...] = begun[...]

    def read(i, first):
        chunk = lax.rem(row + 1 + i // per_row, rows)
        off = pl.multiple_of(lax.rem(i, per_row) * STEP, STEP)
        return sources[chunk, first : first + 8, pl.ds(off, STEP)]

    scatter_tiles((rows - 1) * per_row, read, targets, held, acc, False)
    real = acc[0:8]
    imag = acc[8:16]
    upper = real[0:4] - imag[4:8]
    lower = real[4:8] + imag[0:4]
    both = jnp.concatenate([upper, lower], 0)
    half = both.shape[1] // 2
    first, second = both[:, :half], both[:, half:]
    mine = place[1] == 0
    keep[...] = jnp.where(mine, first, second)
    send[...] = jnp.where(mine, second, first)


def split(x):
    high = x.astype(bf16)
    return high, (x - high.astype(f32)).astype(bf16)


def swap_parts(x, rows):
    lane = lax.broadcasted_iota(jnp.int32, x.shape, 1)
    width = x.shape[1]
    rolled = pltpu.roll(x, rows - 4, 0)
    return jnp.where((lane & 4) == 0, pltpu.roll(rolled, width - 4, 1), pltpu.roll(rolled, 4, 1))


def complex_mix(products):
    lane = lax.broadcasted_iota(jnp.int32, products.shape, 1)
    sub = lax.broadcasted_iota(jnp.int32, products.shape, 0)
    swapped = swap_parts(products, products.shape[0])
    same = ((lane & 4) == 0) == ((sub & 4) == 0)
    return products + jnp.where(same, swapped, -swapped)


def prepare_kernel(place, table, direction, lattice, index, spread, sources, targets):
    rows, _, length = spread.shape
    wide = targets.shape[1]

    def sites(first, count, aim):
        part = lattice[:, pl.ds(pl.multiple_of(first, 128), count)]
        x, y, z = part[0:1], part[1:2], part[2:3]
        norm = x * x + y * y + z * z
        high = lax.shift_right_logical(norm, 8)
        low = norm & 255
        one = jnp.ones_like(x)
        if aim:
            parts = [-2 * x, -2 * y, -2 * z, 256 * one, one, 256 * high, low, 0 * one]
        else:
            parts = [x, y, z, high, low, one, one, 0 * one]
        return jnp.concatenate([p.astype(f32) for p in parts], 0).astype(bf16)

    targets[...] = sites(place[4], wide, True)
    start = pl.multiple_of(place[5], 128)
    chosen = index[:, pl.ds(start, length)]
    strength = jnp.zeros(chosen.shape, f32)
    for k in range(table.shape[0]):
        strength = jnp.where(chosen == k, table[k], strength)
    weighted = (direction[:, pl.ds(start, length)] * strength).astype(bf16)
    packed = jnp.concatenate([weighted, sites(start, length, False)], 0)
    sources[...] = packed
    for k in range(rows):
        spread[k] = packed


def gram_kernel(place, basis, gram, high, low):
    count, points = basis.shape
    chunk = 512
    start = pl.multiple_of(place[2], 16)
    total = jnp.zeros((16, count), f32)
    for k in range(points // chunk):
        cut = slice(k * chunk, (k + 1) * chunk)
        top, rest = split(basis[:, cut])
        high[:, cut] = top
        low[:, cut] = rest
        own = jnp.concatenate([high[pl.ds(start, 16), cut], low[pl.ds(start, 16), cut]], 0)
        first = lax.dot_general(own, top, NT, preferred_element_type=f32)
        second = lax.dot_general(own[:16], rest, NT, preferred_element_type=f32)
        total = total + (first[:16] + first[16:] + second)
    total = jnp.concatenate([total, jnp.zeros((16, 256 - count), f32)], 1)
    mixed = complex_mix(total)
    gram[...] = jnp.concatenate([mixed[0:4], mixed[8:12]], 0)


def project_kernel(place, keep, got, direction, high, low, gram, initial, packed):
    field = direction[...] - (keep[...] + got[...])
    initial[...] = field
    count = high.shape[0]
    width = field.shape[1]
    cut = pl.ds(pl.multiple_of(place[3] * width, 128), width)
    field_high, field_low = split(field)
    both = jnp.concatenate([field_high, field_low], 0)
    first = lax.dot_general(both, high[:, cut], NT, preferred_element_type=f32)
    second = lax.dot_general(field_high, low[:, cut], NT, preferred_element_type=f32)
    own = lax.dot_general(field, field, NT, preferred_element_type=f32, precision=highest)
    rest = jnp.zeros((8, 256 - count - 8), f32)
    packed[0:8, :] = jnp.concatenate([first[:8] + first[8:] + second, own, rest], 1)
    packed[8:, :] = gram[...]


def final_kernel(total, shared, high, low, new, coef, norm, grams):
    parts = shared.shape[0]
    count, points = high.shape
    width = shared.shape[2]
    scale = np.float32(1.0 / total)
    sums = shared[0, 8:16, :]
    for q in range(1, parts):
        sums = sums + shared[q, 8:16, :]
    lane = lax.broadcasted_iota(jnp.int32, sums.shape, 1)
    sub = lax.broadcasted_iota(jnp.int32, sums.shape, 0)
    grams[...] = jnp.zeros_like(grams)
    for q in range(count // 16):
        part = shared[q, 16:24, :]
        grams[16 * q : 16 * q + 8, :] = jnp.where(sub < 4, part, 0.0)
        grams[16 * q + 8 : 16 * q + 16, :] = jnp.where(sub < 4, pltpu.roll(part, 4, 0), 0.0)

    def times_gram(x):
        return complex_mix(
            jnp.dot(x, grams[...], preferred_element_type=f32, precision=highest)
        )

    products = jnp.where(lane < count, complex_mix(sums), 0.0)
    once = products * scale
    mix = 2.0 * once - times_gram(once) * scale
    seen = products - 0.5 * times_gram(mix)
    cross = lax.dot_general(mix, seen, NT, preferred_element_type=f32, precision=highest)
    cross_t = lax.dot_general(seen, mix, NT, preferred_element_type=f32, precision=highest)
    own = complex_mix(pltpu.roll(sums, width - count, 1))[:, 0:8]
    result = (own - cross - cross_t) * scale
    norm[0] = result[0:4, 0:4]
    norm[1] = result[0:4, 4:8]

    row = lax.broadcasted_iota(jnp.int32, (width, 128), 0)
    column = lax.broadcasted_iota(jnp.int32, (width, 128), 1)
    wanted = ((row & 4) == 0) & (column == (row & 7) * 32 + lax.shift_right_logical(row, 3))
    chosen = jnp.dot(
        mix, jnp.where(wanted, 1.0, 0.0), preferred_element_type=f32, precision=highest
    )
    blocks = coef.shape[3]
    for k in range(4):
        moved = pltpu.roll(chosen, (128 - 32 * k) % 128, 1)
        coef[0, k] = moved[0:4, 0:blocks]
        coef[1, k] = moved[4:8, 0:blocks]

    mix_high, mix_low = split(mix[:, :count])
    both = jnp.concatenate([mix_high, mix_low], 0)
    chunk = 4 * width
    for k in range(points // chunk):
        cut = slice(k * chunk, (k + 1) * chunk)
        first = jnp.dot(both, high[:, cut], preferred_element_type=f32)
        second = jnp.dot(mix_high, low[:, cut], preferred_element_type=f32)
        field = jnp.concatenate([shared[4 * k + i, 0:8, :] for i in range(4)], 1)
        new[:, cut] = field - (first[:8] + first[8:] + second)


def gather_all(x, axis):
    length = lax.axis_size(axis)
    return lax.all_to_all(jnp.broadcast_to(x[None], (length, *x.shape)), axis, 0, 0, tiled=True)


VMEM = pl.BlockSpec(memory_space=pltpu.VMEM)
SMEM = pl.BlockSpec(memory_space=pltpu.SMEM)
ANY = pl.BlockSpec(memory_space=pl.ANY)


def params():
    return pltpu.CompilerParams(vmem_limit_bytes=16 << 20)


def cost(flops, size):
    return pl.CostEstimate(flops=flops, bytes_accessed=size, transcendentals=0)


def local(krylov_basis, lattice, strength_index, strength_table):
    blocks, channels, points = krylov_basis.shape
    inc = channels // 2
    count = blocks * channels
    rows = lax.axis_size("row")
    groups = lax.axis_size("grp")
    parts = lax.axis_size(("col", "grp"))
    row, col, grp = lax.axis_index("row"), lax.axis_index("col"), lax.axis_index("grp")
    part = lax.axis_index(("col", "grp"))
    total = points * rows
    own = points // parts
    wide = own * groups
    length = points // groups
    flat = krylov_basis.reshape(count, points)
    place = jnp.stack(
        [row, grp, jnp.minimum(part * 16, count - 16), part, col * wide, grp * length]
    ).astype(jnp.int32)

    spread, sources, targets = pl.pallas_call(
        prepare_kernel,
        grid=(1,),
        in_specs=[
            SMEM,
            SMEM,
            pl.BlockSpec((channels, points), lambda k: (blocks - 1, 0)),
            pl.BlockSpec((3, points), lambda k: (0, 0)),
            pl.BlockSpec((1, points), lambda k: (0, 0)),
        ],
        out_specs=(VMEM, VMEM, VMEM),
        out_shape=(
            jax.ShapeDtypeStruct((rows, 16, length), bf16),
            jax.ShapeDtypeStruct((16, length), bf16),
            jax.ShapeDtypeStruct((8, wide), bf16),
        ),
        compiler_params=params(),
        name="prepare",
    )(place, strength_table, flat, lattice, strength_index[None, :])
    gathered = lax.all_to_all(spread, "row", 0, 0, tiled=True)

    gram, high, low = pl.pallas_call(
        gram_kernel,
        in_specs=[SMEM, VMEM],
        out_specs=(VMEM, VMEM, VMEM),
        out_shape=(
            jax.ShapeDtypeStruct((8, 256), f32),
            jax.ShapeDtypeStruct((count, points), bf16),
            jax.ShapeDtypeStruct((count, points), bf16),
        ),
        compiler_params=params(),
        cost_estimate=cost(2_000_000_000, 8_000_000),
        name="basis_gram",
    )(place, flat)

    held = pltpu.VMEM((2, STEP, wide), f32)
    begun = pl.pallas_call(
        local_kernel,
        out_shape=jax.ShapeDtypeStruct((16, wide), f32),
        in_specs=[VMEM, VMEM, ANY],
        out_specs=VMEM,
        scratch_shapes=[held],
        compiler_params=params(),
        cost_estimate=cost(3_000_000_000, 200_000),
        name="scatter_local",
    )(targets, sources, gram)

    half = jax.ShapeDtypeStruct((channels, own), f32)
    keep, send = pl.pallas_call(
        remote_kernel,
        out_shape=(half, half),
        in_specs=[SMEM, VMEM, VMEM, VMEM],
        out_specs=(VMEM, VMEM),
        scratch_shapes=[held, pltpu.VMEM((16, wide), f32)],
        compiler_params=params(),
        cost_estimate=cost(20_000_000_000, 800_000),
        name="scatter_remote",
    )(place, targets, gathered, begun)
    got = lax.ppermute(send, "grp", [(i, groups - 1 - i) for i in range(groups)])

    initial, partial = pl.pallas_call(
        project_kernel,
        grid_spec=pltpu.PrefetchScalarGridSpec(
            num_scalar_prefetch=1,
            grid=(1,),
            in_specs=[
                VMEM,
                VMEM,
                pl.BlockSpec((channels, own), lambda k, s: (blocks - 1, s[3])),
                VMEM,
                VMEM,
                VMEM,
            ],
            out_specs=[VMEM, VMEM],
        ),
        out_shape=(half, jax.ShapeDtypeStruct((16, 256), f32)),
        compiler_params=params(),
        name="project",
    )(place, keep, got, flat, high, low, gram)

    row_sums = jnp.sum(gather_all(partial, "row"), axis=0)
    shared = gather_all(jnp.concatenate([initial, row_sums], 0), ("col", "grp"))

    new_block, coef, norm = pl.pallas_call(
        functools.partial(final_kernel, total),
        in_specs=[VMEM, VMEM, VMEM],
        out_specs=(VMEM, VMEM, VMEM),
        out_shape=(
            jax.ShapeDtypeStruct((channels, points), f32),
            jax.ShapeDtypeStruct((2, inc, inc, blocks), f32),
            jax.ShapeDtypeStruct((2, inc, inc), f32),
        ),
        scratch_shapes=[pltpu.VMEM((256, 256), f32)],
        compiler_params=params(),
        name="finish",
    )(shared, high, low)
    return new_block, coef.transpose(3, 0, 1, 2), norm


def solution(mesh):
    in_specs = (P(None, None, "row"), P(None, "row"), P("row"), P())
    out_specs = (P(None, "row"), P(), P())
    return jax.shard_map(local, mesh=mesh, in_specs=in_specs, out_specs=out_specs, check_vma=False)
```

time: 88.7 us -> 83.7 us (0.944)
  local copies, waits for them, and re-layouts: 4.25 us -> 9.49 us
  other arithmetic: 4.56 us -> 0.02 us
  waiting for transfers between devices: 5.72 us -> 1.37 us
  Pallas kernels: 36.5 us -> 34.7 us
    unnamed x5 -> x18, local copies, waits for them, and re-layouts: 2.85 us -> 9.36 us
    all_to_all x1, waiting for transfers between devices: 5.72 us -> 0.54 us  [local(): gathered = lax.all_to_all(spread, 'row', 0, 0, tiled=True)]
    another operation x6 -> x0, other arithmetic: 2.76 us -> none
    pallas_call x1, Pallas kernels: 25.8 us -> 24.1 us  [local(): pl.pallas_call(remote_kernel, out_shape=(half, half), in_specs=[SMEM, VME...]
    convert_element_type x1 -> x0, other arithmetic: 0.92 us -> none  [local(): weighted = (direction * strength[None, :]).astype(bf16)]
    pallas_call x3 -> x4, Pallas kernels: 9.81 us -> 9.78 us  [the longest x1 3.87 us: local(): pl.pallas_call(local_kernel, out_shape=jax.ShapeDtypeStruct((16, wide), f...]
  transfers between devices with their start and end apart: 2 -> 2, of which waited for: 1 -> 2; matrix products, arithmetic and copies ran while one was open for 0% -> 0% of each run, Pallas kernels for 7% -> 7%
where the time goes in v2:
time: 83.7 us; the launch traced here: 83.2 us
  Pallas kernels  34.7 us (41%)
  blocking collectives  26.9 us (32%)
  starting transfers between devices  10 us (12%)
  local copies, waits for them, and re-layouts  9.49 us (11%)
  waiting for transfers between devices  1.37 us (2%)
    all_to_all x2, blocking collectives, gather_all(): lax.all_to_all(jnp.broadcast_to(x[None], (length, *x.shape)), axis, 0, 0,...  26.9 us
    pallas_call x1, Pallas kernels, local(): pl.pallas_call(remote_kernel, out_shape=(half, half), in_specs=[SMEM, VME...  24.1 us
    unnamed x18, local copies, waits for them, and re-layouts  9.36 us
    all_to_all x1, starting transfers between devices, local(): gathered = lax.all_to_all(spread, 'row', 0, 0, tiled=True)  8.33 us
    pallas_call x1, Pallas kernels, local(): pl.pallas_call(local_kernel, out_shape=jax.ShapeDtypeStruct((16, wide), f...  3.87 us
    pallas_call x1, Pallas kernels, local(): pl.pallas_call(gram_kernel, in_specs=[SMEM, VMEM], out_specs=(VMEM, VMEM,...  2.29 us
    pallas_call x1, Pallas kernels, local(): pl.pallas_call(functools.partial(final_kernel, total), in_specs=[VMEM, VM...  2.18 us
    ppermute x1, starting transfers between devices, local(): lax.ppermute(send, 'grp', [(i, groups - 1 - i) for i in range(groups)])  1.72 us
  transfers between devices with their start and end apart: 2, of which 2 were waited for; matrix products, arithmetic and copies ran while one was open for 0% of the time, Pallas kernels for 7%

profile of v2, /device:TPU:1, one launch (start us, length us, event | category | flops | bytes accessed | tf_op | source)
XLA Modules:
  0.0 83.2 jit_solution(8314878536206682600)
XLA Ops:
  0.6 0.1 stack.27.place
  0.7 0.0 copy-start
  0.7 2.1 %copy-done = f32[30,8,4096]{2,1,0:T(8,128)S(1)} copy-done((f32[30,8,4096]{2,1,0:T(8,128)S(1)}, f32[30,8,4096]{2,1,0:T(8,128)}, u32[]{:S(2)}) %copy-start) | copy-done | bytes 3932184
  2.8 0.0 copy-start.6
  2.8 0.8 %copy-done.6 = s32[3,4096]{1,0:T(4,128)S(1)} copy-done((s32[3,4096]{1,0:T(4,128)S(1)}, s32[3,4096]{1,0:T(4,128)}, u32[]{:S(2)}) %copy-start.6) | copy-done | bytes 49176
  3.7 0.0 copy-start.7
  3.7 0.7 copy-done.7
  4.4 0.0 copy-start.8
  4.4 0.7 copy-done.8
  5.1 1.4 %prepare.1 = (bf16[8,16,2048]{2,1,0:T(8,128)(2,1)}, bf16[16,2048]{1,0:T(8,128)(2,1)S(1)}, bf16[8,512]{1,0:T(8,128)(2,1)S(1)}) custom-call(s32[6]{0:T(128)S(1)} %stack.27.place, f32[16]{0:T(128)S(1)} %copy-done.8, f32[240,4096]{1,0:T(8,128)S(1)} %bitcast.9, s32[3,4096]{1,0:T(4,128)S(1)} %copy-done.6, s32[1,4096]{1,0:T(1,128)S(1)} %bitcast.12), custom_call_target="tpu_custom_call" | custom-call | tf_op jit(solution)/shard_map/prepare/pallas_call | solution.py:282
  6.5 8.3 %all-to-all-start = ((bf16[8,16,2048]{2,1,0:T(8,128)(2,1)}), bf16[8,16,2048]{2,1,0:T(8,128)(2,1)S(1)}, u32[]{:S(2)}, u32[]{:S(2)}) async-start(bf16[8,16,2048]{2,1,0:T(8,128)(2,1)} %get-tuple-element.17), calls=%async_computation | async-start | bytes 1048576 | tf_op jit(solution)/shard_map/all_to_all | solution.py:301
  14.8 0.0 copy-start.1
  14.8 2.1 %copy-done.1 = f32[30,8,4096]{2,1,0:T(8,128)S(1)} copy-done((f32[30,8,4096]{2,1,0:T(8,128)S(1)}, f32[30,8,4096]{2,1,0:T(8,128)}, u32[]{:S(2)}) %copy-start.1) | copy-done | bytes 3932184
  16.9 2.3 %basis_gram.1 = (f32[8,256]{1,0:T(8,128)S(1)}, bf16[240,4096]{1,0:T(8,128)(2,1)S(1)}, bf16[240,4096]{1,0:T(8,128)(2,1)S(1)}) custom-call(s32[6]{0:T(128)S(1)} %stack.27.place, f32[240,4096]{1,0:T(8,128)S(1)} %bitcast.10), custom_call_target="tpu_custom_call" | custom-call | flops 2000000000 | bytes 8000000 | tf_op jit(solution)/shard_map/basis_gram/pallas_call | solution.py:303
  19.2 0.1 copy-start.3
  19.3 1.3 %copy-done.3 = bf16[240,4096]{1,0:T(8,128)(2,1)} copy-done((bf16[240,4096]{1,0:T(8,128)(2,1)}, bf16[240,4096]{1,0:T(8,128)(2,1)S(1)}, u32[]{:S(2)}) %copy-start.3) | copy-done | bytes 1966104
  20.6 3.9 %scatter_local.1.begun = f32[16,512]{1,0:T(8,128)S(1)} custom-call(bf16[8,512]{1,0:T(8,128)(2,1)S(1)} %get-tuple-element.16.targets, bf16[16,2048]{1,0:T(8,128)(2,1)S(1)} %get-tuple-element.18.sources, f32[8,256]{1,0:T(8,128)S(1)} %get-tuple-element.19.gram), custom_call_target="tpu_custom_call" | custom-call | flops 3000000000 | bytes 200000 | tf_op jit(solution)/shard_map/scatter_local/pallas_call | solution.py:318
  24.5 0.5 all-to-all-done.sources
  25.0 0.0 copy-start.2
  25.0 0.0 copy-start.4
  25.0 24.1 %scatter_remote.1 = (f32[8,256]{1,0:T(8,128)S(1)}, f32[8,256]{1,0:T(8,128)S(1)}) custom-call(s32[6]{0:T(128)S(1)} %stack.27.place, bf16[8,512]{1,0:T(8,128)(2,1)S(1)} %get-tuple-element.16.targets, bf16[8,16,2048]{2,1,0:T(8,128)(2,1)S(1)} %all-to-all-done.sources, f32[16,512]{1,0:T(8,128)S(1)} %scatter_local.1.begun), custom_call_target="tpu_custom_call" | custom-call | flops 20000000000 | bytes 800000 | tf_op jit(solution)/shard_map/scatter_remote/pallas_call | solution.py:330
  49.1 1.7 %collective-permute-start = (f32[8,256]{1,0:T(8,128)S(1)}, f32[8,256]{1,0:T(8,128)S(1)}, u32[]{:S(2)}, u32[]{:S(2)}) collective-permute-start(f32[8,256]{1,0:T(8,128)S(1)} %get-tuple-element.21), channel_id=1, source_target_pairs={{0,1},{1,0},{2,3},{3,2},{4,5},{5,4},{6,7},{7,6},{8,9},{9,8},{10,11... | collective-permute-start | bytes 24584 | tf_op jit(solution)/shard_map/ppermute | solution.py:340
  50.9 0.8 collective-permute-done.got
  51.7 0.0 copy-done.2
  51.7 0.0 copy-done.4
  51.7 0.8 project.1
  52.5 12.5 %all_to_all.15 = f32[8,16,256]{2,1,0:T(8,128)S(1)} all-to-all(f32[8,16,256]{2,1,0:T(8,128)S(1)} %broadcast_in_dim.7), channel_id=1, replica_groups=mesh['row'=8,'col'=8,'grp'=2] {'row'}, dimensions={0} | all-to-all | bytes 262144 | tf_op jit(solution)/shard_map/all_to_all | solution.py:248
  65.0 14.4 %all_to_all.16.shared = f32[16,24,256]{2,1,0:T(8,128)S(1)} all-to-all(f32[16,24,256]{2,1,0:T(8,128)S(1)} %broadcast_in_dim.8), channel_id=1, replica_groups=mesh['row'=8,'col'=8,'grp'=2] {'col','grp'}, dimensions={0} | all-to-all | bytes 786432 | tf_op jit(solution)/shard_map/all_to_all | solution.py:248
  79.5 0.0 copy-start.5
  79.5 1.5 %copy-done.5 = bf16[240,4096]{1,0:T(8,128)(2,1)S(1)} copy-done((bf16[240,4096]{1,0:T(8,128)(2,1)S(1)}, bf16[240,4096]{1,0:T(8,128)(2,1)}, u32[]{:S(2)}) %copy-start.5) | copy-done | bytes 1966104
  81.0 2.2 %finish.1 = (f32[8,4096]{1,0:T(8,128)}, f32[2,4,4,30]{3,2,1,0:T(4,128)}, f32[2,4,4]{2,1,0:T(4,128)}) custom-call(f32[16,24,256]{2,1,0:T(8,128)S(1)} %all_to_all.16.shared, bf16[240,4096]{1,0:T(8,128)(2,1)S(1)} %get-tuple-element.22.high, bf16[240,4096]{1,0:T(8,128)(2,1)S(1)} %copy-done.5), custom_call_target="tpu_custom_call" | custom-call | tf_op jit(solution)/shard_map/finish/pallas_call | solution.py:365
  (4 shorter events, 0.1 us)
Async XLA Ops:
  0.7 2.1 %copy-start = (f32[30,8,4096]{2,1,0:T(8,128)S(1)}, f32[30,8,4096]{2,1,0:T(8,128)}, u32[]{:S(2)}) copy-start(f32[30,8,4096]{2,1,0:T(8,128)} %param.4) | copy-start | bytes 11796484
  2.8 0.8 %copy-start.6 = (s32[3,4096]{1,0:T(4,128)S(1)}, s32[3,4096]{1,0:T(4,128)}, u32[]{:S(2)}) copy-start(s32[3,4096]{1,0:T(4,128)} %lattice.1) | copy-start | bytes 147460
  3.7 0.7 copy-start.7
  4.4 0.7 copy-start.8
  6.5 18.5 %all-to-all-start = ((bf16[8,16,2048]{2,1,0:T(8,128)(2,1)}), bf16[8,16,2048]{2,1,0:T(8,128)(2,1)S(1)}, u32[]{:S(2)}, u32[]{:S(2)}) async-start(bf16[8,16,2048]{2,1,0:T(8,128)(2,1)} %get-tuple-element.17), calls=%async_computation | async-start | bytes 1048576 | tf_op jit(solution)/shard_map/all_to_all | solution.py:301
  14.8 2.1 %copy-start.1 = (f32[30,8,4096]{2,1,0:T(8,128)S(1)}, f32[30,8,4096]{2,1,0:T(8,128)}, u32[]{:S(2)}) copy-start(f32[30,8,4096]{2,1,0:T(8,128)} %param.4) | copy-start | bytes 11796484
  19.2 1.4 %copy-start.3 = (bf16[240,4096]{1,0:T(8,128)(2,1)}, bf16[240,4096]{1,0:T(8,128)(2,1)S(1)}, u32[]{:S(2)}) copy-start(bf16[240,4096]{1,0:T(8,128)(2,1)S(1)} %get-tuple-element.23.low) | copy-start | bytes 5898244
  25.0 26.7 %copy-start.2 = (f32[30,8,4096]{2,1,0:T(8,128)S(1)}, f32[30,8,4096]{2,1,0:T(8,128)}, u32[]{:S(2)}) copy-start(f32[30,8,4096]{2,1,0:T(8,128)} %param.4) | copy-start | bytes 11796484
  25.0 26.7 %copy-start.4 = (bf16[240,4096]{1,0:T(8,128)(2,1)S(1)}, bf16[240,4096]{1,0:T(8,128)(2,1)}, u32[]{:S(2)}) copy-start(bf16[240,4096]{1,0:T(8,128)(2,1)} %copy-done.3) | copy-start | bytes 5898244
  49.1 2.5 %collective-permute-start = (f32[8,256]{1,0:T(8,128)S(1)}, f32[8,256]{1,0:T(8,128)S(1)}, u32[]{:S(2)}, u32[]{:S(2)}) collective-permute-start(f32[8,256]{1,0:T(8,128)S(1)} %get-tuple-element.21), channel_id=1, source_target_pairs={{0,1},{1,0},{2,3},{3,2},{4,5},{5,4},{6,7},{7,6},{8,9},{9,8},{10,11... | collective-permute-start | bytes 24584 | tf_op jit(solution)/shard_map/ppermute | solution.py:340
  79.5 1.5 %copy-start.5 = (bf16[240,4096]{1,0:T(8,128)(2,1)S(1)}, bf16[240,4096]{1,0:T(8,128)(2,1)}, u32[]{:S(2)}) copy-start(bf16[240,4096]{1,0:T(8,128)(2,1)} %copy-done.3) | copy-start | bytes 5898244

commit v3 on v2

--- a/solution.py
+++ b/solution.py
@@ -69,16 +69,6 @@
     lax.fori_loop(0, tiles // 2, body, 0)
 
 
-def local_kernel(targets, sources, gram, acc, held):
-    del gram
-    acc[...] = jnp.zeros_like(acc)
-
-    def read(i, first):
-        return sources[first : first + 8, pl.ds(pl.multiple_of(i * STEP, STEP), STEP)]
-
-    scatter_tiles(sources.shape[1] // STEP, read, targets, held, acc, True)
-
-
 def remote_kernel(place, targets, sources, begun, keep, send, held, acc):
     rows, _, length = sources.shape
     per_row = length // STEP
@@ -123,44 +113,78 @@
     return products + jnp.where(same, swapped, -swapped)
 
 
-def prepare_kernel(place, table, direction, lattice, index, spread, sources, targets):
+def prepare_kernel(place, basis, lattice, index, table, spread, sources, targets, *scratch):
+    direction, chosen, held_table, points, aims, sems = scratch
     rows, _, length = spread.shape
     wide = targets.shape[1]
-
-    def sites(first, count, aim):
-        part = lattice[:, pl.ds(pl.multiple_of(first, 128), count)]
+    channels = direction.shape[0]
+    aim = pl.multiple_of(place[4], 128)
+    start = pl.multiple_of(place[5], 128)
+    last = basis.shape[0] - channels
+    copies = [
+        pltpu.make_async_copy(lattice.at[:, pl.ds(start, length)], points, sems.at[0]),
+        pltpu.make_async_copy(index.at[:, pl.ds(start, length)], chosen, sems.at[1]),
+        pltpu.make_async_copy(table, held_table, sems.at[2]),
+        pltpu.make_async_copy(
+            basis.at[last : last + channels, pl.ds(start, length)], direction, sems.at[3]
+        ),
+        pltpu.make_async_copy(lattice.at[:, pl.ds(aim, wide)], aims, sems.at[4]),
+    ]
+    for copy in copies:
+        copy.start()
+
+    def shared_rows(part):
         x, y, z = part[0:1], part[1:2], part[2:3]
         norm = x * x + y * y + z * z
-        high = lax.shift_right_logical(norm, 8)
-        low = norm & 255
-        one = jnp.ones_like(x)
-        if aim:
-            parts = [-2 * x, -2 * y, -2 * z, 256 * one, one, 256 * high, low, 0 * one]
-        else:
-            parts = [x, y, z, high, low, one, one, 0 * one]
-        return jnp.concatenate([p.astype(f32) for p in parts], 0).astype(bf16)
-
-    targets[...] = sites(place[4], wide, True)
-    start = pl.multiple_of(place[5], 128)
-    chosen = index[:, pl.ds(start, length)]
+        return x, y, z, lax.shift_right_logical(norm, 8), norm & 255, jnp.ones_like(x)
+
+    def stacked(parts):
+        return jnp.concatenate([p.astype(f32) for p in parts], 0)
+
+    copies[0].wait()
+    x, y, z, high, low, one = shared_rows(points[...])
+    sites = stacked([x, y, z, high, low, one, one, 0 * one])
+    copies[1].wait()
+    copies[2].wait()
     strength = jnp.zeros(chosen.shape, f32)
-    for k in range(table.shape[0]):
-        strength = jnp.where(chosen == k, table[k], strength)
-    weighted = (direction[:, pl.ds(start, length)] * strength).astype(bf16)
-    packed = jnp.concatenate([weighted, sites(start, length, False)], 0)
+    for k in range(table.shape[1]):
+        strength = jnp.where(chosen[...] == k, held_table[0:1, k : k + 1], strength)
+    copies[3].wait()
+    packed = jnp.concatenate([direction[...] * strength, sites], 0).astype(bf16)
     sources[...] = packed
     for k in range(rows):
         spread[k] = packed
-
-
-def gram_kernel(place, basis, gram, high, low):
+    copies[4].wait()
+    x, y, z, high, low, one = shared_rows(aims[...])
+    targets[...] = stacked(
+        [-2 * x, -2 * y, -2 * z, 256 * one, one, 256 * high, low, 0 * one]
+    ).astype(bf16)
+
+
+def local_kernel(place, targets, sources, basis, *rest):
+    acc, gram, direction, own_high, own_low, tiles, held, high, low, sems = rest
     count, points = basis.shape
-    chunk = 512
+    chunk = points // sems.shape[0]
+    channels, width = direction.shape
     start = pl.multiple_of(place[2], 16)
+    copies = []
+    for k in range(points // chunk):
+        cut = slice(k * chunk, (k + 1) * chunk)
+        copies.append(pltpu.make_async_copy(basis.at[:, cut], held.at[:, cut], sems.at[k]))
+        copies[-1].start()
+
+    acc[...] = jnp.zeros_like(acc)
+
+    def read(i, first):
+        return sources[first : first + 8, pl.ds(pl.multiple_of(i * STEP, STEP), STEP)]
+
+    scatter_tiles(sources.shape[1] // STEP, read, targets, tiles, acc, True)
+
     total = jnp.zeros((16, count), f32)
     for k in range(points // chunk):
         cut = slice(k * chunk, (k + 1) * chunk)
-        top, rest = split(basis[:, cut])
+        copies[k].wait()
+        top, rest = split(held[:, cut])
         high[:, cut] = top
         low[:, cut] = rest
         own = jnp.concatenate([high[pl.ds(start, 16), cut], low[pl.ds(start, 16), cut]], 0)
@@ -169,38 +193,62 @@
         total = total + (first[:16] + first[16:] + second)
     total = jnp.concatenate([total, jnp.zeros((16, 256 - count), f32)], 1)
     mixed = complex_mix(total)
-    gram[...] = jnp.concatenate([mixed[0:4], mixed[8:12]], 0)
-
-
-def project_kernel(place, keep, got, direction, high, low, gram, initial, packed):
+    gram[...] = stack_halves(jnp.concatenate([mixed[0:4], mixed[8:12]], 0))
+    here = pl.ds(pl.multiple_of(place[3] * width, 128), width)
+    direction[...] = held[count - channels : count, here]
+    own_high[...] = high[:, here]
+    own_low[...] = low[:, here]
+
+
+def stack_halves(x):
+    return jnp.concatenate([x[:, :128], x[:, 128:]], 0)
+
+
+def join_halves(x):
+    rows = x.shape[0] // 2
+    return jnp.concatenate([x[:rows], x[rows:]], 1)
+
+
+def project_kernel(keep, got, direction, high, low, gram, initial, packed):
     field = direction[...] - (keep[...] + got[...])
-    initial[...] = field
+    initial[...] = stack_halves(field)
     count = high.shape[0]
-    width = field.shape[1]
-    cut = pl.ds(pl.multiple_of(place[3] * width, 128), width)
     field_high, field_low = split(field)
     both = jnp.concatenate([field_high, field_low], 0)
-    first = lax.dot_general(both, high[:, cut], NT, preferred_element_type=f32)
-    second = lax.dot_general(field_high, low[:, cut], NT, preferred_element_type=f32)
+    first = lax.dot_general(both, high[...], NT, preferred_element_type=f32)
+    second = lax.dot_general(field_high, low[...], NT, preferred_element_type=f32)
     own = lax.dot_general(field, field, NT, preferred_element_type=f32, precision=highest)
     rest = jnp.zeros((8, 256 - count - 8), f32)
-    packed[0:8, :] = jnp.concatenate([first[:8] + first[8:] + second, own, rest], 1)
+    products = jnp.concatenate([first[:8] + first[8:] + second, own, rest], 1)
+    packed[0:8, :] = stack_halves(complex_mix(products)[0:4])
     packed[8:, :] = gram[...]
 
 
-def final_kernel(total, shared, high, low, new, coef, norm, grams):
+def final_kernel(total, shared, basis, new, coef, norm, grams, held, sems):
     parts = shared.shape[0]
-    count, points = high.shape
-    width = shared.shape[2]
+    count, points = basis.shape
+    width = 256
+    chunk = points // sems.shape[0]
+    copies = []
+    for k in range(points // chunk):
+        cut = slice(k * chunk, (k + 1) * chunk)
+        copies.append(pltpu.make_async_copy(basis.at[:, cut], held.at[:, cut], sems.at[k]))
+        copies[-1].start()
     scale = np.float32(1.0 / total)
-    sums = shared[0, 8:16, :]
+    sums = shared[0, 16:24, :]
     for q in range(1, parts):
-        sums = sums + shared[q, 8:16, :]
+        sums = sums + shared[q, 16:24, :]
+    upper = join_halves(sums)
+    lane = lax.broadcasted_iota(jnp.int32, upper.shape, 1)
+    lower = jnp.where(
+        (lane & 4) == 0, -pltpu.roll(upper, width - 4, 1), pltpu.roll(upper, 4, 1)
+    )
+    sums = jnp.concatenate([upper, lower], 0)
     lane = lax.broadcasted_iota(jnp.int32, sums.shape, 1)
     sub = lax.broadcasted_iota(jnp.int32, sums.shape, 0)
     grams[...] = jnp.zeros_like(grams)
     for q in range(count // 16):
-        part = shared[q, 16:24, :]
+        part = join_halves(shared[q, 24:40, :])
         grams[16 * q : 16 * q + 8, :] = jnp.where(sub < 4, part, 0.0)
         grams[16 * q + 8 : 16 * q + 16, :] = jnp.where(sub < 4, pltpu.roll(part, 4, 0), 0.0)
 
@@ -209,13 +257,13 @@
             jnp.dot(x, grams[...], preferred_element_type=f32, precision=highest)
         )
 
-    products = jnp.where(lane < count, complex_mix(sums), 0.0)
+    products = jnp.where(lane < count, sums, 0.0)
     once = products * scale
     mix = 2.0 * once - times_gram(once) * scale
     seen = products - 0.5 * times_gram(mix)
     cross = lax.dot_general(mix, seen, NT, preferred_element_type=f32, precision=highest)
     cross_t = lax.dot_general(seen, mix, NT, preferred_element_type=f32, precision=highest)
-    own = complex_mix(pltpu.roll(sums, width - count, 1))[:, 0:8]
+    own = pltpu.roll(sums, width - count, 1)[:, 0:8]
     result = (own - cross - cross_t) * scale
     norm[0] = result[0:4, 0:4]
     norm[1] = result[0:4, 4:8]
@@ -234,12 +282,16 @@
 
     mix_high, mix_low = split(mix[:, :count])
     both = jnp.concatenate([mix_high, mix_low], 0)
-    chunk = 4 * width
     for k in range(points // chunk):
         cut = slice(k * chunk, (k + 1) * chunk)
-        first = jnp.dot(both, high[:, cut], preferred_element_type=f32)
-        second = jnp.dot(mix_high, low[:, cut], preferred_element_type=f32)
-        field = jnp.concatenate([shared[4 * k + i, 0:8, :] for i in range(4)], 1)
+        copies[k].wait()
+        top, rest = split(held[:, cut])
+        first = jnp.dot(both, top, preferred_element_type=f32)
+        second = jnp.dot(mix_high, rest, preferred_element_type=f32)
+        each = chunk // width
+        field = jnp.concatenate(
+            [join_halves(shared[each * k + i, 0:16, :]) for i in range(each)], 1
+        )
         new[:, cut] = field - (first[:8] + first[8:] + second)
 
 
@@ -250,11 +302,11 @@
 
 VMEM = pl.BlockSpec(memory_space=pltpu.VMEM)
 SMEM = pl.BlockSpec(memory_space=pltpu.SMEM)
-ANY = pl.BlockSpec(memory_space=pl.ANY)
-
-
-def params():
-    return pltpu.CompilerParams(vmem_limit_bytes=16 << 20)
+HBM = pl.BlockSpec(memory_space=pltpu.HBM)
+
+
+def params(room=16 << 20):
+    return pltpu.CompilerParams(vmem_limit_bytes=room)
 
 
 def cost(flops, size):
@@ -281,52 +333,51 @@
 
     spread, sources, targets = pl.pallas_call(
         prepare_kernel,
-        grid=(1,),
-        in_specs=[
-            SMEM,
-            SMEM,
-            pl.BlockSpec((channels, points), lambda k: (blocks - 1, 0)),
-            pl.BlockSpec((3, points), lambda k: (0, 0)),
-            pl.BlockSpec((1, points), lambda k: (0, 0)),
-        ],
+        in_specs=[SMEM, HBM, HBM, HBM, HBM],
         out_specs=(VMEM, VMEM, VMEM),
         out_shape=(
             jax.ShapeDtypeStruct((rows, 16, length), bf16),
             jax.ShapeDtypeStruct((16, length), bf16),
             jax.ShapeDtypeStruct((8, wide), bf16),
         ),
-        compiler_params=params(),
+        scratch_shapes=[
+            pltpu.VMEM((channels, length), f32),
+            pltpu.VMEM((1, length), jnp.int32),
+            pltpu.VMEM((1, strength_table.shape[0]), f32),
+            pltpu.VMEM((3, length), jnp.int32),
+            pltpu.VMEM((3, wide), jnp.int32),
+            pltpu.SemaphoreType.DMA((5,)),
+        ],
+        compiler_params=params((64 << 20) - (64 << 10)),
         name="prepare",
-    )(place, strength_table, flat, lattice, strength_index[None, :])
+    )(place, flat, lattice, strength_index[None, :], strength_table[None, :])
     gathered = lax.all_to_all(spread, "row", 0, 0, tiled=True)
 
-    gram, high, low = pl.pallas_call(
-        gram_kernel,
-        in_specs=[SMEM, VMEM],
-        out_specs=(VMEM, VMEM, VMEM),
+    half = jax.ShapeDtypeStruct((channels, own), f32)
+    held = pltpu.VMEM((2, STEP, wide), f32)
+    begun, gram, direction, high, low = pl.pallas_call(
+        local_kernel,
+        in_specs=[SMEM, VMEM, VMEM, HBM],
+        out_specs=(VMEM,) * 5,
         out_shape=(
-            jax.ShapeDtypeStruct((8, 256), f32),
-            jax.ShapeDtypeStruct((count, points), bf16),
-            jax.ShapeDtypeStruct((count, points), bf16),
+            jax.ShapeDtypeStruct((16, wide), f32),
+            jax.ShapeDtypeStruct((16, 128), f32),
+            half,
+            jax.ShapeDtypeStruct((count, own), bf16),
+            jax.ShapeDtypeStruct((count, own), bf16),
         ),
-        compiler_params=params(),
-        cost_estimate=cost(2_000_000_000, 8_000_000),
-        name="basis_gram",
-    )(place, flat)
-
-    held = pltpu.VMEM((2, STEP, wide), f32)
-    begun = pl.pallas_call(
-        local_kernel,
-        out_shape=jax.ShapeDtypeStruct((16, wide), f32),
-        in_specs=[VMEM, VMEM, ANY],
-        out_specs=VMEM,
-        scratch_shapes=[held],
-        compiler_params=params(),
-        cost_estimate=cost(3_000_000_000, 200_000),
+        scratch_shapes=[
+            held,
+            pltpu.VMEM((count, points), f32),
+            pltpu.VMEM((count, points), bf16),
+            pltpu.VMEM((count, points), bf16),
+            pltpu.SemaphoreType.DMA((8,)),
+        ],
+        compiler_params=params(52 << 20),
+        cost_estimate=cost(5_000_000_000, 8_000_000),
         name="scatter_local",
-    )(targets, sources, gram)
-
-    half = jax.ShapeDtypeStruct((channels, own), f32)
+    )(place, targets, sources, flat)
+
     keep, send = pl.pallas_call(
         remote_kernel,
         out_shape=(half, half),
@@ -341,40 +392,33 @@
 
     initial, partial = pl.pallas_call(
         project_kernel,
-        grid_spec=pltpu.PrefetchScalarGridSpec(
-            num_scalar_prefetch=1,
-            grid=(1,),
-            in_specs=[
-                VMEM,
-                VMEM,
-                pl.BlockSpec((channels, own), lambda k, s: (blocks - 1, s[3])),
-                VMEM,
-                VMEM,
-                VMEM,
-            ],
-            out_specs=[VMEM, VMEM],
-        ),
-        out_shape=(half, jax.ShapeDtypeStruct((16, 256), f32)),
+        in_specs=[VMEM] * 6,
+        out_specs=(VMEM, VMEM),
+        out_shape=(jax.ShapeDtypeStruct((16, 128), f32), jax.ShapeDtypeStruct((24, 128), f32)),
         compiler_params=params(),
         name="project",
-    )(place, keep, got, flat, high, low, gram)
+    )(keep, got, direction, high, low, gram)
 
     row_sums = jnp.sum(gather_all(partial, "row"), axis=0)
     shared = gather_all(jnp.concatenate([initial, row_sums], 0), ("col", "grp"))
 
     new_block, coef, norm = pl.pallas_call(
         functools.partial(final_kernel, total),
-        in_specs=[VMEM, VMEM, VMEM],
+        in_specs=[VMEM, HBM],
         out_specs=(VMEM, VMEM, VMEM),
         out_shape=(
             jax.ShapeDtypeStruct((channels, points), f32),
             jax.ShapeDtypeStruct((2, inc, inc, blocks), f32),
             jax.ShapeDtypeStruct((2, inc, inc), f32),
         ),
-        scratch_shapes=[pltpu.VMEM((256, 256), f32)],
-        compiler_params=params(),
+        scratch_shapes=[
+            pltpu.VMEM((256, 256), f32),
+            pltpu.VMEM((count, points), f32),
+            pltpu.SemaphoreType.DMA((4,)),
+        ],
+        compiler_params=params(52 << 20),
         name="finish",
-    )(shared, high, low)
+    )(shared, flat)
     return new_block, coef.transpose(3, 0, 1, 2), norm
 
 

time: 83.7 us -> 78.6 us (0.939)
  local copies, waits for them, and re-layouts: 9.49 us -> 2.8 us
  Pallas kernels: 34.7 us -> 37.1 us
  blocking collectives: 26.9 us -> 25.8 us
    unnamed x18 -> x10, local copies, waits for them, and re-layouts: 9.36 us -> 2.15 us
    pallas_call x5 -> x4, Pallas kernels: 10.6 us -> 13 us  [the longest x1 7.17 us: local(): pl.pallas_call(local_kernel, in_specs=[SMEM, VMEM, VMEM, HBM], out_specs=...]
    all_to_all x2, blocking collectives: 26.9 us -> 25.8 us  [gather_all(): lax.all_to_all(jnp.broadcast_to(x[None], (length, *x.shape)), axis, 0, 0,...]
  transfers between devices with their start and end apart: 2 -> 2, of which waited for: 2 -> 2; matrix products, arithmetic and copies ran while one was open for 0% -> 0% of each run, Pallas kernels for 7% -> 9%
where the time goes in v3:
time: 78.6 us; the launch traced here: 78.2 us
  Pallas kernels  37.1 us (47%)
  blocking collectives  25.8 us (33%)
  starting transfers between devices  10.1 us (13%)
  local copies, waits for them, and re-layouts  2.8 us (4%)
  waiting for transfers between devices  1.7 us (2%)
    all_to_all x2, blocking collectives, gather_all(): lax.all_to_all(jnp.broadcast_to(x[None], (length, *x.shape)), axis, 0, 0,...  25.8 us
    pallas_call x1, Pallas kernels, local(): pl.pallas_call(remote_kernel, out_shape=(half, half), in_specs=[SMEM, VME...  24.1 us
    all_to_all x1, starting transfers between devices, local(): gathered = lax.all_to_all(spread, 'row', 0, 0, tiled=True)  8.34 us
    pallas_call x1, Pallas kernels, local(): pl.pallas_call(local_kernel, in_specs=[SMEM, VMEM, VMEM, HBM], out_specs=...  7.17 us
    pallas_call x1, Pallas kernels, local(): pl.pallas_call(functools.partial(final_kernel, total), in_specs=[VMEM, HB...  3.06 us
    pallas_call x1, Pallas kernels, local(): pl.pallas_call(prepare_kernel, in_specs=[SMEM, HBM, HBM, HBM, HBM], out_s...  2.47 us
    unnamed x10, local copies, waits for them, and re-layouts  2.15 us
    ppermute x1, starting transfers between devices, local(): lax.ppermute(send, 'grp', [(i, groups - 1 - i) for i in range(groups)])  1.72 us
  transfers between devices with their start and end apart: 2, of which 2 were waited for; matrix products, arithmetic and copies ran while one was open for 0% of the time, Pallas kernels for 9%

profile of v3, /device:TPU:1, one launch (start us, length us, event | category | flops | bytes accessed | tf_op | source)
XLA Modules:
  0.0 78.2 jit_solution(11432817571022393511)
XLA Ops:
  0.6 0.6 stack.27.place
  1.2 2.5 %prepare.1 = (bf16[8,16,2048]{2,1,0:T(8,128)(2,1)}, bf16[16,2048]{1,0:T(8,128)(2,1)}, bf16[8,512]{1,0:T(8,128)(2,1)}) custom-call(s32[6]{0:T(128)} %stack.27.place, f32[240,4096]{1,0:T(8,128)} %bitcast.10, s32[3,4096]{1,0:T(4,128)} %lattice.1, s32[1,4096]{1,0:T(1,128)} %bitcast.13, f32[1,16]{1,0:T(1,128)} %bitcast.14), custom_call_target="tpu_custom_call" | custom-call | tf_op jit(solution)/shard_map/prepare/pallas_call | solution.py:334
  3.7 8.3 %all-to-all-start = ((bf16[8,16,2048]{2,1,0:T(8,128)(2,1)}), bf16[8,16,2048]{2,1,0:T(8,128)(2,1)S(1)}, u32[]{:S(2)}, u32[]{:S(2)}) async-start(bf16[8,16,2048]{2,1,0:T(8,128)(2,1)} %get-tuple-element.19), calls=%async_computation | async-start | bytes 1048576 | tf_op jit(solution)/shard_map/all_to_all | solution.py:354
  12.1 0.0 copy-start
  12.1 0.6 copy-done
  12.7 0.0 copy-start.2
  12.7 0.8 %copy-done.2 = bf16[16,2048]{1,0:T(8,128)(2,1)S(1)} copy-done((bf16[16,2048]{1,0:T(8,128)(2,1)S(1)}, bf16[16,2048]{1,0:T(8,128)(2,1)}, u32[]{:S(2)}) %copy-start.2) | copy-done | bytes 65560
  13.5 0.0 copy-start.3
  13.5 0.7 copy-done.3
  14.2 0.0 copy-start.1
  14.2 0.0 copy-start.4
  14.2 7.2 %scatter_local.1 = (f32[16,512]{1,0:T(8,128)S(1)}, f32[16,128]{1,0:T(8,128)S(1)}, f32[8,256]{1,0:T(8,128)S(1)}, bf16[240,256]{1,0:T(8,128)(2,1)S(1)}, bf16[240,256]{1,0:T(8,128)(2,1)S(1)}) custom-call(s32[6]{0:T(128)S(1)} %copy-done, bf16[8,512]{1,0:T(8,128)(2,1)S(1)} %copy-done.3, bf16[16,2048]{1,0:T(8,128)(2,1)S(1)} %copy-done.2, f32[240,4096]{1,0:T(8,128)} %bitcast.11), custom_call_target="tpu_custom_call" | custom-call | flops 5000000000 | bytes 8000000 | tf_op jit(solution)/shard_map/scatter_local/pallas_call | solution.py:358
  21.4 0.9 %all-to-all-done.sources = bf16[8,16,2048]{2,1,0:T(8,128)(2,1)S(1)} async-done(((bf16[8,16,2048]{2,1,0:T(8,128)(2,1)}), bf16[8,16,2048]{2,1,0:T(8,128)(2,1)S(1)}, u32[]{:S(2)}, u32[]{:S(2)}) %all-to-all-start) | async-done | bytes 524320 | tf_op jit(solution)/shard_map/all_to_all | solution.py:354
  22.3 0.0 copy-done.1
  22.3 0.0 copy-done.4
  22.3 24.1 %scatter_remote.1 = (f32[8,256]{1,0:T(8,128)S(1)}, f32[8,256]{1,0:T(8,128)S(1)}) custom-call(s32[6]{0:T(128)S(1)} %copy-done.1, bf16[8,512]{1,0:T(8,128)(2,1)S(1)} %copy-done.4, bf16[8,16,2048]{2,1,0:T(8,128)(2,1)S(1)} %all-to-all-done.sources, f32[16,512]{1,0:T(8,128)S(1)} %get-tuple-element.21.begun), custom_call_target="tpu_custom_call" | custom-call | flops 20000000000 | bytes 800000 | tf_op jit(solution)/shard_map/scatter_remote/pallas_call | solution.py:381
  46.4 1.7 %collective-permute-start = (f32[8,256]{1,0:T(8,128)S(1)}, f32[8,256]{1,0:T(8,128)S(1)}, u32[]{:S(2)}, u32[]{:S(2)}) collective-permute-start(f32[8,256]{1,0:T(8,128)S(1)} %get-tuple-element.23), channel_id=1, source_target_pairs={{0,1},{1,0},{2,3},{3,2},{4,5},{5,4},{6,7},{7,6},{8,9},{9,8},{10,11... | collective-permute-start | bytes 24584 | tf_op jit(solution)/shard_map/ppermute | solution.py:391
  48.1 0.8 %collective-permute-done.got = f32[8,256]{1,0:T(8,128)S(1)} collective-permute-done((f32[8,256]{1,0:T(8,128)S(1)}, f32[8,256]{1,0:T(8,128)S(1)}, u32[]{:S(2)}, u32[]{:S(2)}) %collective-permute-start) | collective-permute-done | bytes 8224 | tf_op jit(solution)/shard_map/ppermute | solution.py:391
  48.9 0.3 project.1
  49.3 12.0 %all_to_all.15 = f32[8,24,128]{2,1,0:T(8,128)S(1)} all-to-all(f32[8,24,128]{2,1,0:T(8,128)S(1)} %broadcast_in_dim.20), channel_id=1, replica_groups=mesh['row'=8,'col'=8,'grp'=2] {'row'}, dimensions={0} | all-to-all | bytes 196608 | tf_op jit(solution)/shard_map/all_to_all | solution.py:300
  61.4 13.8 %all_to_all.16.shared = f32[16,40,128]{2,1,0:T(8,128)S(1)} all-to-all(f32[16,40,128]{2,1,0:T(8,128)S(1)} %broadcast_in_dim.21), channel_id=1, replica_groups=mesh['row'=8,'col'=8,'grp'=2] {'col','grp'}, dimensions={0} | all-to-all | bytes 655360 | tf_op jit(solution)/shard_map/all_to_all | solution.py:300
  75.2 3.1 %finish.1 = (f32[8,4096]{1,0:T(8,128)}, f32[2,4,4,30]{3,2,1,0:T(4,128)}, f32[2,4,4]{2,1,0:T(4,128)}) custom-call(f32[16,40,128]{2,1,0:T(8,128)S(1)} %all_to_all.16.shared, f32[240,4096]{1,0:T(8,128)} %bitcast.12), custom_call_target="tpu_custom_call" | custom-call | tf_op jit(solution)/shard_map/finish/pallas_call | solution.py:405
  (4 shorter events, 0.1 us)
Async XLA Ops:
  3.7 18.5 %all-to-all-start = ((bf16[8,16,2048]{2,1,0:T(8,128)(2,1)}), bf16[8,16,2048]{2,1,0:T(8,128)(2,1)S(1)}, u32[]{:S(2)}, u32[]{:S(2)}) async-start(bf16[8,16,2048]{2,1,0:T(8,128)(2,1)} %get-tuple-element.19), calls=%async_computation | async-start | bytes 1048576 | tf_op jit(solution)/shard_map/all_to_all | solution.py:354
  12.1 0.6 copy-start
  12.7 0.8 %copy-start.2 = (bf16[16,2048]{1,0:T(8,128)(2,1)S(1)}, bf16[16,2048]{1,0:T(8,128)(2,1)}, u32[]{:S(2)}) copy-start(bf16[16,2048]{1,0:T(8,128)(2,1)} %get-tuple-element.20.sources) | copy-start | bytes 196612
  13.5 0.7 copy-start.3
  14.2 8.1 %copy-start.1 = (s32[6]{0:T(128)S(1)}, s32[6]{0:T(128)}, u32[]{:S(2)}) copy-start(s32[6]{0:T(128)} %stack.27.place) | copy-start | bytes 76
  14.2 8.1 %copy-start.4 = (bf16[8,512]{1,0:T(8,128)(2,1)S(1)}, bf16[8,512]{1,0:T(8,128)(2,1)}, u32[]{:S(2)}) copy-start(bf16[8,512]{1,0:T(8,128)(2,1)} %get-tuple-element.18.targets) | copy-start | bytes 24580
  46.4 2.5 %collective-permute-start = (f32[8,256]{1,0:T(8,128)S(1)}, f32[8,256]{1,0:T(8,128)S(1)}, u32[]{:S(2)}, u32[]{:S(2)}) collective-permute-start(f32[8,256]{1,0:T(8,128)S(1)} %get-tuple-element.23), channel_id=1, source_target_pairs={{0,1},{1,0},{2,3},{3,2},{4,5},{5,4},{6,7},{7,6},{8,9},{9,8},{10,11... | collective-permute-start | bytes 24584 | tf_op jit(solution)/shard_map/ppermute | solution.py:391

commit v4 on v3

--- a/solution.py
+++ b/solution.py
@@ -69,10 +69,11 @@
     lax.fori_loop(0, tiles // 2, body, 0)
 
 
-def remote_kernel(place, targets, sources, begun, keep, send, held, acc):
+def remote_kernel(ready, sources, begun, keep, send, held, acc):
     rows, _, length = sources.shape
     per_row = length // STEP
-    row = place[0]
+    row = lax.axis_index("row")
+    targets = ready.at[8:16, length:]
     acc[...] = begun[...]
 
     def read(i, first):
@@ -88,7 +89,7 @@
     both = jnp.concatenate([upper, lower], 0)
     half = both.shape[1] // 2
     first, second = both[:, :half], both[:, half:]
-    mine = place[1] == 0
+    mine = lax.axis_index("grp") == 0
     keep[...] = jnp.where(mine, first, second)
     send[...] = jnp.where(mine, second, first)
 
@@ -113,13 +114,13 @@
     return products + jnp.where(same, swapped, -swapped)
 
 
-def prepare_kernel(place, basis, lattice, index, table, spread, sources, targets, *scratch):
+def prepare_kernel(basis, lattice, index, table, spread, ready, *scratch):
     direction, chosen, held_table, points, aims, sems = scratch
     rows, _, length = spread.shape
-    wide = targets.shape[1]
+    wide = aims.shape[1]
     channels = direction.shape[0]
-    aim = pl.multiple_of(place[4], 128)
-    start = pl.multiple_of(place[5], 128)
+    aim = pl.multiple_of(lax.axis_index("col") * wide, 128)
+    start = pl.multiple_of(lax.axis_index("grp") * length, 128)
     last = basis.shape[0] - channels
     copies = [
         pltpu.make_async_copy(lattice.at[:, pl.ds(start, length)], points, sems.at[0]),
@@ -151,51 +152,66 @@
         strength = jnp.where(chosen[...] == k, held_table[0:1, k : k + 1], strength)
     copies[3].wait()
     packed = jnp.concatenate([direction[...] * strength, sites], 0).astype(bf16)
-    sources[...] = packed
+    ready[:, :length] = packed
     for k in range(rows):
         spread[k] = packed
     copies[4].wait()
     x, y, z, high, low, one = shared_rows(aims[...])
-    targets[...] = stacked(
-        [-2 * x, -2 * y, -2 * z, 256 * one, one, 256 * high, low, 0 * one]
-    ).astype(bf16)
-
-
-def local_kernel(place, targets, sources, basis, *rest):
-    acc, gram, direction, own_high, own_low, tiles, held, high, low, sems = rest
+    sites = stacked([-2 * x, -2 * y, -2 * z, 256 * one, one, 256 * high, low, 0 * one])
+    ready[:, length:] = jnp.concatenate([jnp.zeros_like(sites), sites], 0).astype(bf16)
+
+
+def local_kernel(ready, basis, *rest):
+    acc, gram, direction, own_high, own_low, kept, tiles, held, high, low, sems = rest
+    half = kept.shape[1]
+    length = ready.shape[1] - tiles.shape[2]
+    targets = ready.at[8:16, length:]
+    part = lax.axis_index(("col", "grp"))
     count, points = basis.shape
-    chunk = points // sems.shape[0]
+    pieces = sems.shape[0] - 1
+    chunk = points // pieces
     channels, width = direction.shape
-    start = pl.multiple_of(place[2], 16)
+    here = pl.ds(pl.multiple_of(part * width, 128), width)
+    own = pltpu.make_async_copy(
+        basis.at[count - channels : count, here], direction, sems.at[pieces]
+    )
+    own.start()
+    start = pl.multiple_of(jnp.minimum(part * 16, count - 16), 16)
+
+    def place_of(k):
+        first = k * chunk
+        if first < half:
+            return kept.at[:, first : first + chunk]
+        return held.at[:, first - half : first - half + chunk]
+
     copies = []
     for k in range(points // chunk):
         cut = slice(k * chunk, (k + 1) * chunk)
-        copies.append(pltpu.make_async_copy(basis.at[:, cut], held.at[:, cut], sems.at[k]))
+        copies.append(pltpu.make_async_copy(basis.at[:, cut], place_of(k), sems.at[k]))
         copies[-1].start()
 
     acc[...] = jnp.zeros_like(acc)
 
     def read(i, first):
-        return sources[first : first + 8, pl.ds(pl.multiple_of(i * STEP, STEP), STEP)]
-
-    scatter_tiles(sources.shape[1] // STEP, read, targets, tiles, acc, True)
+        return ready[first : first + 8, pl.ds(pl.multiple_of(i * STEP, STEP), STEP)]
+
+    scatter_tiles(length // STEP, read, targets, tiles, acc, True)
 
     total = jnp.zeros((16, count), f32)
     for k in range(points // chunk):
         cut = slice(k * chunk, (k + 1) * chunk)
         copies[k].wait()
-        top, rest = split(held[:, cut])
+        top, rest = split(place_of(k)[...])
         high[:, cut] = top
         low[:, cut] = rest
-        own = jnp.concatenate([high[pl.ds(start, 16), cut], low[pl.ds(start, 16), cut]], 0)
-        first = lax.dot_general(own, top, NT, preferred_element_type=f32)
-        second = lax.dot_general(own[:16], rest, NT, preferred_element_type=f32)
+        mine = jnp.concatenate([high[pl.ds(start, 16), cut], low[pl.ds(start, 16), cut]], 0)
+        first = lax.dot_general(mine, top, NT, preferred_element_type=f32)
+        second = lax.dot_general(mine[:16], rest, NT, preferred_element_type=f32)
         total = total + (first[:16] + first[16:] + second)
     total = jnp.concatenate([total, jnp.zeros((16, 256 - count), f32)], 1)
     mixed = complex_mix(total)
     gram[...] = stack_halves(jnp.concatenate([mixed[0:4], mixed[8:12]], 0))
-    here = pl.ds(pl.multiple_of(place[3] * width, 128), width)
-    direction[...] = held[count - channels : count, here]
+    own.wait()
     own_high[...] = high[:, here]
     own_low[...] = low[:, here]
 
@@ -224,15 +240,17 @@
     packed[8:, :] = gram[...]
 
 
-def final_kernel(total, shared, basis, new, coef, norm, grams, held, sems):
+def final_kernel(total, shared, kept, basis, new, coef, norm, grams, held, sems):
     parts = shared.shape[0]
     count, points = basis.shape
     width = 256
-    chunk = points // sems.shape[0]
+    chunk = 512
+    half = points - held.shape[1]
     copies = []
-    for k in range(points // chunk):
+    for k in range(sems.shape[0]):
         cut = slice(k * chunk, (k + 1) * chunk)
-        copies.append(pltpu.make_async_copy(basis.at[:, cut], held.at[:, cut], sems.at[k]))
+        there = slice(half + k * chunk, half + (k + 1) * chunk)
+        copies.append(pltpu.make_async_copy(basis.at[:, there], held.at[:, cut], sems.at[k]))
         copies[-1].start()
     scale = np.float32(1.0 / total)
     sums = shared[0, 16:24, :]
@@ -284,8 +302,13 @@
     both = jnp.concatenate([mix_high, mix_low], 0)
     for k in range(points // chunk):
         cut = slice(k * chunk, (k + 1) * chunk)
-        copies[k].wait()
-        top, rest = split(held[:, cut])
+        if k * chunk < half:
+            columns = kept[:, cut]
+        else:
+            later = k - half // chunk
+            copies[later].wait()
+            columns = held[:, later * chunk : (later + 1) * chunk]
+        top, rest = split(columns)
         first = jnp.dot(both, top, preferred_element_type=f32)
         second = jnp.dot(mix_high, rest, preferred_element_type=f32)
         each = chunk // width
@@ -320,25 +343,18 @@
     rows = lax.axis_size("row")
     groups = lax.axis_size("grp")
     parts = lax.axis_size(("col", "grp"))
-    row, col, grp = lax.axis_index("row"), lax.axis_index("col"), lax.axis_index("grp")
-    part = lax.axis_index(("col", "grp"))
     total = points * rows
     own = points // parts
     wide = own * groups
     length = points // groups
     flat = krylov_basis.reshape(count, points)
-    place = jnp.stack(
-        [row, grp, jnp.minimum(part * 16, count - 16), part, col * wide, grp * length]
-    ).astype(jnp.int32)
-
-    spread, sources, targets = pl.pallas_call(
+    spread, ready = pl.pallas_call(
         prepare_kernel,
-        in_specs=[SMEM, HBM, HBM, HBM, HBM],
-        out_specs=(VMEM, VMEM, VMEM),
+        in_specs=[HBM, HBM, HBM, HBM],
+        out_specs=(VMEM, VMEM),
         out_shape=(
             jax.ShapeDtypeStruct((rows, 16, length), bf16),
-            jax.ShapeDtypeStruct((16, length), bf16),
-            jax.ShapeDtypeStruct((8, wide), bf16),
+            jax.ShapeDtypeStruct((16, length + wide), bf16),
         ),
         scratch_shapes=[
             pltpu.VMEM((channels, length), f32),
@@ -350,44 +366,45 @@
         ],
         compiler_params=params((64 << 20) - (64 << 10)),
         name="prepare",
-    )(place, flat, lattice, strength_index[None, :], strength_table[None, :])
+    )(flat, lattice, strength_index[None, :], strength_table[None, :])
     gathered = lax.all_to_all(spread, "row", 0, 0, tiled=True)
 
     half = jax.ShapeDtypeStruct((channels, own), f32)
     held = pltpu.VMEM((2, STEP, wide), f32)
-    begun, gram, direction, high, low = pl.pallas_call(
+    begun, gram, direction, high, low, kept = pl.pallas_call(
         local_kernel,
-        in_specs=[SMEM, VMEM, VMEM, HBM],
-        out_specs=(VMEM,) * 5,
+        in_specs=[VMEM, HBM],
+        out_specs=(VMEM,) * 6,
         out_shape=(
             jax.ShapeDtypeStruct((16, wide), f32),
             jax.ShapeDtypeStruct((16, 128), f32),
             half,
             jax.ShapeDtypeStruct((count, own), bf16),
             jax.ShapeDtypeStruct((count, own), bf16),
+            jax.ShapeDtypeStruct((count, points // 2), f32),
         ),
         scratch_shapes=[
             held,
-            pltpu.VMEM((count, points), f32),
+            pltpu.VMEM((count, points // 2), f32),
             pltpu.VMEM((count, points), bf16),
             pltpu.VMEM((count, points), bf16),
-            pltpu.SemaphoreType.DMA((8,)),
+            pltpu.SemaphoreType.DMA((9,)),
         ],
-        compiler_params=params(52 << 20),
+        compiler_params=params(50 << 20),
         cost_estimate=cost(5_000_000_000, 8_000_000),
         name="scatter_local",
-    )(place, targets, sources, flat)
+    )(ready, flat)
 
     keep, send = pl.pallas_call(
         remote_kernel,
         out_shape=(half, half),
-        in_specs=[SMEM, VMEM, VMEM, VMEM],
+        in_specs=[VMEM, VMEM, VMEM],
         out_specs=(VMEM, VMEM),
         scratch_shapes=[held, pltpu.VMEM((16, wide), f32)],
         compiler_params=params(),
         cost_estimate=cost(20_000_000_000, 800_000),
         name="scatter_remote",
-    )(place, targets, gathered, begun)
+    )(ready, gathered, begun)
     got = lax.ppermute(send, "grp", [(i, groups - 1 - i) for i in range(groups)])
 
     initial, partial = pl.pallas_call(
@@ -404,7 +421,7 @@
 
     new_block, coef, norm = pl.pallas_call(
         functools.partial(final_kernel, total),
-        in_specs=[VMEM, HBM],
+        in_specs=[VMEM, VMEM, HBM],
         out_specs=(VMEM, VMEM, VMEM),
         out_shape=(
             jax.ShapeDtypeStruct((channels, points), f32),
@@ -413,12 +430,12 @@
         ),
         scratch_shapes=[
             pltpu.VMEM((256, 256), f32),
-            pltpu.VMEM((count, points), f32),
-            pltpu.SemaphoreType.DMA((4,)),
+            pltpu.VMEM((count, points // 2), f32),
+            pltpu.SemaphoreType.DMA((points // 2 // 512,)),
         ],
-        compiler_params=params(52 << 20),
+        compiler_params=params(50 << 20),
         name="finish",
-    )(shared, flat)
+    )(shared, kept, flat)
     return new_block, coef.transpose(3, 0, 1, 2), norm
 
 

time: 78.6 us -> 75 us (0.954)
  local copies, waits for them, and re-layouts: 2.8 us -> 0.93 us
  blocking collectives: 25.8 us -> 24 us
  waiting for transfers between devices: 1.7 us -> 3.49 us
  Pallas kernels: 37.1 us -> 35.4 us
    all_to_all x2, blocking collectives: 25.8 us -> 24 us  [gather_all(): lax.all_to_all(jnp.broadcast_to(x[None], (length, *x.shape)), axis, 0, 0,...]
    all_to_all x1, waiting for transfers between devices: 0.87 us -> 2.66 us  [local(): gathered = lax.all_to_all(spread, 'row', 0, 0, tiled=True)]
    pallas_call x4, Pallas kernels: 36.8 us -> 35 us  [the longest x1 23.6 us: local(): pl.pallas_call(remote_kernel, out_shape=(half, half), in_specs=[VMEM, VME...]
    unnamed x10 -> x4, local copies, waits for them, and re-layouts: 2.15 us -> 0.89 us
where the time goes in v4:
time: 75 us; the launch traced here: 74.6 us
  Pallas kernels  35.4 us (47%)
  blocking collectives  24 us (32%)
  starting transfers between devices  10.1 us (13%)
  waiting for transfers between devices  3.49 us (5%)
  local copies, waits for them, and re-layouts  0.93 us (1%)
    all_to_all x2, blocking collectives, gather_all(): lax.all_to_all(jnp.broadcast_to(x[None], (length, *x.shape)), axis, 0, 0,...  24 us
    pallas_call x1, Pallas kernels, local(): pl.pallas_call(remote_kernel, out_shape=(half, half), in_specs=[VMEM, VME...  23.6 us
    all_to_all x1, starting transfers between devices, local(): gathered = lax.all_to_all(spread, 'row', 0, 0, tiled=True)  8.34 us
    pallas_call x1, Pallas kernels, local(): pl.pallas_call(local_kernel, in_specs=[VMEM, HBM], out_specs=(VMEM,) * 6,...  6.64 us
    pallas_call x1, Pallas kernels, local(): pl.pallas_call(functools.partial(final_kernel, total), in_specs=[VMEM, VM...  3.03 us
    all_to_all x1, waiting for transfers between devices, local(): gathered = lax.all_to_all(spread, 'row', 0, 0, tiled=True)  2.66 us
    pallas_call x1, Pallas kernels, local(): pl.pallas_call(prepare_kernel, in_specs=[HBM, HBM, HBM, HBM], out_specs=(...  1.8 us
    ppermute x1, starting transfers between devices, local(): lax.ppermute(send, 'grp', [(i, groups - 1 - i) for i in range(groups)])  1.75 us
  transfers between devices with their start and end apart: 2, of which 2 were waited for; matrix products, arithmetic and copies ran while one was open for 0% of the time, Pallas kernels for 9%

profile of v4, /device:TPU:1, one launch (start us, length us, event | category | flops | bytes accessed | tf_op | source)
XLA Modules:
  0.0 74.6 jit_solution(6086835078846466369)
XLA Ops:
  0.6 1.8 %prepare.1 = (bf16[8,16,2048]{2,1,0:T(8,128)(2,1)}, bf16[16,2560]{1,0:T(8,128)(2,1)}) custom-call(f32[240,4096]{1,0:T(8,128)} %bitcast.4, s32[3,4096]{1,0:T(4,128)} %lattice.1, s32[1,4096]{1,0:T(1,128)} %bitcast.7, f32[1,16]{1,0:T(1,128)} %bitcast.8), custom_call_target="tpu_custom_call" | custom-call | tf_op jit(solution)/shard_map/prepare/pallas_call | solution.py:351
  2.4 8.3 %all-to-all-start = ((bf16[8,16,2048]{2,1,0:T(8,128)(2,1)}), bf16[8,16,2048]{2,1,0:T(8,128)(2,1)S(1)}, u32[]{:S(2)}, u32[]{:S(2)}) async-start(bf16[8,16,2048]{2,1,0:T(8,128)(2,1)} %get-tuple-element.19), calls=%async_computation | async-start | bytes 1048576 | tf_op jit(solution)/shard_map/all_to_all | solution.py:370
  10.8 0.0 copy-start
  10.8 0.9 %copy-done = bf16[16,2560]{1,0:T(8,128)(2,1)S(1)} copy-done((bf16[16,2560]{1,0:T(8,128)(2,1)S(1)}, bf16[16,2560]{1,0:T(8,128)(2,1)}, u32[]{:S(2)}) %copy-start) | copy-done | bytes 81944
  11.7 0.0 copy-start.1
  11.7 6.6 %scatter_local.1 = (f32[16,512]{1,0:T(8,128)S(1)}, f32[16,128]{1,0:T(8,128)S(1)}, f32[8,256]{1,0:T(8,128)S(1)}, bf16[240,256]{1,0:T(8,128)(2,1)S(1)}, bf16[240,2...) custom-call(bf16[16,2560]{1,0:T(8,128)(2,1)S(1)} %copy-done, f32[240,4096]{1,0:T(8,128)} %bitcast.5), custom_call_target="tpu_custom_call" | custom-call | flops 5000000000 | bytes 8000000 | tf_op jit(solution)/shard_map/scatter_local/pallas_call | solution.py:374
  18.3 2.7 %all-to-all-done.sources = bf16[8,16,2048]{2,1,0:T(8,128)(2,1)S(1)} async-done(((bf16[8,16,2048]{2,1,0:T(8,128)(2,1)}), bf16[8,16,2048]{2,1,0:T(8,128)(2,1)S(1)}, u32[]{:S(2)}, u32[]{:S(2)}) %all-to-all-start) | async-done | bytes 524320 | tf_op jit(solution)/shard_map/all_to_all | solution.py:370
  21.0 0.0 copy-done.1
  21.0 23.6 %scatter_remote.1 = (f32[8,256]{1,0:T(8,128)S(1)}, f32[8,256]{1,0:T(8,128)S(1)}) custom-call(bf16[16,2560]{1,0:T(8,128)(2,1)S(1)} %copy-done.1, bf16[8,16,2048]{2,1,0:T(8,128)(2,1)S(1)} %all-to-all-done.sources, f32[16,512]{1,0:T(8,128)S(1)} %get-tuple-element.20.begun), custom_call_target="tpu_custom_call" | custom-call | flops 20000000000 | bytes 800000 | tf_op jit(solution)/shard_map/scatter_remote/pallas_call | solution.py:398
  44.6 1.7 %collective-permute-start = (f32[8,256]{1,0:T(8,128)S(1)}, f32[8,256]{1,0:T(8,128)S(1)}, u32[]{:S(2)}, u32[]{:S(2)}) collective-permute-start(f32[8,256]{1,0:T(8,128)S(1)} %get-tuple-element.22), channel_id=1, source_target_pairs={{0,1},{1,0},{2,3},{3,2},{4,5},{5,4},{6,7},{7,6},{8,9},{9,8},{10,11... | collective-permute-start | bytes 24584 | tf_op jit(solution)/shard_map/ppermute | solution.py:408
  46.3 0.8 %collective-permute-done.got = f32[8,256]{1,0:T(8,128)S(1)} collective-permute-done((f32[8,256]{1,0:T(8,128)S(1)}, f32[8,256]{1,0:T(8,128)S(1)}, u32[]{:S(2)}, u32[]{:S(2)}) %collective-permute-start) | collective-permute-done | bytes 8224 | tf_op jit(solution)/shard_map/ppermute | solution.py:408
  47.1 0.3 project.1
  47.5 10.2 %all_to_all.15 = f32[8,24,128]{2,1,0:T(8,128)S(1)} all-to-all(f32[8,24,128]{2,1,0:T(8,128)S(1)} %broadcast_in_dim.20), channel_id=1, replica_groups=mesh['row'=8,'col'=8,'grp'=2] {'row'}, dimensions={0} | all-to-all | bytes 196608 | tf_op jit(solution)/shard_map/all_to_all | solution.py:323
  57.7 13.8 %all_to_all.16.shared = f32[16,40,128]{2,1,0:T(8,128)S(1)} all-to-all(f32[16,40,128]{2,1,0:T(8,128)S(1)} %broadcast_in_dim.21), channel_id=1, replica_groups=mesh['row'=8,'col'=8,'grp'=2] {'col','grp'}, dimensions={0} | all-to-all | bytes 655360 | tf_op jit(solution)/shard_map/all_to_all | solution.py:323
  71.6 3.0 %finish.1 = (f32[8,4096]{1,0:T(8,128)}, f32[2,4,4,30]{3,2,1,0:T(4,128)}, f32[2,4,4]{2,1,0:T(4,128)}) custom-call(f32[16,40,128]{2,1,0:T(8,128)S(1)} %all_to_all.16.shared, f32[240,2048]{1,0:T(8,128)S(1)} %get-tuple-element.29.kept, f32[240,4096]{1,0:T(8,128)} %bitcast.6), custom_call_target="tpu_custom_call" | custom-call | tf_op jit(solution)/shard_map/finish/pallas_call | solution.py:422
  (4 shorter events, 0.1 us)
Async XLA Ops:
  2.4 18.5 %all-to-all-start = ((bf16[8,16,2048]{2,1,0:T(8,128)(2,1)}), bf16[8,16,2048]{2,1,0:T(8,128)(2,1)S(1)}, u32[]{:S(2)}, u32[]{:S(2)}) async-start(bf16[8,16,2048]{2,1,0:T(8,128)(2,1)} %get-tuple-element.19), calls=%async_computation | async-start | bytes 1048576 | tf_op jit(solution)/shard_map/all_to_all | solution.py:370
  10.8 0.9 %copy-start = (bf16[16,2560]{1,0:T(8,128)(2,1)S(1)}, bf16[16,2560]{1,0:T(8,128)(2,1)}, u32[]{:S(2)}) copy-start(bf16[16,2560]{1,0:T(8,128)(2,1)} %get-tuple-element.18.ready) | copy-start | bytes 245764
  11.7 9.3 %copy-start.1 = (bf16[16,2560]{1,0:T(8,128)(2,1)S(1)}, bf16[16,2560]{1,0:T(8,128)(2,1)}, u32[]{:S(2)}) copy-start(bf16[16,2560]{1,0:T(8,128)(2,1)} %get-tuple-element.18.ready) | copy-start | bytes 245764
  44.6 2.6 %collective-permute-start = (f32[8,256]{1,0:T(8,128)S(1)}, f32[8,256]{1,0:T(8,128)S(1)}, u32[]{:S(2)}, u32[]{:S(2)}) collective-permute-start(f32[8,256]{1,0:T(8,128)S(1)} %get-tuple-element.22), channel_id=1, source_target_pairs={{0,1},{1,0},{2,3},{3,2},{4,5},{5,4},{6,7},{7,6},{8,9},{9,8},{10,11... | collective-permute-start | bytes 24584 | tf_op jit(solution)/shard_map/ppermute | solution.py:408

commit v5 on v4

--- a/solution.py
+++ b/solution.py
@@ -41,15 +41,14 @@
     return real_part.astype(bf16), imag_part.astype(bf16)
 
 
-def scatter_tiles(tiles, read, targets, held, acc, masked):
+def scatter_tiles(tiles, sites_of, weights_of, targets, held, acc, masked, unroll):
     width = targets.shape[1]
 
     def fill(i, slot):
-        sites = read(i, 8)
-        held[slot] = lax.dot_general(sites, targets[...], TN, preferred_element_type=f32)
+        held[slot] = lax.dot_general(sites_of(i), targets[...], TN, preferred_element_type=f32)
 
     def work(i, slot):
-        weights = read(i, 0)
+        weights = weights_of(i)
         for k in range(width // SUB):
             cut = slice(k * SUB, (k + 1) * SUB)
             real_part, imag_part = green_pair(held[slot, :, cut], masked)
@@ -59,29 +58,52 @@
     fill(0, 0)
 
     def body(h, carry):
-        i = 2 * h
-        fill(i + 1, 1)
-        work(i, 0)
-        fill(jnp.minimum(i + 2, tiles - 1), 0)
-        work(i + 1, 1)
+        for u in range(unroll):
+            i = unroll * h + u
+            fill(jnp.minimum(i + 1, tiles - 1), 1 - u % 2)
+            work(i, u % 2)
         return carry
 
-    lax.fori_loop(0, tiles // 2, body, 0)
-
-
-def remote_kernel(ready, sources, begun, keep, send, held, acc):
-    rows, _, length = sources.shape
+    lax.fori_loop(0, tiles // unroll, body, 0)
+
+
+def remote_kernel(ready, sources, begun, keep, send, held, acc, spots):
+    rows, _, length = spots.shape
     per_row = length // STEP
     row = lax.axis_index("row")
     targets = ready.at[8:16, length:]
     acc[...] = begun[...]
-
-    def read(i, first):
+    width = length // 8
+
+    def spread_sites(c, carry):
+        x, y, z = [
+            sources[c, :, length + k * width : length + (k + 1) * width].astype(f32)
+            for k in range(3)
+        ]
+        norm = x * x + y * y + z * z
+        high = jnp.floor(norm * np.float32(1.0 / 256.0))
+        low = norm - 256.0 * high
+        one = jnp.ones((2, width), f32)
+        for k in range(8):
+            parts = [p[k : k + 1] for p in (x, y, z, high, low)] + [one, 0.0 * one[0:1]]
+            spots[c, :, k * width : (k + 1) * width] = jnp.concatenate(parts, 0).astype(bf16)
+        return carry
+
+    lax.fori_loop(0, rows, spread_sites, 0)
+
+    def where(i):
         chunk = lax.rem(row + 1 + i // per_row, rows)
-        off = pl.multiple_of(lax.rem(i, per_row) * STEP, STEP)
-        return sources[chunk, first : first + 8, pl.ds(off, STEP)]
-
-    scatter_tiles((rows - 1) * per_row, read, targets, held, acc, False)
+        return chunk, pl.ds(pl.multiple_of(lax.rem(i, per_row) * STEP, STEP), STEP)
+
+    def sites_of(i):
+        chunk, cut = where(i)
+        return spots[chunk, :, cut]
+
+    def weights_of(i):
+        chunk, cut = where(i)
+        return sources[chunk, :, cut]
+
+    scatter_tiles((rows - 1) * per_row, sites_of, weights_of, targets, held, acc, False, 4)
     real = acc[0:8]
     imag = acc[8:16]
     upper = real[0:4] - imag[4:8]
@@ -116,7 +138,8 @@
 
 def prepare_kernel(basis, lattice, index, table, spread, ready, *scratch):
     direction, chosen, held_table, points, aims, sems = scratch
-    rows, _, length = spread.shape
+    rows = spread.shape[0]
+    length = points.shape[1]
     wide = aims.shape[1]
     channels = direction.shape[0]
     aim = pl.multiple_of(lax.axis_index("col") * wide, 128)
@@ -151,8 +174,15 @@
     for k in range(table.shape[1]):
         strength = jnp.where(chosen[...] == k, held_table[0:1, k : k + 1], strength)
     copies[3].wait()
-    packed = jnp.concatenate([direction[...] * strength, sites], 0).astype(bf16)
-    ready[:, :length] = packed
+    weighted = (direction[...] * strength).astype(bf16)
+    ready[0:8, :length] = weighted
+    ready[8:16, :length] = sites.astype(bf16)
+    width = length // 8
+    dense = [
+        jnp.concatenate([sites[p : p + 1, k * width : (k + 1) * width] for k in range(8)], 0)
+        for p in range(3)
+    ]
+    packed = jnp.concatenate([weighted] + [d.astype(bf16) for d in dense], 1)
     for k in range(rows):
         spread[k] = packed
     copies[4].wait()
@@ -192,10 +222,13 @@
 
     acc[...] = jnp.zeros_like(acc)
 
-    def read(i, first):
-        return ready[first : first + 8, pl.ds(pl.multiple_of(i * STEP, STEP), STEP)]
-
-    scatter_tiles(length // STEP, read, targets, tiles, acc, True)
+    def sites_of(i):
+        return ready[8:16, pl.ds(pl.multiple_of(i * STEP, STEP), STEP)]
+
+    def weights_of(i):
+        return ready[0:8, pl.ds(pl.multiple_of(i * STEP, STEP), STEP)]
+
+    scatter_tiles(length // STEP, sites_of, weights_of, targets, tiles, acc, True, 2)
 
     total = jnp.zeros((16, count), f32)
     for k in range(points // chunk):
@@ -240,7 +273,7 @@
     packed[8:, :] = gram[...]
 
 
-def final_kernel(total, shared, kept, basis, new, coef, norm, grams, held, sems):
+def final_kernel(total, shared, kept, basis, new, coef, norm, gram_high, gram_low, held, sems):
     parts = shared.shape[0]
     count, points = basis.shape
     width = 256
@@ -264,40 +297,28 @@
     sums = jnp.concatenate([upper, lower], 0)
     lane = lax.broadcasted_iota(jnp.int32, sums.shape, 1)
     sub = lax.broadcasted_iota(jnp.int32, sums.shape, 0)
-    grams[...] = jnp.zeros_like(grams)
+    gram_high[...] = jnp.zeros_like(gram_high)
+    gram_low[...] = jnp.zeros_like(gram_low)
     for q in range(count // 16):
         part = join_halves(shared[q, 24:40, :])
-        grams[16 * q : 16 * q + 8, :] = jnp.where(sub < 4, part, 0.0)
-        grams[16 * q + 8 : 16 * q + 16, :] = jnp.where(sub < 4, pltpu.roll(part, 4, 0), 0.0)
+        pair = jnp.concatenate(
+            [jnp.where(sub < 4, part, 0.0), jnp.where(sub < 4, pltpu.roll(part, 4, 0), 0.0)], 0
+        )
+        top, rest = split(pair)
+        gram_high[16 * q : 16 * q + 16, :] = top
+        gram_low[16 * q : 16 * q + 16, :] = rest
 
     def times_gram(x):
-        return complex_mix(
-            jnp.dot(x, grams[...], preferred_element_type=f32, precision=highest)
+        top, rest = split(x)
+        first = jnp.dot(
+            jnp.concatenate([top, rest], 0), gram_high[...], preferred_element_type=f32
         )
+        second = jnp.dot(top, gram_low[...], preferred_element_type=f32)
+        return complex_mix(first[:8] + first[8:] + second)
 
     products = jnp.where(lane < count, sums, 0.0)
     once = products * scale
     mix = 2.0 * once - times_gram(once) * scale
-    seen = products - 0.5 * times_gram(mix)
-    cross = lax.dot_general(mix, seen, NT, preferred_element_type=f32, precision=highest)
-    cross_t = lax.dot_general(seen, mix, NT, preferred_element_type=f32, precision=highest)
-    own = pltpu.roll(sums, width - count, 1)[:, 0:8]
-    result = (own - cross - cross_t) * scale
-    norm[0] = result[0:4, 0:4]
-    norm[1] = result[0:4, 4:8]
-
-    row = lax.broadcasted_iota(jnp.int32, (width, 128), 0)
-    column = lax.broadcasted_iota(jnp.int32, (width, 128), 1)
-    wanted = ((row & 4) == 0) & (column == (row & 7) * 32 + lax.shift_right_logical(row, 3))
-    chosen = jnp.dot(
-        mix, jnp.where(wanted, 1.0, 0.0), preferred_element_type=f32, precision=highest
-    )
-    blocks = coef.shape[3]
-    for k in range(4):
-        moved = pltpu.roll(chosen, (128 - 32 * k) % 128, 1)
-        coef[0, k] = moved[0:4, 0:blocks]
-        coef[1, k] = moved[4:8, 0:blocks]
-
     mix_high, mix_low = split(mix[:, :count])
     both = jnp.concatenate([mix_high, mix_low], 0)
     for k in range(points // chunk):
@@ -317,6 +338,31 @@
         )
         new[:, cut] = field - (first[:8] + first[8:] + second)
 
+    seen = products - 0.5 * times_gram(mix)
+    cross = lax.dot_general(mix, seen, NT, preferred_element_type=f32, precision=highest)
+    cross_t = lax.dot_general(seen, mix, NT, preferred_element_type=f32, precision=highest)
+    own = pltpu.roll(sums, width - count, 1)[:, 0:8]
+    result = (own - cross - cross_t) * scale
+    norm[0] = result[0:4, 0:4]
+    norm[1] = result[0:4, 4:8]
+
+    row = lax.broadcasted_iota(jnp.int32, (width, 128), 0)
+    column = lax.broadcasted_iota(jnp.int32, (width, 128), 1)
+    wanted = ((row & 4) == 0) & (column == (row & 7) * 32 + lax.shift_right_logical(row, 3))
+    top, rest = split(mix)
+    least = (mix - top.astype(f32) - rest.astype(f32)).astype(bf16)
+    chosen = jnp.dot(
+        jnp.concatenate([top, rest, least], 0),
+        jnp.where(wanted, 1.0, 0.0).astype(bf16),
+        preferred_element_type=f32,
+    )
+    chosen = chosen[:8] + chosen[8:16] + chosen[16:]
+    blocks = coef.shape[3]
+    for k in range(4):
+        moved = pltpu.roll(chosen, (128 - 32 * k) % 128, 1)
+        coef[0, k] = moved[0:4, 0:blocks]
+        coef[1, k] = moved[4:8, 0:blocks]
+
 
 def gather_all(x, axis):
     length = lax.axis_size(axis)
@@ -353,7 +399,7 @@
         in_specs=[HBM, HBM, HBM, HBM],
         out_specs=(VMEM, VMEM),
         out_shape=(
-            jax.ShapeDtypeStruct((rows, 16, length), bf16),
+            jax.ShapeDtypeStruct((rows, 8, length + 3 * (length // 8)), bf16),
             jax.ShapeDtypeStruct((16, length + wide), bf16),
         ),
         scratch_shapes=[
@@ -400,7 +446,11 @@
         out_shape=(half, half),
         in_specs=[VMEM, VMEM, VMEM],
         out_specs=(VMEM, VMEM),
-        scratch_shapes=[held, pltpu.VMEM((16, wide), f32)],
+        scratch_shapes=[
+            held,
+            pltpu.VMEM((16, wide), f32),
+            pltpu.VMEM((rows, 8, length), bf16),
+        ],
         compiler_params=params(),
         cost_estimate=cost(20_000_000_000, 800_000),
         name="scatter_remote",
@@ -429,7 +479,8 @@
             jax.ShapeDtypeStruct((2, inc, inc), f32),
         ),
         scratch_shapes=[
-            pltpu.VMEM((256, 256), f32),
+            pltpu.VMEM((256, 256), bf16),
+            pltpu.VMEM((256, 256), bf16),
             pltpu.VMEM((count, points // 2), f32),
             pltpu.SemaphoreType.DMA((points // 2 // 512,)),
         ],

time: 75 us -> 73.9 us (0.985)
  waiting for transfers between devices: 3.49 us -> 0.96 us
  blocking collectives: 24 us -> 25.6 us
  Pallas kernels: 35.4 us -> 34.3 us
  starting transfers between devices: 10.1 us -> 11.1 us
    all_to_all x1, waiting for transfers between devices: 2.66 us -> 0.13 us  [local(): gathered = lax.all_to_all(spread, 'row', 0, 0, tiled=True)]
    all_to_all x2, blocking collectives: 24 us -> 25.6 us  [gather_all(): lax.all_to_all(jnp.broadcast_to(x[None], (length, *x.shape)), axis, 0, 0,...]
    ppermute x1, starting transfers between devices: 1.75 us -> 2.71 us  [local(): lax.ppermute(send, 'grp', [(i, groups - 1 - i) for i in range(groups)])]
    pallas_call x1, Pallas kernels: 23.6 us -> 22.8 us  [local(): pl.pallas_call(remote_kernel, out_shape=(half, half), in_specs=[VMEM, VME...]
where the time goes in v5:
time: 73.9 us; the launch traced here: 73.5 us
  Pallas kernels  34.3 us (46%)
  blocking collectives  25.6 us (35%)
  starting transfers between devices  11.1 us (15%)
  waiting for transfers between devices  0.96 us (1%)
  local copies, waits for them, and re-layouts  0.93 us (1%)
    all_to_all x2, blocking collectives, gather_all(): lax.all_to_all(jnp.broadcast_to(x[None], (length, *x.shape)), axis, 0, 0,...  25.6 us
    pallas_call x1, Pallas kernels, local(): pl.pallas_call(remote_kernel, out_shape=(half, half), in_specs=[VMEM, VME...  22.8 us
    all_to_all x1, starting transfers between devices, local(): gathered = lax.all_to_all(spread, 'row', 0, 0, tiled=True)  8.34 us
    pallas_call x1, Pallas kernels, local(): pl.pallas_call(local_kernel, in_specs=[VMEM, HBM], out_specs=(VMEM,) * 6,...  6.65 us
    pallas_call x1, Pallas kernels, local(): pl.pallas_call(functools.partial(final_kernel, total), in_specs=[VMEM, VM...  2.77 us
    ppermute x1, starting transfers between devices, local(): lax.ppermute(send, 'grp', [(i, groups - 1 - i) for i in range(groups)])  2.71 us
    pallas_call x1, Pallas kernels, local(): pl.pallas_call(prepare_kernel, in_specs=[HBM, HBM, HBM, HBM], out_specs=(...  1.74 us
  transfers between devices with their start and end apart: 2, of which 2 were waited for; matrix products, arithmetic and copies ran while one was open for 0% of the time, Pallas kernels for 9%

profile of v5, /device:TPU:1, one launch (start us, length us, event | category | flops | bytes accessed | tf_op | source)
XLA Modules:
  0.0 73.5 jit_solution(3084863179999444960)
XLA Ops:
  0.6 1.7 %prepare.1 = (bf16[8,8,2816]{2,1,0:T(8,128)(2,1)}, bf16[16,2560]{1,0:T(8,128)(2,1)}) custom-call(f32[240,4096]{1,0:T(8,128)} %bitcast.4, s32[3,4096]{1,0:T(4,128)} %lattice.1, s32[1,4096]{1,0:T(1,128)} %bitcast.7, f32[1,16]{1,0:T(1,128)} %bitcast.8), custom_call_target="tpu_custom_call" | custom-call | tf_op jit(solution)/shard_map/prepare/pallas_call | solution.py:397
  2.4 8.3 %all-to-all-start = ((bf16[8,8,2816]{2,1,0:T(8,128)(2,1)}), bf16[8,8,2816]{2,1,0:T(8,128)(2,1)S(1)}, u32[]{:S(2)}, u32[]{:S(2)}) async-start(bf16[8,8,2816]{2,1,0:T(8,128)(2,1)} %get-tuple-element.19), calls=%async_computation | async-start | bytes 720896 | tf_op jit(solution)/shard_map/all_to_all | solution.py:416
  10.7 0.0 copy-start
  10.7 0.9 %copy-done = bf16[16,2560]{1,0:T(8,128)(2,1)S(1)} copy-done((bf16[16,2560]{1,0:T(8,128)(2,1)S(1)}, bf16[16,2560]{1,0:T(8,128)(2,1)}, u32[]{:S(2)}) %copy-start) | copy-done | bytes 81944
  11.6 0.0 copy-start.1
  11.6 6.7 %scatter_local.1 = (f32[16,512]{1,0:T(8,128)S(1)}, f32[16,128]{1,0:T(8,128)S(1)}, f32[8,256]{1,0:T(8,128)S(1)}, bf16[240,256]{1,0:T(8,128)(2,1)S(1)}, bf16[240,2...) custom-call(bf16[16,2560]{1,0:T(8,128)(2,1)S(1)} %copy-done, f32[240,4096]{1,0:T(8,128)} %bitcast.5), custom_call_target="tpu_custom_call" | custom-call | flops 5000000000 | bytes 8000000 | tf_op jit(solution)/shard_map/scatter_local/pallas_call | solution.py:420
  18.3 0.1 all-to-all-done.sources
  18.4 0.0 copy-done.1
  18.4 22.8 %scatter_remote.1 = (f32[8,256]{1,0:T(8,128)S(1)}, f32[8,256]{1,0:T(8,128)S(1)}) custom-call(bf16[16,2560]{1,0:T(8,128)(2,1)S(1)} %copy-done.1, bf16[8,8,2816]{2,1,0:T(8,128)(2,1)S(1)} %all-to-all-done.sources, f32[16,512]{1,0:T(8,128)S(1)} %get-tuple-element.20.begun), custom_call_target="tpu_custom_call" | custom-call | flops 20000000000 | bytes 800000 | tf_op jit(solution)/shard_map/scatter_remote/pallas_call | solution.py:444
  41.2 2.7 %collective-permute-start = (f32[8,256]{1,0:T(8,128)S(1)}, f32[8,256]{1,0:T(8,128)S(1)}, u32[]{:S(2)}, u32[]{:S(2)}) collective-permute-start(f32[8,256]{1,0:T(8,128)S(1)} %get-tuple-element.22), channel_id=1, source_target_pairs={{0,1},{1,0},{2,3},{3,2},{4,5},{5,4},{6,7},{7,6},{8,9},{9,8},{10,11... | collective-permute-start | bytes 24584 | tf_op jit(solution)/shard_map/ppermute | solution.py:458
  43.9 0.8 %collective-permute-done.got = f32[8,256]{1,0:T(8,128)S(1)} collective-permute-done((f32[8,256]{1,0:T(8,128)S(1)}, f32[8,256]{1,0:T(8,128)S(1)}, u32[]{:S(2)}, u32[]{:S(2)}) %collective-permute-start) | collective-permute-done | bytes 8224 | tf_op jit(solution)/shard_map/ppermute | solution.py:458
  44.7 0.3 project.1
  45.1 11.7 %all_to_all.15 = f32[8,24,128]{2,1,0:T(8,128)S(1)} all-to-all(f32[8,24,128]{2,1,0:T(8,128)S(1)} %broadcast_in_dim.20), channel_id=1, replica_groups=mesh['row'=8,'col'=8,'grp'=2] {'row'}, dimensions={0} | all-to-all | bytes 196608 | tf_op jit(solution)/shard_map/all_to_all | solution.py:369
  56.9 13.8 %all_to_all.16.shared = f32[16,40,128]{2,1,0:T(8,128)S(1)} all-to-all(f32[16,40,128]{2,1,0:T(8,128)S(1)} %broadcast_in_dim.21), channel_id=1, replica_groups=mesh['row'=8,'col'=8,'grp'=2] {'col','grp'}, dimensions={0} | all-to-all | bytes 655360 | tf_op jit(solution)/shard_map/all_to_all | solution.py:369
  70.7 2.8 %finish.1 = (f32[8,4096]{1,0:T(8,128)}, f32[2,4,4,30]{3,2,1,0:T(4,128)}, f32[2,4,4]{2,1,0:T(4,128)}) custom-call(f32[16,40,128]{2,1,0:T(8,128)S(1)} %all_to_all.16.shared, f32[240,2048]{1,0:T(8,128)S(1)} %get-tuple-element.29.kept, f32[240,4096]{1,0:T(8,128)} %bitcast.6), custom_call_target="tpu_custom_call" | custom-call | tf_op jit(solution)/shard_map/finish/pallas_call | solution.py:472
  (4 shorter events, 0.1 us)
Async XLA Ops:
  2.4 16.0 %all-to-all-start = ((bf16[8,8,2816]{2,1,0:T(8,128)(2,1)}), bf16[8,8,2816]{2,1,0:T(8,128)(2,1)S(1)}, u32[]{:S(2)}, u32[]{:S(2)}) async-start(bf16[8,8,2816]{2,1,0:T(8,128)(2,1)} %get-tuple-element.19), calls=%async_computation | async-start | bytes 720896 | tf_op jit(solution)/shard_map/all_to_all | solution.py:416
  10.7 0.9 %copy-start = (bf16[16,2560]{1,0:T(8,128)(2,1)S(1)}, bf16[16,2560]{1,0:T(8,128)(2,1)}, u32[]{:S(2)}) copy-start(bf16[16,2560]{1,0:T(8,128)(2,1)} %get-tuple-element.18.ready) | copy-start | bytes 245764
  11.6 6.8 %copy-start.1 = (bf16[16,2560]{1,0:T(8,128)(2,1)S(1)}, bf16[16,2560]{1,0:T(8,128)(2,1)}, u32[]{:S(2)}) copy-start(bf16[16,2560]{1,0:T(8,128)(2,1)} %get-tuple-element.18.ready) | copy-start | bytes 245764
  41.2 3.5 %collective-permute-start = (f32[8,256]{1,0:T(8,128)S(1)}, f32[8,256]{1,0:T(8,128)S(1)}, u32[]{:S(2)}, u32[]{:S(2)}) collective-permute-start(f32[8,256]{1,0:T(8,128)S(1)} %get-tuple-element.22), channel_id=1, source_target_pairs={{0,1},{1,0},{2,3},{3,2},{4,5},{5,4},{6,7},{7,6},{8,9},{9,8},{10,11... | collective-permute-start | bytes 24584 | tf_op jit(solution)/shard_map/ppermute | solution.py:458

commit v6 on v5

--- a/solution.py
+++ b/solution.py
@@ -273,7 +273,8 @@
     packed[8:, :] = gram[...]
 
 
-def final_kernel(total, shared, kept, basis, new, coef, norm, gram_high, gram_low, held, sems):
+def final_kernel(total, shared, kept, basis, new, coef, norm, *scratch):
+    gram_high, gram_low, held, result, sems, out_sems = scratch
     parts = shared.shape[0]
     count, points = basis.shape
     width = 256
@@ -321,6 +322,7 @@
     mix = 2.0 * once - times_gram(once) * scale
     mix_high, mix_low = split(mix[:, :count])
     both = jnp.concatenate([mix_high, mix_low], 0)
+    writes = []
     for k in range(points // chunk):
         cut = slice(k * chunk, (k + 1) * chunk)
         if k * chunk < half:
@@ -336,15 +338,17 @@
         field = jnp.concatenate(
             [join_halves(shared[each * k + i, 0:16, :]) for i in range(each)], 1
         )
-        new[:, cut] = field - (first[:8] + first[8:] + second)
+        result[:, cut] = field - (first[:8] + first[8:] + second)
+        writes.append(pltpu.make_async_copy(result.at[:, cut], new.at[:, cut], out_sems.at[k]))
+        writes[-1].start()
 
     seen = products - 0.5 * times_gram(mix)
     cross = lax.dot_general(mix, seen, NT, preferred_element_type=f32, precision=highest)
     cross_t = lax.dot_general(seen, mix, NT, preferred_element_type=f32, precision=highest)
     own = pltpu.roll(sums, width - count, 1)[:, 0:8]
-    result = (own - cross - cross_t) * scale
-    norm[0] = result[0:4, 0:4]
-    norm[1] = result[0:4, 4:8]
+    squares = (own - cross - cross_t) * scale
+    norm[0] = squares[0:4, 0:4]
+    norm[1] = squares[0:4, 4:8]
 
     row = lax.broadcasted_iota(jnp.int32, (width, 128), 0)
     column = lax.broadcasted_iota(jnp.int32, (width, 128), 1)
@@ -362,6 +366,8 @@
         moved = pltpu.roll(chosen, (128 - 32 * k) % 128, 1)
         coef[0, k] = moved[0:4, 0:blocks]
         coef[1, k] = moved[4:8, 0:blocks]
+    for write in writes:
+        write.wait()
 
 
 def gather_all(x, axis):
@@ -394,6 +400,7 @@
     wide = own * groups
     length = points // groups
     flat = krylov_basis.reshape(count, points)
+    stay = points // 2
     spread, ready = pl.pallas_call(
         prepare_kernel,
         in_specs=[HBM, HBM, HBM, HBM],
@@ -427,11 +434,11 @@
             half,
             jax.ShapeDtypeStruct((count, own), bf16),
             jax.ShapeDtypeStruct((count, own), bf16),
-            jax.ShapeDtypeStruct((count, points // 2), f32),
+            jax.ShapeDtypeStruct((count, stay), f32),
         ),
         scratch_shapes=[
             held,
-            pltpu.VMEM((count, points // 2), f32),
+            pltpu.VMEM((count, points - stay), f32),
             pltpu.VMEM((count, points), bf16),
             pltpu.VMEM((count, points), bf16),
             pltpu.SemaphoreType.DMA((9,)),
@@ -472,7 +479,7 @@
     new_block, coef, norm = pl.pallas_call(
         functools.partial(final_kernel, total),
         in_specs=[VMEM, VMEM, HBM],
-        out_specs=(VMEM, VMEM, VMEM),
+        out_specs=(HBM, VMEM, VMEM),
         out_shape=(
             jax.ShapeDtypeStruct((channels, points), f32),
             jax.ShapeDtypeStruct((2, inc, inc, blocks), f32),
@@ -481,8 +488,10 @@
         scratch_shapes=[
             pltpu.VMEM((256, 256), bf16),
             pltpu.VMEM((256, 256), bf16),
-            pltpu.VMEM((count, points // 2), f32),
-            pltpu.SemaphoreType.DMA((points // 2 // 512,)),
+            pltpu.VMEM((count, points - stay), f32),
+            pltpu.VMEM((channels, points), f32),
+            pltpu.SemaphoreType.DMA(((points - stay) // 512,)),
+            pltpu.SemaphoreType.DMA((points // 512,)),
         ],
         compiler_params=params(50 << 20),
         name="finish",

time: 73.9 us -> 74.2 us (level)
  no operation moved by 1% of the time
where the time goes in v6:
time: 74.2 us; the launch traced here: 73.8 us
  Pallas kernels  34.6 us (47%)
  blocking collectives  25.6 us (35%)
  starting transfers between devices  11.1 us (15%)
  waiting for transfers between devices  0.96 us (1%)
  local copies, waits for them, and re-layouts  0.93 us (1%)
    all_to_all x2, blocking collectives, gather_all(): lax.all_to_all(jnp.broadcast_to(x[None], (length, *x.shape)), axis, 0, 0,...  25.6 us
    pallas_call x1, Pallas kernels, local(): pl.pallas_call(remote_kernel, out_shape=(half, half), in_specs=[VMEM, VME...  22.8 us
    all_to_all x1, starting transfers between devices, local(): gathered = lax.all_to_all(spread, 'row', 0, 0, tiled=True)  8.34 us
    pallas_call x1, Pallas kernels, local(): pl.pallas_call(local_kernel, in_specs=[VMEM, HBM], out_specs=(VMEM,) * 6,...  6.65 us
    pallas_call x1, Pallas kernels, local(): pl.pallas_call(functools.partial(final_kernel, total), in_specs=[VMEM, VM...  3.1 us
    ppermute x1, starting transfers between devices, local(): lax.ppermute(send, 'grp', [(i, groups - 1 - i) for i in range(groups)])  2.71 us
    pallas_call x1, Pallas kernels, local(): pl.pallas_call(prepare_kernel, in_specs=[HBM, HBM, HBM, HBM], out_specs=(...  1.74 us
  transfers between devices with their start and end apart: 2, of which 2 were waited for; matrix products, arithmetic and copies ran while one was open for 0% of the time, Pallas kernels for 9%

profile of v6, /device:TPU:1, one launch (start us, length us, event | category | flops | bytes accessed | tf_op | source)
XLA Modules:
  0.0 73.8 jit_solution(8944816113224333624)
XLA Ops:
  0.6 1.7 %prepare.1 = (bf16[8,8,2816]{2,1,0:T(8,128)(2,1)}, bf16[16,2560]{1,0:T(8,128)(2,1)}) custom-call(f32[240,4096]{1,0:T(8,128)} %bitcast.4, s32[3,4096]{1,0:T(4,128)} %lattice.1, s32[1,4096]{1,0:T(1,128)} %bitcast.7, f32[1,16]{1,0:T(1,128)} %bitcast.8), custom_call_target="tpu_custom_call" | custom-call | tf_op jit(solution)/shard_map/prepare/pallas_call | solution.py:404
  2.4 8.3 %all-to-all-start = ((bf16[8,8,2816]{2,1,0:T(8,128)(2,1)}), bf16[8,8,2816]{2,1,0:T(8,128)(2,1)S(1)}, u32[]{:S(2)}, u32[]{:S(2)}) async-start(bf16[8,8,2816]{2,1,0:T(8,128)(2,1)} %get-tuple-element.19), calls=%async_computation | async-start | bytes 720896 | tf_op jit(solution)/shard_map/all_to_all | solution.py:423
  10.7 0.0 copy-start
  10.7 0.9 %copy-done = bf16[16,2560]{1,0:T(8,128)(2,1)S(1)} copy-done((bf16[16,2560]{1,0:T(8,128)(2,1)S(1)}, bf16[16,2560]{1,0:T(8,128)(2,1)}, u32[]{:S(2)}) %copy-start) | copy-done | bytes 81944
  11.6 0.0 copy-start.1
  11.6 6.7 %scatter_local.1 = (f32[16,512]{1,0:T(8,128)S(1)}, f32[16,128]{1,0:T(8,128)S(1)}, f32[8,256]{1,0:T(8,128)S(1)}, bf16[240,256]{1,0:T(8,128)(2,1)S(1)}, bf16[240,2...) custom-call(bf16[16,2560]{1,0:T(8,128)(2,1)S(1)} %copy-done, f32[240,4096]{1,0:T(8,128)} %bitcast.5), custom_call_target="tpu_custom_call" | custom-call | flops 5000000000 | bytes 8000000 | tf_op jit(solution)/shard_map/scatter_local/pallas_call | solution.py:427
  18.3 0.1 all-to-all-done.sources
  18.4 0.0 copy-done.1
  18.4 22.8 %scatter_remote.1 = (f32[8,256]{1,0:T(8,128)S(1)}, f32[8,256]{1,0:T(8,128)S(1)}) custom-call(bf16[16,2560]{1,0:T(8,128)(2,1)S(1)} %copy-done.1, bf16[8,8,2816]{2,1,0:T(8,128)(2,1)S(1)} %all-to-all-done.sources, f32[16,512]{1,0:T(8,128)S(1)} %get-tuple-element.20.begun), custom_call_target="tpu_custom_call" | custom-call | flops 20000000000 | bytes 800000 | tf_op jit(solution)/shard_map/scatter_remote/pallas_call | solution.py:451
  41.2 2.7 %collective-permute-start = (f32[8,256]{1,0:T(8,128)S(1)}, f32[8,256]{1,0:T(8,128)S(1)}, u32[]{:S(2)}, u32[]{:S(2)}) collective-permute-start(f32[8,256]{1,0:T(8,128)S(1)} %get-tuple-element.22), channel_id=1, source_target_pairs={{0,1},{1,0},{2,3},{3,2},{4,5},{5,4},{6,7},{7,6},{8,9},{9,8},{10,11... | collective-permute-start | bytes 24584 | tf_op jit(solution)/shard_map/ppermute | solution.py:465
  43.9 0.8 %collective-permute-done.got = f32[8,256]{1,0:T(8,128)S(1)} collective-permute-done((f32[8,256]{1,0:T(8,128)S(1)}, f32[8,256]{1,0:T(8,128)S(1)}, u32[]{:S(2)}, u32[]{:S(2)}) %collective-permute-start) | collective-permute-done | bytes 8224 | tf_op jit(solution)/shard_map/ppermute | solution.py:465
  44.7 0.3 project.1
  45.1 11.7 %all_to_all.15 = f32[8,24,128]{2,1,0:T(8,128)S(1)} all-to-all(f32[8,24,128]{2,1,0:T(8,128)S(1)} %broadcast_in_dim.20), channel_id=1, replica_groups=mesh['row'=8,'col'=8,'grp'=2] {'row'}, dimensions={0} | all-to-all | bytes 196608 | tf_op jit(solution)/shard_map/all_to_all | solution.py:375
  56.9 13.8 %all_to_all.16.shared = f32[16,40,128]{2,1,0:T(8,128)S(1)} all-to-all(f32[16,40,128]{2,1,0:T(8,128)S(1)} %broadcast_in_dim.21), channel_id=1, replica_groups=mesh['row'=8,'col'=8,'grp'=2] {'col','grp'}, dimensions={0} | all-to-all | bytes 655360 | tf_op jit(solution)/shard_map/all_to_all | solution.py:375
  70.7 3.1 %finish.1 = (f32[8,4096]{1,0:T(8,128)}, f32[2,4,4,30]{3,2,1,0:T(4,128)}, f32[2,4,4]{2,1,0:T(4,128)}) custom-call(f32[16,40,128]{2,1,0:T(8,128)S(1)} %all_to_all.16.shared, f32[240,2048]{1,0:T(8,128)S(1)} %get-tuple-element.29.kept, f32[240,4096]{1,0:T(8,128)} %bitcast.6), custom_call_target="tpu_custom_call" | custom-call | tf_op jit(solution)/shard_map/finish/pallas_call | solution.py:479
  (4 shorter events, 0.1 us)
Async XLA Ops:
  2.4 16.0 %all-to-all-start = ((bf16[8,8,2816]{2,1,0:T(8,128)(2,1)}), bf16[8,8,2816]{2,1,0:T(8,128)(2,1)S(1)}, u32[]{:S(2)}, u32[]{:S(2)}) async-start(bf16[8,8,2816]{2,1,0:T(8,128)(2,1)} %get-tuple-element.19), calls=%async_computation | async-start | bytes 720896 | tf_op jit(solution)/shard_map/all_to_all | solution.py:423
  10.7 0.9 %copy-start = (bf16[16,2560]{1,0:T(8,128)(2,1)S(1)}, bf16[16,2560]{1,0:T(8,128)(2,1)}, u32[]{:S(2)}) copy-start(bf16[16,2560]{1,0:T(8,128)(2,1)} %get-tuple-element.18.ready) | copy-start | bytes 245764
  11.6 6.8 %copy-start.1 = (bf16[16,2560]{1,0:T(8,128)(2,1)S(1)}, bf16[16,2560]{1,0:T(8,128)(2,1)}, u32[]{:S(2)}) copy-start(bf16[16,2560]{1,0:T(8,128)(2,1)} %get-tuple-element.18.ready) | copy-start | bytes 245764
  41.2 3.5 %collective-permute-start = (f32[8,256]{1,0:T(8,128)S(1)}, f32[8,256]{1,0:T(8,128)S(1)}, u32[]{:S(2)}, u32[]{:S(2)}) collective-permute-start(f32[8,256]{1,0:T(8,128)S(1)} %get-tuple-element.22), channel_id=1, source_target_pairs={{0,1},{1,0},{2,3},{3,2},{4,5},{5,4},{6,7},{7,6},{8,9},{9,8},{10,11... | collective-permute-start | bytes 24584 | tf_op jit(solution)/shard_map/ppermute | solution.py:465

commit v7 on v5

--- a/solution.py
+++ b/solution.py
@@ -273,16 +273,32 @@
     packed[8:, :] = gram[...]
 
 
-def final_kernel(total, shared, kept, basis, new, coef, norm, gram_high, gram_low, held, sems):
+def preload_kernel(sums, basis, ahead, sems):
+    del sums
+    chunk = 512
+    first = basis.shape[1] // 2
+    copies = []
+    for k in range(sems.shape[0]):
+        cut = slice(k * chunk, (k + 1) * chunk)
+        there = slice(first + k * chunk, first + (k + 1) * chunk)
+        copies.append(pltpu.make_async_copy(basis.at[:, there], ahead.at[:, cut], sems.at[k]))
+        copies[-1].start()
+    for copy in copies:
+        copy.wait()
+
+
+def final_kernel(total, shared, kept, ahead, basis, new, coef, norm, *scratch):
+    gram_high, gram_low, held, sems = scratch
     parts = shared.shape[0]
     count, points = basis.shape
     width = 256
     chunk = 512
-    half = points - held.shape[1]
+    half = kept.shape[1]
+    last = points - held.shape[1]
     copies = []
     for k in range(sems.shape[0]):
         cut = slice(k * chunk, (k + 1) * chunk)
-        there = slice(half + k * chunk, half + (k + 1) * chunk)
+        there = slice(last + k * chunk, last + (k + 1) * chunk)
         copies.append(pltpu.make_async_copy(basis.at[:, there], held.at[:, cut], sems.at[k]))
         copies[-1].start()
     scale = np.float32(1.0 / total)
@@ -325,8 +341,10 @@
         cut = slice(k * chunk, (k + 1) * chunk)
         if k * chunk < half:
             columns = kept[:, cut]
+        elif k * chunk < last:
+            columns = ahead[:, k * chunk - half : (k + 1) * chunk - half]
         else:
-            later = k - half // chunk
+            later = k - last // chunk
             copies[later].wait()
             columns = held[:, later * chunk : (later + 1) * chunk]
         top, rest = split(columns)
@@ -469,9 +487,20 @@
     row_sums = jnp.sum(gather_all(partial, "row"), axis=0)
     shared = gather_all(jnp.concatenate([initial, row_sums], 0), ("col", "grp"))
 
+    ahead = pl.pallas_call(
+        preload_kernel,
+        in_specs=[VMEM, HBM],
+        out_specs=VMEM,
+        out_shape=jax.ShapeDtypeStruct((count, points // 4), f32),
+        scratch_shapes=[pltpu.SemaphoreType.DMA((points // 4 // 512,))],
+        compiler_params=params(50 << 20),
+        cost_estimate=cost(3_000_000_000, 8_000_000),
+        name="preload",
+    )(row_sums, flat)
+
     new_block, coef, norm = pl.pallas_call(
         functools.partial(final_kernel, total),
-        in_specs=[VMEM, VMEM, HBM],
+        in_specs=[VMEM, VMEM, VMEM, HBM],
         out_specs=(VMEM, VMEM, VMEM),
         out_shape=(
             jax.ShapeDtypeStruct((channels, points), f32),
@@ -481,12 +510,12 @@
         scratch_shapes=[
             pltpu.VMEM((256, 256), bf16),
             pltpu.VMEM((256, 256), bf16),
-            pltpu.VMEM((count, points // 2), f32),
-            pltpu.SemaphoreType.DMA((points // 2 // 512,)),
+            pltpu.VMEM((count, points // 4), f32),
+            pltpu.SemaphoreType.DMA((points // 4 // 512,)),
         ],
         compiler_params=params(50 << 20),
         name="finish",
-    )(shared, kept, flat)
+    )(shared, kept, ahead, flat)
     return new_block, coef.transpose(3, 0, 1, 2), norm
 
 

time: 73.9 us -> 75.1 us (1.016)
  blocking collectives: 25.6 us -> 11.7 us
  waiting for transfers between devices: 0.96 us -> 7.37 us
  starting transfers between devices: 11.1 us -> 17.5 us
  Pallas kernels: 34.3 us -> 35.8 us
    all_to_all x2 -> x1, blocking collectives: 25.6 us -> 11.7 us  [gather_all(): lax.all_to_all(jnp.broadcast_to(x[None], (length, *x.shape)), axis, 0, 0,...]
    all_to_all x0 -> x1, starting transfers between devices: none -> 6.44 us  [gather_all(): lax.all_to_all(jnp.broadcast_to(x[None], (length, *x.shape)), axis, 0, 0,...]
    all_to_all x0 -> x1, waiting for transfers between devices: none -> 6.41 us  [gather_all(): lax.all_to_all(jnp.broadcast_to(x[None], (length, *x.shape)), axis, 0, 0,...]
    pallas_call x0 -> x1, Pallas kernels: none -> 1.2 us  [local(): pl.pallas_call(preload_kernel, in_specs=[VMEM, HBM], out_specs=VMEM, out_...]
  transfers between devices with their start and end apart: 2 -> 3, of which waited for: 2 -> 3; matrix products, arithmetic and copies ran while one was open for 0% -> 0% of each run, Pallas kernels for 9% -> 11%
where the time goes in v7:
time: 75.1 us; the launch traced here: 74.7 us
  Pallas kernels  35.8 us (48%)
  starting transfers between devices  17.5 us (23%)
  blocking collectives  11.7 us (16%)
  waiting for transfers between devices  7.37 us (10%)
  local copies, waits for them, and re-layouts  1.65 us (2%)
    pallas_call x1, Pallas kernels, local(): pl.pallas_call(remote_kernel, out_shape=(half, half), in_specs=[VMEM, VME...  22.8 us
    all_to_all x1, blocking collectives, gather_all(): lax.all_to_all(jnp.broadcast_to(x[None], (length, *x.shape)), axis, 0, 0,...  11.7 us
    all_to_all x1, starting transfers between devices, local(): gathered = lax.all_to_all(spread, 'row', 0, 0, tiled=True)  8.34 us
    pallas_call x1, Pallas kernels, local(): pl.pallas_call(local_kernel, in_specs=[VMEM, HBM], out_specs=(VMEM,) * 6,...  6.65 us
    all_to_all x1, starting transfers between devices, gather_all(): lax.all_to_all(jnp.broadcast_to(x[None], (length, *x.shape)), axis, 0, 0,...  6.44 us
    all_to_all x1, waiting for transfers between devices, gather_all(): lax.all_to_all(jnp.broadcast_to(x[None], (length, *x.shape)), axis, 0, 0,...  6.41 us
    pallas_call x1, Pallas kernels, local(): pl.pallas_call(functools.partial(final_kernel, total), in_specs=[VMEM, VM...  3.04 us
    ppermute x1, starting transfers between devices, local(): lax.ppermute(send, 'grp', [(i, groups - 1 - i) for i in range(groups)])  2.71 us
  transfers between devices with their start and end apart: 3, of which 3 were waited for; matrix products, arithmetic and copies ran while one was open for 0% of the time, Pallas kernels for 11%

profile of v7, /device:TPU:1, one launch (start us, length us, event | category | flops | bytes accessed | tf_op | source)
XLA Modules:
  0.0 74.7 jit_solution(17377894502588196201)
XLA Ops:
  0.6 1.7 %prepare.1 = (bf16[8,8,2816]{2,1,0:T(8,128)(2,1)}, bf16[16,2560]{1,0:T(8,128)(2,1)}) custom-call(f32[240,4096]{1,0:T(8,128)} %bitcast.4, s32[3,4096]{1,0:T(4,128)} %lattice.1, s32[1,4096]{1,0:T(1,128)} %bitcast.8, f32[1,16]{1,0:T(1,128)} %bitcast.9), custom_call_target="tpu_custom_call" | custom-call | tf_op jit(solution)/shard_map/prepare/pallas_call | solution.py:415
  2.4 8.3 %all-to-all-start = ((bf16[8,8,2816]{2,1,0:T(8,128)(2,1)}), bf16[8,8,2816]{2,1,0:T(8,128)(2,1)S(1)}, u32[]{:S(2)}, u32[]{:S(2)}) async-start(bf16[8,8,2816]{2,1,0:T(8,128)(2,1)} %get-tuple-element.19), calls=%async_computation | async-start | bytes 720896 | tf_op jit(solution)/shard_map/all_to_all | solution.py:434
  10.7 0.0 copy-start
  10.7 0.9 %copy-done = bf16[16,2560]{1,0:T(8,128)(2,1)S(1)} copy-done((bf16[16,2560]{1,0:T(8,128)(2,1)S(1)}, bf16[16,2560]{1,0:T(8,128)(2,1)}, u32[]{:S(2)}) %copy-start) | copy-done | bytes 81944
  11.6 0.0 copy-start.1
  11.6 6.7 %scatter_local.1 = (f32[16,512]{1,0:T(8,128)S(1)}, f32[16,128]{1,0:T(8,128)S(1)}, f32[8,256]{1,0:T(8,128)S(1)}, bf16[240,256]{1,0:T(8,128)(2,1)S(1)}, bf16[240,2...) custom-call(bf16[16,2560]{1,0:T(8,128)(2,1)S(1)} %copy-done, f32[240,4096]{1,0:T(8,128)} %bitcast.5), custom_call_target="tpu_custom_call" | custom-call | flops 5000000000 | bytes 8000000 | tf_op jit(solution)/shard_map/scatter_local/pallas_call | solution.py:438
  18.3 0.1 all-to-all-done.sources
  18.4 0.0 copy-done.1
  18.4 22.8 %scatter_remote.1 = (f32[8,256]{1,0:T(8,128)S(1)}, f32[8,256]{1,0:T(8,128)S(1)}) custom-call(bf16[16,2560]{1,0:T(8,128)(2,1)S(1)} %copy-done.1, bf16[8,8,2816]{2,1,0:T(8,128)(2,1)S(1)} %all-to-all-done.sources, f32[16,512]{1,0:T(8,128)S(1)} %get-tuple-element.20.begun), custom_call_target="tpu_custom_call" | custom-call | flops 20000000000 | bytes 800000 | tf_op jit(solution)/shard_map/scatter_remote/pallas_call | solution.py:462
  41.2 2.7 %collective-permute-start = (f32[8,256]{1,0:T(8,128)S(1)}, f32[8,256]{1,0:T(8,128)S(1)}, u32[]{:S(2)}, u32[]{:S(2)}) collective-permute-start(f32[8,256]{1,0:T(8,128)S(1)} %get-tuple-element.22), channel_id=1, source_target_pairs={{0,1},{1,0},{2,3},{3,2},{4,5},{5,4},{6,7},{7,6},{8,9},{9,8},{10,11... | collective-permute-start | bytes 24584 | tf_op jit(solution)/shard_map/ppermute | solution.py:476
  43.9 0.8 %collective-permute-done.got = f32[8,256]{1,0:T(8,128)S(1)} collective-permute-done((f32[8,256]{1,0:T(8,128)S(1)}, f32[8,256]{1,0:T(8,128)S(1)}, u32[]{:S(2)}, u32[]{:S(2)}) %collective-permute-start) | collective-permute-done | bytes 8224 | tf_op jit(solution)/shard_map/ppermute | solution.py:476
  44.7 0.3 project.1
  45.1 11.7 %all_to_all.15 = f32[8,24,128]{2,1,0:T(8,128)S(1)} all-to-all(f32[8,24,128]{2,1,0:T(8,128)S(1)} %broadcast_in_dim.20), channel_id=1, replica_groups=mesh['row'=8,'col'=8,'grp'=2] {'row'}, dimensions={0} | all-to-all | bytes 196608 | tf_op jit(solution)/shard_map/all_to_all | solution.py:387
  56.8 0.7 broadcast_in_dim.21
  57.6 6.4 %all-to-all-start.2 = ((f32[16,40,128]{2,1,0:T(8,128)}), f32[16,40,128]{2,1,0:T(8,128)S(1)}, u32[]{:S(2)}, u32[]{:S(2)}) async-start(f32[16,40,128]{2,1,0:T(8,128)} %broadcast_in_dim.21), calls=%async_computation.2 | async-start | bytes 655360 | tf_op jit(solution)/shard_map/all_to_all | solution.py:387
  64.0 1.2 %preload.1.ahead = f32[240,1024]{1,0:T(8,128)S(1)} custom-call(f32[24,128]{1,0:T(8,128)S(1)} %reduce_sum.9.sums, f32[240,4096]{1,0:T(8,128)} %bitcast.6), custom_call_target="tpu_custom_call" | custom-call | flops 3000000000 | bytes 8000000 | tf_op jit(solution)/shard_map/preload/pallas_call | solution.py:490
  65.2 6.4 %all-to-all-done.2.shared = f32[16,40,128]{2,1,0:T(8,128)S(1)} async-done(((f32[16,40,128]{2,1,0:T(8,128)}), f32[16,40,128]{2,1,0:T(8,128)S(1)}, u32[]{:S(2)}, u32[]{:S(2)}) %all-to-all-start.2) | async-done | bytes 327712 | tf_op jit(solution)/shard_map/all_to_all | solution.py:387
  71.6 3.0 %finish.1 = (f32[8,4096]{1,0:T(8,128)}, f32[2,4,4,30]{3,2,1,0:T(4,128)}, f32[2,4,4]{2,1,0:T(4,128)}) custom-call(f32[16,40,128]{2,1,0:T(8,128)S(1)} %all-to-all-done.2.shared, f32[240,2048]{1,0:T(8,128)S(1)} %get-tuple-element.29.kept, f32[240,1024]{1,0:T(8,128)S(1)} %preload.1.ahead, f32[240,4096]{1,0:T(8,128)} %bitcast.7), custom_call_target="tpu_custom_call" | custom-call | tf_op jit(solution)/shard_map/finish/pallas_call | solution.py:501
  (3 shorter events, 0.0 us)
Async XLA Ops:
  2.4 16.0 %all-to-all-start = ((bf16[8,8,2816]{2,1,0:T(8,128)(2,1)}), bf16[8,8,2816]{2,1,0:T(8,128)(2,1)S(1)}, u32[]{:S(2)}, u32[]{:S(2)}) async-start(bf16[8,8,2816]{2,1,0:T(8,128)(2,1)} %get-tuple-element.19), calls=%async_computation | async-start | bytes 720896 | tf_op jit(solution)/shard_map/all_to_all | solution.py:434
  10.7 0.9 %copy-start = (bf16[16,2560]{1,0:T(8,128)(2,1)S(1)}, bf16[16,2560]{1,0:T(8,128)(2,1)}, u32[]{:S(2)}) copy-start(bf16[16,2560]{1,0:T(8,128)(2,1)} %get-tuple-element.18.ready) | copy-start | bytes 245764
  11.6 6.8 %copy-start.1 = (bf16[16,2560]{1,0:T(8,128)(2,1)S(1)}, bf16[16,2560]{1,0:T(8,128)(2,1)}, u32[]{:S(2)}) copy-start(bf16[16,2560]{1,0:T(8,128)(2,1)} %get-tuple-element.18.ready) | copy-start | bytes 245764
  41.2 3.5 %collective-permute-start = (f32[8,256]{1,0:T(8,128)S(1)}, f32[8,256]{1,0:T(8,128)S(1)}, u32[]{:S(2)}, u32[]{:S(2)}) collective-permute-start(f32[8,256]{1,0:T(8,128)S(1)} %get-tuple-element.22), channel_id=1, source_target_pairs={{0,1},{1,0},{2,3},{3,2},{4,5},{5,4},{6,7},{7,6},{8,9},{9,8},{10,11... | collective-permute-start | bytes 24584 | tf_op jit(solution)/shard_map/ppermute | solution.py:476
  57.6 14.1 %all-to-all-start.2 = ((f32[16,40,128]{2,1,0:T(8,128)}), f32[16,40,128]{2,1,0:T(8,128)S(1)}, u32[]{:S(2)}, u32[]{:S(2)}) async-start(f32[16,40,128]{2,1,0:T(8,128)} %broadcast_in_dim.21), calls=%async_computation.2 | async-start | bytes 655360 | tf_op jit(solution)/shard_map/all_to_all | solution.py:387

commit v8 on v5

--- a/solution.py
+++ b/solution.py
@@ -137,7 +137,7 @@
 
 
 def prepare_kernel(basis, lattice, index, table, spread, ready, *scratch):
-    direction, chosen, held_table, points, aims, sems = scratch
+    direction, chosen, held_table, points, aims, packed, sems, out_sems = scratch
     rows = spread.shape[0]
     length = points.shape[1]
     wide = aims.shape[1]
@@ -175,20 +175,25 @@
         strength = jnp.where(chosen[...] == k, held_table[0:1, k : k + 1], strength)
     copies[3].wait()
     weighted = (direction[...] * strength).astype(bf16)
-    ready[0:8, :length] = weighted
-    ready[8:16, :length] = sites.astype(bf16)
     width = length // 8
     dense = [
         jnp.concatenate([sites[p : p + 1, k * width : (k + 1) * width] for k in range(8)], 0)
         for p in range(3)
     ]
-    packed = jnp.concatenate([weighted] + [d.astype(bf16) for d in dense], 1)
-    for k in range(rows):
-        spread[k] = packed
+    packed[...] = jnp.concatenate([weighted] + [d.astype(bf16) for d in dense], 1)
+    writes = [
+        pltpu.make_async_copy(packed, spread.at[k], out_sems.at[k]) for k in range(rows)
+    ]
+    for write in writes:
+        write.start()
+    ready[0:8, :length] = weighted
+    ready[8:16, :length] = sites.astype(bf16)
     copies[4].wait()
     x, y, z, high, low, one = shared_rows(aims[...])
     sites = stacked([-2 * x, -2 * y, -2 * z, 256 * one, one, 256 * high, low, 0 * one])
     ready[:, length:] = jnp.concatenate([jnp.zeros_like(sites), sites], 0).astype(bf16)
+    for write in writes:
+        write.wait()
 
 
 def local_kernel(ready, basis, *rest):
@@ -397,7 +402,7 @@
     spread, ready = pl.pallas_call(
         prepare_kernel,
         in_specs=[HBM, HBM, HBM, HBM],
-        out_specs=(VMEM, VMEM),
+        out_specs=(HBM, VMEM),
         out_shape=(
             jax.ShapeDtypeStruct((rows, 8, length + 3 * (length // 8)), bf16),
             jax.ShapeDtypeStruct((16, length + wide), bf16),
@@ -408,7 +413,9 @@
             pltpu.VMEM((1, strength_table.shape[0]), f32),
             pltpu.VMEM((3, length), jnp.int32),
             pltpu.VMEM((3, wide), jnp.int32),
+            pltpu.VMEM((8, length + 3 * (length // 8)), bf16),
             pltpu.SemaphoreType.DMA((5,)),
+            pltpu.SemaphoreType.DMA((rows,)),
         ],
         compiler_params=params((64 << 20) - (64 << 10)),
         name="prepare",

time: 73.9 us -> 74.5 us (level)
  no operation moved by 1% of the time
where the time goes in v8:
time: 74.5 us; the launch traced here: 74.1 us
  Pallas kernels  35 us (47%)
  blocking collectives  25.5 us (34%)
  starting transfers between devices  11.1 us (15%)
  waiting for transfers between devices  0.95 us (1%)
  local copies, waits for them, and re-layouts  0.93 us (1%)
    all_to_all x2, blocking collectives, gather_all(): lax.all_to_all(jnp.broadcast_to(x[None], (length, *x.shape)), axis, 0, 0,...  25.5 us
    pallas_call x1, Pallas kernels, local(): pl.pallas_call(remote_kernel, out_shape=(half, half), in_specs=[VMEM, VME...  22.8 us
    all_to_all x1, starting transfers between devices, local(): gathered = lax.all_to_all(spread, 'row', 0, 0, tiled=True)  8.34 us
    pallas_call x1, Pallas kernels, local(): pl.pallas_call(local_kernel, in_specs=[VMEM, HBM], out_specs=(VMEM,) * 6,...  6.66 us
    pallas_call x1, Pallas kernels, local(): pl.pallas_call(functools.partial(final_kernel, total), in_specs=[VMEM, VM...  2.77 us
    ppermute x1, starting transfers between devices, local(): lax.ppermute(send, 'grp', [(i, groups - 1 - i) for i in range(groups)])  2.71 us
    pallas_call x1, Pallas kernels, local(): pl.pallas_call(prepare_kernel, in_specs=[HBM, HBM, HBM, HBM], out_specs=(...  2.4 us
  transfers between devices with their start and end apart: 2, of which 2 were waited for; matrix products, arithmetic and copies ran while one was open for 0% of the time, Pallas kernels for 9%

profile of v8, /device:TPU:1, one launch (start us, length us, event | category | flops | bytes accessed | tf_op | source)
XLA Modules:
  0.0 74.1 jit_solution(5596110827409351245)
XLA Ops:
  0.6 2.4 %prepare.1 = (bf16[8,8,2816]{2,1,0:T(8,128)(2,1)}, bf16[16,2560]{1,0:T(8,128)(2,1)}) custom-call(f32[240,4096]{1,0:T(8,128)} %bitcast.4, s32[3,4096]{1,0:T(4,128)} %lattice.1, s32[1,4096]{1,0:T(1,128)} %bitcast.7, f32[1,16]{1,0:T(1,128)} %bitcast.8), custom_call_target="tpu_custom_call" | custom-call | tf_op jit(solution)/shard_map/prepare/pallas_call | solution.py:402
  3.0 8.3 %all-to-all-start = ((bf16[8,8,2816]{2,1,0:T(8,128)(2,1)}), bf16[8,8,2816]{2,1,0:T(8,128)(2,1)S(1)}, u32[]{:S(2)}, u32[]{:S(2)}) async-start(bf16[8,8,2816]{2,1,0:T(8,128)(2,1)} %get-tuple-element.19), calls=%async_computation | async-start | bytes 720896 | tf_op jit(solution)/shard_map/all_to_all | solution.py:423
  11.4 0.0 copy-start
  11.4 0.9 %copy-done = bf16[16,2560]{1,0:T(8,128)(2,1)S(1)} copy-done((bf16[16,2560]{1,0:T(8,128)(2,1)S(1)}, bf16[16,2560]{1,0:T(8,128)(2,1)}, u32[]{:S(2)}) %copy-start) | copy-done | bytes 81944
  12.3 0.0 copy-start.1
  12.3 6.7 %scatter_local.1 = (f32[16,512]{1,0:T(8,128)S(1)}, f32[16,128]{1,0:T(8,128)S(1)}, f32[8,256]{1,0:T(8,128)S(1)}, bf16[240,256]{1,0:T(8,128)(2,1)S(1)}, bf16[240,2...) custom-call(bf16[16,2560]{1,0:T(8,128)(2,1)S(1)} %copy-done, f32[240,4096]{1,0:T(8,128)} %bitcast.5), custom_call_target="tpu_custom_call" | custom-call | flops 5000000000 | bytes 8000000 | tf_op jit(solution)/shard_map/scatter_local/pallas_call | solution.py:427
  18.9 0.1 all-to-all-done.sources
  19.1 0.0 copy-done.1
  19.1 22.8 %scatter_remote.1 = (f32[8,256]{1,0:T(8,128)S(1)}, f32[8,256]{1,0:T(8,128)S(1)}) custom-call(bf16[16,2560]{1,0:T(8,128)(2,1)S(1)} %copy-done.1, bf16[8,8,2816]{2,1,0:T(8,128)(2,1)S(1)} %all-to-all-done.sources, f32[16,512]{1,0:T(8,128)S(1)} %get-tuple-element.20.begun), custom_call_target="tpu_custom_call" | custom-call | flops 20000000000 | bytes 800000 | tf_op jit(solution)/shard_map/scatter_remote/pallas_call | solution.py:451
  41.9 2.7 %collective-permute-start = (f32[8,256]{1,0:T(8,128)S(1)}, f32[8,256]{1,0:T(8,128)S(1)}, u32[]{:S(2)}, u32[]{:S(2)}) collective-permute-start(f32[8,256]{1,0:T(8,128)S(1)} %get-tuple-element.22), channel_id=1, source_target_pairs={{0,1},{1,0},{2,3},{3,2},{4,5},{5,4},{6,7},{7,6},{8,9},{9,8},{10,11... | collective-permute-start | bytes 24584 | tf_op jit(solution)/shard_map/ppermute | solution.py:465
  44.6 0.8 %collective-permute-done.got = f32[8,256]{1,0:T(8,128)S(1)} collective-permute-done((f32[8,256]{1,0:T(8,128)S(1)}, f32[8,256]{1,0:T(8,128)S(1)}, u32[]{:S(2)}, u32[]{:S(2)}) %collective-permute-start) | collective-permute-done | bytes 8224 | tf_op jit(solution)/shard_map/ppermute | solution.py:465
  45.4 0.3 project.1
  45.8 11.7 %all_to_all.15 = f32[8,24,128]{2,1,0:T(8,128)S(1)} all-to-all(f32[8,24,128]{2,1,0:T(8,128)S(1)} %broadcast_in_dim.20), channel_id=1, replica_groups=mesh['row'=8,'col'=8,'grp'=2] {'row'}, dimensions={0} | all-to-all | bytes 196608 | tf_op jit(solution)/shard_map/all_to_all | solution.py:374
  57.5 13.8 %all_to_all.16.shared = f32[16,40,128]{2,1,0:T(8,128)S(1)} all-to-all(f32[16,40,128]{2,1,0:T(8,128)S(1)} %broadcast_in_dim.21), channel_id=1, replica_groups=mesh['row'=8,'col'=8,'grp'=2] {'col','grp'}, dimensions={0} | all-to-all | bytes 655360 | tf_op jit(solution)/shard_map/all_to_all | solution.py:374
  71.4 2.8 %finish.1 = (f32[8,4096]{1,0:T(8,128)}, f32[2,4,4,30]{3,2,1,0:T(4,128)}, f32[2,4,4]{2,1,0:T(4,128)}) custom-call(f32[16,40,128]{2,1,0:T(8,128)S(1)} %all_to_all.16.shared, f32[240,2048]{1,0:T(8,128)S(1)} %get-tuple-element.29.kept, f32[240,4096]{1,0:T(8,128)} %bitcast.6), custom_call_target="tpu_custom_call" | custom-call | tf_op jit(solution)/shard_map/finish/pallas_call | solution.py:479
  (4 shorter events, 0.1 us)
Async XLA Ops:
  3.0 16.0 %all-to-all-start = ((bf16[8,8,2816]{2,1,0:T(8,128)(2,1)}), bf16[8,8,2816]{2,1,0:T(8,128)(2,1)S(1)}, u32[]{:S(2)}, u32[]{:S(2)}) async-start(bf16[8,8,2816]{2,1,0:T(8,128)(2,1)} %get-tuple-element.19), calls=%async_computation | async-start | bytes 720896 | tf_op jit(solution)/shard_map/all_to_all | solution.py:423
  11.4 0.9 %copy-start = (bf16[16,2560]{1,0:T(8,128)(2,1)S(1)}, bf16[16,2560]{1,0:T(8,128)(2,1)}, u32[]{:S(2)}) copy-start(bf16[16,2560]{1,0:T(8,128)(2,1)} %get-tuple-element.18.ready) | copy-start | bytes 245764
  12.3 6.8 %copy-start.1 = (bf16[16,2560]{1,0:T(8,128)(2,1)S(1)}, bf16[16,2560]{1,0:T(8,128)(2,1)}, u32[]{:S(2)}) copy-start(bf16[16,2560]{1,0:T(8,128)(2,1)} %get-tuple-element.18.ready) | copy-start | bytes 245764
  41.9 3.5 %collective-permute-start = (f32[8,256]{1,0:T(8,128)S(1)}, f32[8,256]{1,0:T(8,128)S(1)}, u32[]{:S(2)}, u32[]{:S(2)}) collective-permute-start(f32[8,256]{1,0:T(8,128)S(1)} %get-tuple-element.22), channel_id=1, source_target_pairs={{0,1},{1,0},{2,3},{3,2},{4,5},{5,4},{6,7},{7,6},{8,9},{9,8},{10,11... | collective-permute-start | bytes 24584 | tf_op jit(solution)/shard_map/ppermute | solution.py:465

commit v9 on v5

--- a/solution.py
+++ b/solution.py
@@ -137,22 +137,21 @@
 
 
 def prepare_kernel(basis, lattice, index, table, spread, ready, *scratch):
-    direction, chosen, held_table, points, aims, sems = scratch
+    direction, chosen, held_table, points, sems = scratch
     rows = spread.shape[0]
-    length = points.shape[1]
-    wide = aims.shape[1]
+    length = chosen.shape[1]
+    wide = ready.shape[1] - length
     channels = direction.shape[0]
     aim = pl.multiple_of(lax.axis_index("col") * wide, 128)
     start = pl.multiple_of(lax.axis_index("grp") * length, 128)
     last = basis.shape[0] - channels
     copies = [
-        pltpu.make_async_copy(lattice.at[:, pl.ds(start, length)], points, sems.at[0]),
+        pltpu.make_async_copy(lattice, points, sems.at[0]),
         pltpu.make_async_copy(index.at[:, pl.ds(start, length)], chosen, sems.at[1]),
         pltpu.make_async_copy(table, held_table, sems.at[2]),
         pltpu.make_async_copy(
             basis.at[last : last + channels, pl.ds(start, length)], direction, sems.at[3]
         ),
-        pltpu.make_async_copy(lattice.at[:, pl.ds(aim, wide)], aims, sems.at[4]),
     ]
     for copy in copies:
         copy.start()
@@ -166,7 +165,7 @@
         return jnp.concatenate([p.astype(f32) for p in parts], 0)
 
     copies[0].wait()
-    x, y, z, high, low, one = shared_rows(points[...])
+    x, y, z, high, low, one = shared_rows(points[:, pl.ds(start, length)])
     sites = stacked([x, y, z, high, low, one, one, 0 * one])
     copies[1].wait()
     copies[2].wait()
@@ -185,8 +184,7 @@
     packed = jnp.concatenate([weighted] + [d.astype(bf16) for d in dense], 1)
     for k in range(rows):
         spread[k] = packed
-    copies[4].wait()
-    x, y, z, high, low, one = shared_rows(aims[...])
+    x, y, z, high, low, one = shared_rows(points[:, pl.ds(aim, wide)])
     sites = stacked([-2 * x, -2 * y, -2 * z, 256 * one, one, 256 * high, low, 0 * one])
     ready[:, length:] = jnp.concatenate([jnp.zeros_like(sites), sites], 0).astype(bf16)
 
@@ -277,7 +275,7 @@
     parts = shared.shape[0]
     count, points = basis.shape
     width = 256
-    chunk = 512
+    chunk = 1024
     half = points - held.shape[1]
     copies = []
     for k in range(sems.shape[0]):
@@ -406,9 +404,8 @@
             pltpu.VMEM((channels, length), f32),
             pltpu.VMEM((1, length), jnp.int32),
             pltpu.VMEM((1, strength_table.shape[0]), f32),
-            pltpu.VMEM((3, length), jnp.int32),
-            pltpu.VMEM((3, wide), jnp.int32),
-            pltpu.SemaphoreType.DMA((5,)),
+            pltpu.VMEM((3, points), jnp.int32),
+            pltpu.SemaphoreType.DMA((4,)),
         ],
         compiler_params=params((64 << 20) - (64 << 10)),
         name="prepare",
@@ -434,7 +431,7 @@
             pltpu.VMEM((count, points // 2), f32),
             pltpu.VMEM((count, points), bf16),
             pltpu.VMEM((count, points), bf16),
-            pltpu.SemaphoreType.DMA((9,)),
+            pltpu.SemaphoreType.DMA((5,)),
         ],
         compiler_params=params(50 << 20),
         cost_estimate=cost(5_000_000_000, 8_000_000),
@@ -482,7 +479,7 @@
             pltpu.VMEM((256, 256), bf16),
             pltpu.VMEM((256, 256), bf16),
             pltpu.VMEM((count, points // 2), f32),
-            pltpu.SemaphoreType.DMA((points // 2 // 512,)),
+            pltpu.SemaphoreType.DMA((points // 2 // 1024,)),
         ],
         compiler_params=params(50 << 20),
         name="finish",

time: 73.9 us -> 74.5 us (level)
  no operation moved by 1% of the time
where the time goes in v9:
time: 74.5 us; the launch traced here: 74.1 us
  Pallas kernels  34.9 us (47%)
  blocking collectives  25.6 us (34%)
  starting transfers between devices  11 us (15%)
  local copies, waits for them, and re-layouts  0.93 us (1%)
  waiting for transfers between devices  0.88 us (1%)
    all_to_all x2, blocking collectives, gather_all(): lax.all_to_all(jnp.broadcast_to(x[None], (length, *x.shape)), axis, 0, 0,...  25.6 us
    pallas_call x1, Pallas kernels, local(): pl.pallas_call(remote_kernel, out_shape=(half, half), in_specs=[VMEM, VME...  22.8 us
    all_to_all x1, starting transfers between devices, local(): gathered = lax.all_to_all(spread, 'row', 0, 0, tiled=True)  8.34 us
    pallas_call x1, Pallas kernels, local(): pl.pallas_call(local_kernel, in_specs=[VMEM, HBM], out_specs=(VMEM,) * 6,...  6.73 us
    pallas_call x1, Pallas kernels, local(): pl.pallas_call(functools.partial(final_kernel, total), in_specs=[VMEM, VM...  3.27 us
    ppermute x1, starting transfers between devices, local(): lax.ppermute(send, 'grp', [(i, groups - 1 - i) for i in range(groups)])  2.7 us
    pallas_call x1, Pallas kernels, local(): pl.pallas_call(prepare_kernel, in_specs=[HBM, HBM, HBM, HBM], out_specs=(...  1.8 us
  transfers between devices with their start and end apart: 2, of which 2 were waited for; matrix products, arithmetic and copies ran while one was open for 0% of the time, Pallas kernels for 9%

profile of v9, /device:TPU:1, one launch (start us, length us, event | category | flops | bytes accessed | tf_op | source)
XLA Modules:
  0.0 74.1 jit_solution(8715953888383121675)
XLA Ops:
  0.6 1.8 %prepare.1 = (bf16[8,8,2816]{2,1,0:T(8,128)(2,1)}, bf16[16,2560]{1,0:T(8,128)(2,1)}) custom-call(f32[240,4096]{1,0:T(8,128)} %bitcast.4, s32[3,4096]{1,0:T(4,128)} %lattice.1, s32[1,4096]{1,0:T(1,128)} %bitcast.7, f32[1,16]{1,0:T(1,128)} %bitcast.8), custom_call_target="tpu_custom_call" | custom-call | tf_op jit(solution)/shard_map/prepare/pallas_call | solution.py:395
  2.4 8.3 %all-to-all-start = ((bf16[8,8,2816]{2,1,0:T(8,128)(2,1)}), bf16[8,8,2816]{2,1,0:T(8,128)(2,1)S(1)}, u32[]{:S(2)}, u32[]{:S(2)}) async-start(bf16[8,8,2816]{2,1,0:T(8,128)(2,1)} %get-tuple-element.19), calls=%async_computation | async-start | bytes 720896 | tf_op jit(solution)/shard_map/all_to_all | solution.py:413
  10.8 0.0 copy-start
  10.8 0.9 %copy-done = bf16[16,2560]{1,0:T(8,128)(2,1)S(1)} copy-done((bf16[16,2560]{1,0:T(8,128)(2,1)S(1)}, bf16[16,2560]{1,0:T(8,128)(2,1)}, u32[]{:S(2)}) %copy-start) | copy-done | bytes 81944
  11.7 0.0 copy-start.1
  11.7 6.7 %scatter_local.1 = (f32[16,512]{1,0:T(8,128)S(1)}, f32[16,128]{1,0:T(8,128)S(1)}, f32[8,256]{1,0:T(8,128)S(1)}, bf16[240,256]{1,0:T(8,128)(2,1)S(1)}, bf16[240,2...) custom-call(bf16[16,2560]{1,0:T(8,128)(2,1)S(1)} %copy-done, f32[240,4096]{1,0:T(8,128)} %bitcast.5), custom_call_target="tpu_custom_call" | custom-call | flops 5000000000 | bytes 8000000 | tf_op jit(solution)/shard_map/scatter_local/pallas_call | solution.py:417
  18.4 0.1 all-to-all-done.sources
  18.5 0.0 copy-done.1
  18.5 22.8 %scatter_remote.1 = (f32[8,256]{1,0:T(8,128)S(1)}, f32[8,256]{1,0:T(8,128)S(1)}) custom-call(bf16[16,2560]{1,0:T(8,128)(2,1)S(1)} %copy-done.1, bf16[8,8,2816]{2,1,0:T(8,128)(2,1)S(1)} %all-to-all-done.sources, f32[16,512]{1,0:T(8,128)S(1)} %get-tuple-element.20.begun), custom_call_target="tpu_custom_call" | custom-call | flops 20000000000 | bytes 800000 | tf_op jit(solution)/shard_map/scatter_remote/pallas_call | solution.py:441
  41.3 2.7 %collective-permute-start = (f32[8,256]{1,0:T(8,128)S(1)}, f32[8,256]{1,0:T(8,128)S(1)}, u32[]{:S(2)}, u32[]{:S(2)}) collective-permute-start(f32[8,256]{1,0:T(8,128)S(1)} %get-tuple-element.22), channel_id=1, source_target_pairs={{0,1},{1,0},{2,3},{3,2},{4,5},{5,4},{6,7},{7,6},{8,9},{9,8},{10,11... | collective-permute-start | bytes 24584 | tf_op jit(solution)/shard_map/ppermute | solution.py:455
  44.0 0.8 %collective-permute-done.got = f32[8,256]{1,0:T(8,128)S(1)} collective-permute-done((f32[8,256]{1,0:T(8,128)S(1)}, f32[8,256]{1,0:T(8,128)S(1)}, u32[]{:S(2)}, u32[]{:S(2)}) %collective-permute-start) | collective-permute-done | bytes 8224 | tf_op jit(solution)/shard_map/ppermute | solution.py:455
  44.8 0.3 project.1
  45.2 11.8 %all_to_all.15 = f32[8,24,128]{2,1,0:T(8,128)S(1)} all-to-all(f32[8,24,128]{2,1,0:T(8,128)S(1)} %broadcast_in_dim.20), channel_id=1, replica_groups=mesh['row'=8,'col'=8,'grp'=2] {'row'}, dimensions={0} | all-to-all | bytes 196608 | tf_op jit(solution)/shard_map/all_to_all | solution.py:367
  57.0 13.8 %all_to_all.16.shared = f32[16,40,128]{2,1,0:T(8,128)S(1)} all-to-all(f32[16,40,128]{2,1,0:T(8,128)S(1)} %broadcast_in_dim.21), channel_id=1, replica_groups=mesh['row'=8,'col'=8,'grp'=2] {'col','grp'}, dimensions={0} | all-to-all | bytes 655360 | tf_op jit(solution)/shard_map/all_to_all | solution.py:367
  70.8 3.3 %finish.1 = (f32[8,4096]{1,0:T(8,128)}, f32[2,4,4,30]{3,2,1,0:T(4,128)}, f32[2,4,4]{2,1,0:T(4,128)}) custom-call(f32[16,40,128]{2,1,0:T(8,128)S(1)} %all_to_all.16.shared, f32[240,2048]{1,0:T(8,128)S(1)} %get-tuple-element.29.kept, f32[240,4096]{1,0:T(8,128)} %bitcast.6), custom_call_target="tpu_custom_call" | custom-call | tf_op jit(solution)/shard_map/finish/pallas_call | solution.py:469
  (4 shorter events, 0.1 us)
Async XLA Ops:
  2.4 16.0 %all-to-all-start = ((bf16[8,8,2816]{2,1,0:T(8,128)(2,1)}), bf16[8,8,2816]{2,1,0:T(8,128)(2,1)S(1)}, u32[]{:S(2)}, u32[]{:S(2)}) async-start(bf16[8,8,2816]{2,1,0:T(8,128)(2,1)} %get-tuple-element.19), calls=%async_computation | async-start | bytes 720896 | tf_op jit(solution)/shard_map/all_to_all | solution.py:413
  10.8 0.9 %copy-start = (bf16[16,2560]{1,0:T(8,128)(2,1)S(1)}, bf16[16,2560]{1,0:T(8,128)(2,1)}, u32[]{:S(2)}) copy-start(bf16[16,2560]{1,0:T(8,128)(2,1)} %get-tuple-element.18.ready) | copy-start | bytes 245764
  11.7 6.8 %copy-start.1 = (bf16[16,2560]{1,0:T(8,128)(2,1)S(1)}, bf16[16,2560]{1,0:T(8,128)(2,1)}, u32[]{:S(2)}) copy-start(bf16[16,2560]{1,0:T(8,128)(2,1)} %get-tuple-element.18.ready) | copy-start | bytes 245764
  41.3 3.5 %collective-permute-start = (f32[8,256]{1,0:T(8,128)S(1)}, f32[8,256]{1,0:T(8,128)S(1)}, u32[]{:S(2)}, u32[]{:S(2)}) collective-permute-start(f32[8,256]{1,0:T(8,128)S(1)} %get-tuple-element.22), channel_id=1, source_target_pairs={{0,1},{1,0},{2,3},{3,2},{4,5},{5,4},{6,7},{7,6},{8,9},{9,8},{10,11... | collective-permute-start | bytes 24584 | tf_op jit(solution)/shard_map/ppermute | solution.py:455

commit v10 on v5

--- a/solution.py
+++ b/solution.py
@@ -192,7 +192,7 @@
 
 
 def local_kernel(ready, basis, *rest):
-    acc, gram, direction, own_high, own_low, kept, tiles, held, high, low, sems = rest
+    acc, gram, direction, own_high, own_low, kept_high, kept_low, tiles, kept, held, high, low, sems = rest
     half = kept.shape[1]
     length = ready.shape[1] - tiles.shape[2]
     targets = ready.at[8:16, length:]
@@ -247,6 +247,8 @@
     own.wait()
     own_high[...] = high[:, here]
     own_low[...] = low[:, here]
+    kept_high[...] = high[:, :half]
+    kept_low[...] = low[:, :half]
 
 
 def stack_halves(x):
@@ -273,7 +275,8 @@
     packed[8:, :] = gram[...]
 
 
-def final_kernel(total, shared, kept, basis, new, coef, norm, gram_high, gram_low, held, sems):
+def final_kernel(total, shared, kept_high, kept_low, basis, new, coef, norm, *scratch):
+    gram_high, gram_low, held, sems = scratch
     parts = shared.shape[0]
     count, points = basis.shape
     width = 256
@@ -324,12 +327,11 @@
     for k in range(points // chunk):
         cut = slice(k * chunk, (k + 1) * chunk)
         if k * chunk < half:
-            columns = kept[:, cut]
+            top, rest = kept_high[:, cut], kept_low[:, cut]
         else:
             later = k - half // chunk
             copies[later].wait()
-            columns = held[:, later * chunk : (later + 1) * chunk]
-        top, rest = split(columns)
+            top, rest = split(held[:, later * chunk : (later + 1) * chunk])
         first = jnp.dot(both, top, preferred_element_type=f32)
         second = jnp.dot(mix_high, rest, preferred_element_type=f32)
         each = chunk // width
@@ -417,20 +419,22 @@
 
     half = jax.ShapeDtypeStruct((channels, own), f32)
     held = pltpu.VMEM((2, STEP, wide), f32)
-    begun, gram, direction, high, low, kept = pl.pallas_call(
+    begun, gram, direction, high, low, kept_high, kept_low = pl.pallas_call(
         local_kernel,
         in_specs=[VMEM, HBM],
-        out_specs=(VMEM,) * 6,
+        out_specs=(VMEM,) * 7,
         out_shape=(
             jax.ShapeDtypeStruct((16, wide), f32),
             jax.ShapeDtypeStruct((16, 128), f32),
             half,
             jax.ShapeDtypeStruct((count, own), bf16),
             jax.ShapeDtypeStruct((count, own), bf16),
-            jax.ShapeDtypeStruct((count, points // 2), f32),
+            jax.ShapeDtypeStruct((count, points // 2), bf16),
+            jax.ShapeDtypeStruct((count, points // 2), bf16),
         ),
         scratch_shapes=[
             held,
+            pltpu.VMEM((count, points // 2), f32),
             pltpu.VMEM((count, points // 2), f32),
             pltpu.VMEM((count, points), bf16),
             pltpu.VMEM((count, points), bf16),
@@ -471,7 +475,7 @@
 
     new_block, coef, norm = pl.pallas_call(
         functools.partial(final_kernel, total),
-        in_specs=[VMEM, VMEM, HBM],
+        in_specs=[VMEM, VMEM, VMEM, HBM],
         out_specs=(VMEM, VMEM, VMEM),
         out_shape=(
             jax.ShapeDtypeStruct((channels, points), f32),
@@ -486,7 +490,7 @@
         ],
         compiler_params=params(50 << 20),
         name="finish",
-    )(shared, kept, flat)
+    )(shared, kept_high, kept_low, flat)
     return new_block, coef.transpose(3, 0, 1, 2), norm
 
 

time: 73.9 us -> 74.5 us (level)
  transfers between devices with their start and end apart: 2 -> 2, of which waited for: 2 -> 1; matrix products, arithmetic and copies ran while one was open for 0% -> 0% of each run, Pallas kernels for 9% -> 9%
where the time goes in v10:
time: 74.5 us; the launch traced here: 74.1 us
  Pallas kernels  34.9 us (47%)
  blocking collectives  25.7 us (34%)
  starting transfers between devices  11 us (15%)
  local copies, waits for them, and re-layouts  0.93 us (1%)
  waiting for transfers between devices  0.84 us (1%)
    all_to_all x2, blocking collectives, gather_all(): lax.all_to_all(jnp.broadcast_to(x[None], (length, *x.shape)), axis, 0, 0,...  25.7 us
    pallas_call x1, Pallas kernels, local(): pl.pallas_call(remote_kernel, out_shape=(half, half), in_specs=[VMEM, VME...  22.8 us
    all_to_all x1, starting transfers between devices, local(): gathered = lax.all_to_all(spread, 'row', 0, 0, tiled=True)  8.34 us
    pallas_call x1, Pallas kernels, local(): pl.pallas_call(local_kernel, in_specs=[VMEM, HBM], out_specs=(VMEM,) * 7,...  6.77 us
    pallas_call x1, Pallas kernels, local(): pl.pallas_call(functools.partial(final_kernel, total), in_specs=[VMEM, VM...  3.26 us
    ppermute x1, starting transfers between devices, local(): lax.ppermute(send, 'grp', [(i, groups - 1 - i) for i in range(groups)])  2.69 us
    pallas_call x1, Pallas kernels, local(): pl.pallas_call(prepare_kernel, in_specs=[HBM, HBM, HBM, HBM], out_specs=(...  1.74 us
  transfers between devices with their start and end apart: 2, of which 1 were waited for; matrix products, arithmetic and copies ran while one was open for 0% of the time, Pallas kernels for 9%

profile of v10, /device:TPU:1, one launch (start us, length us, event | category | flops | bytes accessed | tf_op | source)
XLA Modules:
  0.0 74.1 jit_solution(3429450967285724983)
XLA Ops:
  0.6 1.7 %prepare.1 = (bf16[8,8,2816]{2,1,0:T(8,128)(2,1)}, bf16[16,2560]{1,0:T(8,128)(2,1)}) custom-call(f32[240,4096]{1,0:T(8,128)} %bitcast.4, s32[3,4096]{1,0:T(4,128)} %lattice.1, s32[1,4096]{1,0:T(1,128)} %bitcast.7, f32[1,16]{1,0:T(1,128)} %bitcast.8), custom_call_target="tpu_custom_call" | custom-call | tf_op jit(solution)/shard_map/prepare/pallas_call | solution.py:399
  2.4 8.3 %all-to-all-start = ((bf16[8,8,2816]{2,1,0:T(8,128)(2,1)}), bf16[8,8,2816]{2,1,0:T(8,128)(2,1)S(1)}, u32[]{:S(2)}, u32[]{:S(2)}) async-start(bf16[8,8,2816]{2,1,0:T(8,128)(2,1)} %get-tuple-element.20), calls=%async_computation | async-start | bytes 720896 | tf_op jit(solution)/shard_map/all_to_all | solution.py:418
  10.7 0.0 copy-start
  10.7 0.9 %copy-done = bf16[16,2560]{1,0:T(8,128)(2,1)S(1)} copy-done((bf16[16,2560]{1,0:T(8,128)(2,1)S(1)}, bf16[16,2560]{1,0:T(8,128)(2,1)}, u32[]{:S(2)}) %copy-start) | copy-done | bytes 81944
  11.6 0.0 copy-start.1
  11.6 6.8 %scatter_local.1 = (f32[16,512]{1,0:T(8,128)S(1)}, f32[16,128]{1,0:T(8,128)S(1)}, f32[8,256]{1,0:T(8,128)S(1)}, bf16[240,256]{1,0:T(8,128)(2,1)S(1)}, bf16[240,2...) custom-call(bf16[16,2560]{1,0:T(8,128)(2,1)S(1)} %copy-done, f32[240,4096]{1,0:T(8,128)} %bitcast.5), custom_call_target="tpu_custom_call" | custom-call | flops 5000000000 | bytes 8000000 | tf_op jit(solution)/shard_map/scatter_local/pallas_call | solution.py:422
  18.4 0.0 all-to-all-done.sources
  18.4 0.0 copy-done.1
  18.4 22.8 %scatter_remote.1 = (f32[8,256]{1,0:T(8,128)S(1)}, f32[8,256]{1,0:T(8,128)S(1)}) custom-call(bf16[16,2560]{1,0:T(8,128)(2,1)S(1)} %copy-done.1, bf16[8,8,2816]{2,1,0:T(8,128)(2,1)S(1)} %all-to-all-done.sources, f32[16,512]{1,0:T(8,128)S(1)} %get-tuple-element.21.begun), custom_call_target="tpu_custom_call" | custom-call | flops 20000000000 | bytes 800000 | tf_op jit(solution)/shard_map/scatter_remote/pallas_call | solution.py:448
  41.2 2.7 %collective-permute-start = (f32[8,256]{1,0:T(8,128)S(1)}, f32[8,256]{1,0:T(8,128)S(1)}, u32[]{:S(2)}, u32[]{:S(2)}) collective-permute-start(f32[8,256]{1,0:T(8,128)S(1)} %get-tuple-element.23), channel_id=1, source_target_pairs={{0,1},{1,0},{2,3},{3,2},{4,5},{5,4},{6,7},{7,6},{8,9},{9,8},{10,11... | collective-permute-start | bytes 24584 | tf_op jit(solution)/shard_map/ppermute | solution.py:462
  43.9 0.8 %collective-permute-done.got = f32[8,256]{1,0:T(8,128)S(1)} collective-permute-done((f32[8,256]{1,0:T(8,128)S(1)}, f32[8,256]{1,0:T(8,128)S(1)}, u32[]{:S(2)}, u32[]{:S(2)}) %collective-permute-start) | collective-permute-done | bytes 8224 | tf_op jit(solution)/shard_map/ppermute | solution.py:462
  44.7 0.3 project.1
  45.1 11.8 %all_to_all.15 = f32[8,24,128]{2,1,0:T(8,128)S(1)} all-to-all(f32[8,24,128]{2,1,0:T(8,128)S(1)} %broadcast_in_dim.20), channel_id=1, replica_groups=mesh['row'=8,'col'=8,'grp'=2] {'row'}, dimensions={0} | all-to-all | bytes 196608 | tf_op jit(solution)/shard_map/all_to_all | solution.py:371
  57.0 13.8 %all_to_all.16.shared = f32[16,40,128]{2,1,0:T(8,128)S(1)} all-to-all(f32[16,40,128]{2,1,0:T(8,128)S(1)} %broadcast_in_dim.21), channel_id=1, replica_groups=mesh['row'=8,'col'=8,'grp'=2] {'col','grp'}, dimensions={0} | all-to-all | bytes 655360 | tf_op jit(solution)/shard_map/all_to_all | solution.py:371
  70.8 3.3 %finish.1 = (f32[8,4096]{1,0:T(8,128)}, f32[2,4,4,30]{3,2,1,0:T(4,128)}, f32[2,4,4]{2,1,0:T(4,128)}) custom-call(f32[16,40,128]{2,1,0:T(8,128)S(1)} %all_to_all.16.shared, bf16[240,2048]{1,0:T(8,128)(2,1)S(1)} %get-tuple-element.30.kept_high, bf16[240,2048]{1,0:T(8,128)(2,1)S(1)} %get-tuple-element.31.kept_low, f32[240,4096]{1,0:T(8,128)} %bitcast.6), custom_call_target="tpu_custom_call" | custom-call | tf_op jit(solution)/shard_map/finish/pallas_call | solution.py:476
  (4 shorter events, 0.1 us)
Async XLA Ops:
  2.4 16.0 %all-to-all-start = ((bf16[8,8,2816]{2,1,0:T(8,128)(2,1)}), bf16[8,8,2816]{2,1,0:T(8,128)(2,1)S(1)}, u32[]{:S(2)}, u32[]{:S(2)}) async-start(bf16[8,8,2816]{2,1,0:T(8,128)(2,1)} %get-tuple-element.20), calls=%async_computation | async-start | bytes 720896 | tf_op jit(solution)/shard_map/all_to_all | solution.py:418
  10.7 0.9 %copy-start = (bf16[16,2560]{1,0:T(8,128)(2,1)S(1)}, bf16[16,2560]{1,0:T(8,128)(2,1)}, u32[]{:S(2)}) copy-start(bf16[16,2560]{1,0:T(8,128)(2,1)} %get-tuple-element.19.ready) | copy-start | bytes 245764
  11.6 6.8 %copy-start.1 = (bf16[16,2560]{1,0:T(8,128)(2,1)S(1)}, bf16[16,2560]{1,0:T(8,128)(2,1)}, u32[]{:S(2)}) copy-start(bf16[16,2560]{1,0:T(8,128)(2,1)} %get-tuple-element.19.ready) | copy-start | bytes 245764
  41.2 3.5 %collective-permute-start = (f32[8,256]{1,0:T(8,128)S(1)}, f32[8,256]{1,0:T(8,128)S(1)}, u32[]{:S(2)}, u32[]{:S(2)}) collective-permute-start(f32[8,256]{1,0:T(8,128)S(1)} %get-tuple-element.23), channel_id=1, source_target_pairs={{0,1},{1,0},{2,3},{3,2},{4,5},{5,4},{6,7},{7,6},{8,9},{9,8},{10,11... | collective-permute-start | bytes 24584 | tf_op jit(solution)/shard_map/ppermute | solution.py:462

commit v11 on v5

--- a/solution.py
+++ b/solution.py
@@ -277,7 +277,7 @@
     parts = shared.shape[0]
     count, points = basis.shape
     width = 256
-    chunk = 512
+    chunk = 256
     half = points - held.shape[1]
     copies = []
     for k in range(sems.shape[0]):
@@ -482,7 +482,7 @@
             pltpu.VMEM((256, 256), bf16),
             pltpu.VMEM((256, 256), bf16),
             pltpu.VMEM((count, points // 2), f32),
-            pltpu.SemaphoreType.DMA((points // 2 // 512,)),
+            pltpu.SemaphoreType.DMA((points // 2 // 256,)),
         ],
         compiler_params=params(50 << 20),
         name="finish",

time: 73.9 us -> 74.6 us (level)
  no operation moved by 1% of the time
where the time goes in v11:
time: 74.6 us; the launch traced here: 74.2 us
  Pallas kernels  35 us (47%)
  blocking collectives  25.6 us (34%)
  starting transfers between devices  11.1 us (15%)
  waiting for transfers between devices  0.96 us (1%)
  local copies, waits for them, and re-layouts  0.93 us (1%)
    all_to_all x2, blocking collectives, gather_all(): lax.all_to_all(jnp.broadcast_to(x[None], (length, *x.shape)), axis, 0, 0,...  25.6 us
    pallas_call x1, Pallas kernels, local(): pl.pallas_call(remote_kernel, out_shape=(half, half), in_specs=[VMEM, VME...  22.8 us
    all_to_all x1, starting transfers between devices, local(): gathered = lax.all_to_all(spread, 'row', 0, 0, tiled=True)  8.34 us
    pallas_call x1, Pallas kernels, local(): pl.pallas_call(local_kernel, in_specs=[VMEM, HBM], out_specs=(VMEM,) * 6,...  6.65 us
    pallas_call x1, Pallas kernels, local(): pl.pallas_call(functools.partial(final_kernel, total), in_specs=[VMEM, VM...  3.45 us
    ppermute x1, starting transfers between devices, local(): lax.ppermute(send, 'grp', [(i, groups - 1 - i) for i in range(groups)])  2.71 us
    pallas_call x1, Pallas kernels, local(): pl.pallas_call(prepare_kernel, in_specs=[HBM, HBM, HBM, HBM], out_specs=(...  1.74 us
  transfers between devices with their start and end apart: 2, of which 2 were waited for; matrix products, arithmetic and copies ran while one was open for 0% of the time, Pallas kernels for 9%

profile of v11, /device:TPU:1, one launch (start us, length us, event | category | flops | bytes accessed | tf_op | source)
XLA Modules:
  0.0 74.2 jit_solution(17454894403779108231)
XLA Ops:
  0.6 1.7 %prepare.1 = (bf16[8,8,2816]{2,1,0:T(8,128)(2,1)}, bf16[16,2560]{1,0:T(8,128)(2,1)}) custom-call(f32[240,4096]{1,0:T(8,128)} %bitcast.4, s32[3,4096]{1,0:T(4,128)} %lattice.1, s32[1,4096]{1,0:T(1,128)} %bitcast.7, f32[1,16]{1,0:T(1,128)} %bitcast.8), custom_call_target="tpu_custom_call" | custom-call | tf_op jit(solution)/shard_map/prepare/pallas_call | solution.py:397
  2.4 8.3 %all-to-all-start = ((bf16[8,8,2816]{2,1,0:T(8,128)(2,1)}), bf16[8,8,2816]{2,1,0:T(8,128)(2,1)S(1)}, u32[]{:S(2)}, u32[]{:S(2)}) async-start(bf16[8,8,2816]{2,1,0:T(8,128)(2,1)} %get-tuple-element.19), calls=%async_computation | async-start | bytes 720896 | tf_op jit(solution)/shard_map/all_to_all | solution.py:416
  10.7 0.0 copy-start
  10.7 0.9 %copy-done = bf16[16,2560]{1,0:T(8,128)(2,1)S(1)} copy-done((bf16[16,2560]{1,0:T(8,128)(2,1)S(1)}, bf16[16,2560]{1,0:T(8,128)(2,1)}, u32[]{:S(2)}) %copy-start) | copy-done | bytes 81944
  11.6 0.0 copy-start.1
  11.6 6.7 %scatter_local.1 = (f32[16,512]{1,0:T(8,128)S(1)}, f32[16,128]{1,0:T(8,128)S(1)}, f32[8,256]{1,0:T(8,128)S(1)}, bf16[240,256]{1,0:T(8,128)(2,1)S(1)}, bf16[240,2...) custom-call(bf16[16,2560]{1,0:T(8,128)(2,1)S(1)} %copy-done, f32[240,4096]{1,0:T(8,128)} %bitcast.5), custom_call_target="tpu_custom_call" | custom-call | flops 5000000000 | bytes 8000000 | tf_op jit(solution)/shard_map/scatter_local/pallas_call | solution.py:420
  18.3 0.1 all-to-all-done.sources
  18.4 0.0 copy-done.1
  18.4 22.8 %scatter_remote.1 = (f32[8,256]{1,0:T(8,128)S(1)}, f32[8,256]{1,0:T(8,128)S(1)}) custom-call(bf16[16,2560]{1,0:T(8,128)(2,1)S(1)} %copy-done.1, bf16[8,8,2816]{2,1,0:T(8,128)(2,1)S(1)} %all-to-all-done.sources, f32[16,512]{1,0:T(8,128)S(1)} %get-tuple-element.20.begun), custom_call_target="tpu_custom_call" | custom-call | flops 20000000000 | bytes 800000 | tf_op jit(solution)/shard_map/scatter_remote/pallas_call | solution.py:444
  41.2 2.7 %collective-permute-start = (f32[8,256]{1,0:T(8,128)S(1)}, f32[8,256]{1,0:T(8,128)S(1)}, u32[]{:S(2)}, u32[]{:S(2)}) collective-permute-start(f32[8,256]{1,0:T(8,128)S(1)} %get-tuple-element.22), channel_id=1, source_target_pairs={{0,1},{1,0},{2,3},{3,2},{4,5},{5,4},{6,7},{7,6},{8,9},{9,8},{10,11... | collective-permute-start | bytes 24584 | tf_op jit(solution)/shard_map/ppermute | solution.py:458
  43.9 0.8 %collective-permute-done.got = f32[8,256]{1,0:T(8,128)S(1)} collective-permute-done((f32[8,256]{1,0:T(8,128)S(1)}, f32[8,256]{1,0:T(8,128)S(1)}, u32[]{:S(2)}, u32[]{:S(2)}) %collective-permute-start) | collective-permute-done | bytes 8224 | tf_op jit(solution)/shard_map/ppermute | solution.py:458
  44.7 0.3 project.1
  45.1 11.7 %all_to_all.15 = f32[8,24,128]{2,1,0:T(8,128)S(1)} all-to-all(f32[8,24,128]{2,1,0:T(8,128)S(1)} %broadcast_in_dim.20), channel_id=1, replica_groups=mesh['row'=8,'col'=8,'grp'=2] {'row'}, dimensions={0} | all-to-all | bytes 196608 | tf_op jit(solution)/shard_map/all_to_all | solution.py:369
  56.9 13.8 %all_to_all.16.shared = f32[16,40,128]{2,1,0:T(8,128)S(1)} all-to-all(f32[16,40,128]{2,1,0:T(8,128)S(1)} %broadcast_in_dim.21), channel_id=1, replica_groups=mesh['row'=8,'col'=8,'grp'=2] {'col','grp'}, dimensions={0} | all-to-all | bytes 655360 | tf_op jit(solution)/shard_map/all_to_all | solution.py:369
  70.7 3.5 %finish.1 = (f32[8,4096]{1,0:T(8,128)}, f32[2,4,4,30]{3,2,1,0:T(4,128)}, f32[2,4,4]{2,1,0:T(4,128)}) custom-call(f32[16,40,128]{2,1,0:T(8,128)S(1)} %all_to_all.16.shared, f32[240,2048]{1,0:T(8,128)S(1)} %get-tuple-element.29.kept, f32[240,4096]{1,0:T(8,128)} %bitcast.6), custom_call_target="tpu_custom_call" | custom-call | tf_op jit(solution)/shard_map/finish/pallas_call | solution.py:472
  (4 shorter events, 0.1 us)
Async XLA Ops:
  2.4 16.0 %all-to-all-start = ((bf16[8,8,2816]{2,1,0:T(8,128)(2,1)}), bf16[8,8,2816]{2,1,0:T(8,128)(2,1)S(1)}, u32[]{:S(2)}, u32[]{:S(2)}) async-start(bf16[8,8,2816]{2,1,0:T(8,128)(2,1)} %get-tuple-element.19), calls=%async_computation | async-start | bytes 720896 | tf_op jit(solution)/shard_map/all_to_all | solution.py:416
  10.7 0.9 %copy-start = (bf16[16,2560]{1,0:T(8,128)(2,1)S(1)}, bf16[16,2560]{1,0:T(8,128)(2,1)}, u32[]{:S(2)}) copy-start(bf16[16,2560]{1,0:T(8,128)(2,1)} %get-tuple-element.18.ready) | copy-start | bytes 245764
  11.6 6.8 %copy-start.1 = (bf16[16,2560]{1,0:T(8,128)(2,1)S(1)}, bf16[16,2560]{1,0:T(8,128)(2,1)}, u32[]{:S(2)}) copy-start(bf16[16,2560]{1,0:T(8,128)(2,1)} %get-tuple-element.18.ready) | copy-start | bytes 245764
  41.2 3.5 %collective-permute-start = (f32[8,256]{1,0:T(8,128)S(1)}, f32[8,256]{1,0:T(8,128)S(1)}, u32[]{:S(2)}, u32[]{:S(2)}) collective-permute-start(f32[8,256]{1,0:T(8,128)S(1)} %get-tuple-element.22), channel_id=1, source_target_pairs={{0,1},{1,0},{2,3},{3,2},{4,5},{5,4},{6,7},{7,6},{8,9},{9,8},{10,11... | collective-permute-start | bytes 24584 | tf_op jit(solution)/shard_map/ppermute | solution.py:458
